TPU v7x, 32 devices: a whole 2x2x4 slice. The times are simulated.
32 devices in a mesh: dp: 16 (over z, x, core), mp: 2 (over y).
Axes of the slice: x: 2, y: 2, z: 4, core: 2. Of those that a mesh axis runs over, the one named last changes fastest.
Arguments:
- tokens: bfloat16 [12544, 768], P(('dp', 'mp')), may hold values from -6 to 6
- tissue: int32 [16, 784], P('dp'), may hold values from 0 to 1, as said below
- first_gain: float32 [768], replicated, may hold values from 0.5 to 1.5
- first_shift: float32 [768], replicated, may hold values from -3 to 3
- w_query: bfloat16 [768, 768], P(None, 'mp'), may hold values from -0.21875 to 0.21875
- b_query: float32 [768], P('mp'), may hold values from -3 to 3
- w_key: bfloat16 [768, 768], P(None, 'mp'), may hold values from -0.21875 to 0.21875
- w_value: bfloat16 [768, 768], P(None, 'mp'), may hold values from -0.21875 to 0.21875
- b_value: float32 [768], P('mp'), may hold values from -3 to 3
- w_output: bfloat16 [768, 768], P('mp'), may hold values from -1.75 to 1.75
- b_output: float32 [768], replicated, may hold values from -3 to 3
- second_gain: float32 [768], replicated, may hold values from 0.5 to 1.5
- second_shift: float32 [768], replicated, may hold values from -3 to 3
- w_upward: bfloat16 [768, 3072], P(None, 'mp'), may hold values from -0.21875 to 0.21875
- b_upward: float32 [3072], P('mp'), may hold values from -3 to 3
- w_down: bfloat16 [3072, 768], P('mp'), may hold values from -0.109375 to 0.109375
- b_down: float32 [768], replicated, may hold values from -3 to 3
- cotangent: bfloat16 [12544, 768], P(('dp', 'mp')), may hold values from -6 to 6
Outputs:
- output: bfloat16 [12544, 768], P(('dp', 'mp'))
- grad_tokens: float32 [12544, 768], P(('dp', 'mp'))
- grad_first_gain: float32 [768], replicated
- grad_first_shift: float32 [768], replicated
- grad_w_query: float32 [768, 768], P(None, 'mp')
- grad_b_query: float32 [768], P('mp')
- grad_w_key: float32 [768, 768], P(None, 'mp')
- grad_w_value: float32 [768, 768], P(None, 'mp')
- grad_b_value: float32 [768], P('mp')
- grad_w_output: float32 [768, 768], P('mp')
- grad_b_output: float32 [768], replicated
- grad_second_gain: float32 [768], replicated
- grad_second_shift: float32 [768], replicated
- grad_w_upward: float32 [768, 3072], P(None, 'mp')
- grad_b_upward: float32 [3072], P('mp')
- grad_w_down: float32 [3072, 768], P('mp')
- grad_b_down: float32 [768], replicated
Inputs may be any that keep to these rules, and one draw needn't show every extreme that they name: `tissue`: every image has from 196 to 784 patches marked 1, in no particular places.
All inputs are finite; a program needn't handle non-finite values.
Results may differ from a plain program's by a relative error of at most 0.015.
Values may be sent and summed in bfloat16 or wider, within the bound.
No kernel may reach another device: no remote copies, remote signals or barrier semaphores. Data moves between devices by JAX's collectives and lax.ppermute only.
A program may use at most 128 MiB of HBM per device.

v0:
```python
import jax
import jax.numpy as jnp
from jax import lax
from jax.sharding import PartitionSpec as P

HEAD = 64


epsilon = 1e-06
masked_score = -1e30


def normalize(values, gain, shift):
    average = jnp.mean(values, axis=-1, keepdims=True)
    centred = values - average
    spread = jnp.mean(centred * centred, axis=-1, keepdims=True)
    return centred * lax.rsqrt(spread + epsilon) * gain + shift


def exact_gelu(values):
    return jax.nn.gelu(values, approximate=False)


def head_layer(
    tokens,
    tissue,
    first_gain,
    first_shift,
    w_query,
    b_query,
    w_key,
    w_value,
    b_value,
    w_output,
    b_output,
    second_gain,
    second_shift,
    w_upward,
    b_upward,
    w_down,
    b_down,
    cotangent,
):
    images = tissue.shape[0]
    patches = tissue.shape[1]
    width_local = w_query.shape[1]
    heads_local = width_local // HEAD
    head_shape = (images, patches, heads_local, HEAD)
    group_rows = images * patches
    scale = HEAD ** (-0.5)
    inputs = tokens.astype(jnp.float32)
    normed1 = normalize(inputs, first_gain, first_shift).astype(jnp.bfloat16)
    gathered1 = lax.all_gather(normed1, "mp", axis=0, tiled=True)
    w_stack = jnp.concatenate([w_query, w_key, w_value], axis=1)
    b_stack = jnp.concatenate([b_query, jnp.zeros_like(b_query), b_value])
    stacked = (jnp.dot(gathered1, w_stack, preferred_element_type=jnp.float32) + b_stack).astype(
        jnp.bfloat16
    )
    queries = stacked[:, :width_local].reshape(head_shape)
    key_rows = stacked[:, width_local : 2 * width_local].reshape(head_shape)
    value_rows = stacked[:, 2 * width_local :].reshape(head_shape)
    valid_keys = (tissue > 0)[:, None, None, :]

    def masked_scores():
        raw_scores = (
            jnp.einsum("ipha,iqha->ihpq", queries, key_rows, preferred_element_type=jnp.float32)
            * scale
        )
        return jnp.where(valid_keys, raw_scores, masked_score)

    scores = masked_scores()
    highest = jnp.max(scores, axis=-1, keepdims=True)
    log_total = highest + jnp.log(jnp.sum(jnp.exp(scores - highest), axis=-1, keepdims=True))
    chance_low = jnp.exp(scores - log_total).astype(jnp.bfloat16)
    context = jnp.einsum(
        "ihpq,iqha->ipha", chance_low, value_rows, preferred_element_type=jnp.float32
    )
    context = context.reshape(group_rows, width_local).astype(jnp.bfloat16)
    part_rows = context
    attention = (
        lax.psum_scatter(
            jnp.dot(part_rows, w_output, preferred_element_type=jnp.float32).astype(jnp.bfloat16),
            "mp",
            scatter_dimension=0,
            tiled=True,
        ).astype(jnp.float32)
        + b_output
    )
    hidden1 = inputs + attention
    normed2 = normalize(hidden1, second_gain, second_shift).astype(jnp.bfloat16)
    gathered2 = lax.all_gather(normed2, "mp", axis=0, tiled=True)
    pre_gelu = jnp.dot(gathered2, w_upward, preferred_element_type=jnp.float32) + b_upward
    activated = exact_gelu(pre_gelu).astype(jnp.bfloat16)
    part_rows = activated
    branch_mlp = (
        lax.psum_scatter(
            jnp.dot(part_rows, w_down, preferred_element_type=jnp.float32).astype(jnp.bfloat16),
            "mp",
            scatter_dimension=0,
            tiled=True,
        ).astype(jnp.float32)
        + b_down
    )
    output = (hidden1 + branch_mlp).astype(jnp.bfloat16)
    grad_rows = lax.all_gather(cotangent, "mp", axis=0, tiled=True)
    grad_down = jnp.einsum("gf,gd->fd", activated, grad_rows, preferred_element_type=jnp.float32)
    grad_active = jnp.einsum("gd,fd->gf", grad_rows, w_down, preferred_element_type=jnp.float32)
    gelu_back = jax.vjp(exact_gelu, pre_gelu)[1]
    grad_pre = gelu_back(grad_active)[0].astype(jnp.bfloat16)
    grad_upward = jnp.einsum("gd,gf->df", gathered2, grad_pre, preferred_element_type=jnp.float32)
    grad_bupward = jnp.sum(grad_pre.astype(jnp.float32), axis=0)
    part_rows = grad_pre
    grad_normed2 = lax.psum_scatter(
        jnp.einsum("gf,df->gd", part_rows, w_upward, preferred_element_type=jnp.float32).astype(
            jnp.bfloat16
        ),
        "mp",
        scatter_dimension=0,
        tiled=True,
    ).astype(jnp.float32)
    norm2_back = jax.vjp(normalize, hidden1, second_gain, second_shift)[1]
    grad_hidden, grad_gain2, grad_shift2 = norm2_back(grad_normed2)
    cotangent_f = cotangent.astype(jnp.float32)
    grad_hidden = grad_hidden + cotangent_f
    grad_bdown = jnp.sum(cotangent_f, axis=0)
    grad_branch = grad_hidden.astype(jnp.bfloat16)
    grad_boutput = jnp.sum(grad_branch.astype(jnp.float32), axis=0)
    grad_columns = lax.all_gather(grad_branch, "mp", axis=0, tiled=True)
    grad_woutput = jnp.einsum(
        "gc,gd->cd", context, grad_columns, preferred_element_type=jnp.float32
    )
    grad_context = jnp.einsum(
        "gd,cd->gc", grad_columns, w_output, preferred_element_type=jnp.float32
    )
    grad_context = grad_context.astype(jnp.bfloat16).reshape(head_shape)
    chances = jnp.exp(masked_scores() - log_total)
    grad_chances = jnp.einsum(
        "ipha,iqha->ihpq", grad_context, value_rows, preferred_element_type=jnp.float32
    )
    grad_value = jnp.einsum(
        "ihpq,ipha->iqha",
        chances.astype(jnp.bfloat16),
        grad_context,
        preferred_element_type=jnp.float32,
    ).astype(jnp.bfloat16)
    grad_scores = chances * (grad_chances - jnp.sum(chances * grad_chances, axis=-1, keepdims=True))
    grad_scores = grad_scores.astype(jnp.bfloat16)
    grad_query = (
        jnp.einsum("ihpq,iqha->ipha", grad_scores, key_rows, preferred_element_type=jnp.float32)
        * scale
    ).astype(jnp.bfloat16)
    grad_key = (
        jnp.einsum("ihpq,ipha->iqha", grad_scores, queries, preferred_element_type=jnp.float32)
        * scale
    ).astype(jnp.bfloat16)
    grad_stack = jnp.concatenate(
        [
            grad_query.reshape(group_rows, width_local),
            grad_key.reshape(group_rows, width_local),
            grad_value.reshape(group_rows, width_local),
        ],
        axis=1,
    )
    grad_wstack = jnp.einsum("gd,gc->dc", gathered1, grad_stack, preferred_element_type=jnp.float32)
    stack_sums = jnp.sum(grad_stack.astype(jnp.float32), axis=0)
    part_rows = grad_stack
    grad_normed1 = lax.psum_scatter(
        jnp.einsum("gc,dc->gd", part_rows, w_stack, preferred_element_type=jnp.float32).astype(
            jnp.bfloat16
        ),
        "mp",
        scatter_dimension=0,
        tiled=True,
    ).astype(jnp.float32)
    norm1_back = jax.vjp(normalize, inputs, first_gain, first_shift)[1]
    grad_inputs, grad_gain1, grad_shift1 = norm1_back(grad_normed1)
    grad_tokens = grad_hidden + grad_inputs
    weight_grads = (
        grad_wstack[:, :width_local],
        stack_sums[:width_local],
        grad_wstack[:, width_local : 2 * width_local],
        grad_wstack[:, 2 * width_local :],
        stack_sums[2 * width_local :],
        grad_woutput,
        grad_upward,
        grad_bupward,
        grad_down,
    )
    small_grads = (grad_gain1, grad_shift1, grad_boutput, grad_gain2, grad_shift2, grad_bdown)
    return (output, grad_tokens, small_grads, weight_grads)


def local(
    tokens,
    tissue,
    first_gain,
    first_shift,
    w_query,
    b_query,
    w_key,
    w_value,
    b_value,
    w_output,
    b_output,
    second_gain,
    second_shift,
    w_upward,
    b_upward,
    w_down,
    b_down,
    cotangent,
):
    arguments = (
        tokens,
        tissue,
        first_gain,
        first_shift,
        w_query,
        b_query,
        w_key,
        w_value,
        b_value,
        w_output,
        b_output,
        second_gain,
        second_shift,
        w_upward,
        b_upward,
        w_down,
        b_down,
        cotangent,
    )
    output, grad_tokens, small_grads, weight_grads = head_layer(*arguments)
    (
        grad_wquery,
        grad_bquery,
        grad_wkey,
        grad_wvalue,
        grad_bvalue,
        grad_woutput,
        grad_upward,
        grad_bupward,
        grad_down,
    ) = weight_grads
    (
        grad_wquery,
        grad_bquery,
        grad_wkey,
        grad_wvalue,
        grad_bvalue,
        grad_woutput,
        grad_upward,
        grad_bupward,
        grad_down,
    ) = lax.psum(
        (
            grad_wquery,
            grad_bquery,
            grad_wkey,
            grad_wvalue,
            grad_bvalue,
            grad_woutput,
            grad_upward,
            grad_bupward,
            grad_down,
        ),
        "dp",
    )
    grad_gain1, grad_shift1, grad_boutput, grad_gain2, grad_shift2, grad_bdown = small_grads
    grad_gain1, grad_shift1, grad_boutput, grad_gain2, grad_shift2, grad_bdown = lax.psum(
        (grad_gain1, grad_shift1, grad_boutput, grad_gain2, grad_shift2, grad_bdown), ("dp", "mp")
    )
    return (
        output,
        grad_tokens,
        grad_gain1,
        grad_shift1,
        grad_wquery,
        grad_bquery,
        grad_wkey,
        grad_wvalue,
        grad_bvalue,
        grad_woutput,
        grad_boutput,
        grad_gain2,
        grad_shift2,
        grad_upward,
        grad_bupward,
        grad_down,
        grad_bdown,
    )


def solution(mesh):
    in_specs = (
        P(("dp", "mp"), None),
        P("dp", None),
        P(),
        P(),
        P(None, "mp"),
        P("mp"),
        P(None, "mp"),
        P(None, "mp"),
        P("mp"),
        P("mp", None),
        P(),
        P(),
        P(),
        P(None, "mp"),
        P("mp"),
        P("mp", None),
        P(),
        P(("dp", "mp"), None),
    )
    out_specs = (
        P(("dp", "mp"), None),
        P(("dp", "mp"), None),
        P(),
        P(),
        P(None, "mp"),
        P("mp"),
        P(None, "mp"),
        P(None, "mp"),
        P("mp"),
        P("mp", None),
        P(),
        P(),
        P(),
        P(None, "mp"),
        P("mp"),
        P("mp", None),
        P(),
    )
    return jax.shard_map(local, mesh=mesh, in_specs=in_specs, out_specs=out_specs, check_vma=False)
```

profile of v0, /device:TPU:0, one launch (start us, length us, event | category | flops | bytes accessed | tf_op | source)
XLA Modules:
  0.0 604.2 jit_solution(9951858389328352436)
XLA Ops:
  17.1 21.1 %all-gather.5.cloned.1.call-done = bf16[784,768]{1,0:T(8,128)(2,1)} async-done(((bf16[392,768]{1,0:T(8,128)(2,1)}), bf16[784,768]{1,0:T(8,128)(2,1)}) %all-gather.5.cloned.1.call-update) | async-done | bytes 1204240 | tf_op jit(solution)/shard_map/all_gather | solution.py:53
  38.2 3.5 fusion.8
  48.5 10.4 %fusion = (f32[6,784]{1,0:T(8,128)S(1)}, f32[6,784,784]{1,2,0:T(8,128)}) fusion(pred[784]{0:T(1024)(128)(4,1)S(1)} %compare_reduce_fusion, bf16[784,6,64]{0,2,1:T(8,128)(2,1)} %bitcast.58, bf16[784,6,64]{0,2,1:T(8,128)(2,1)} %bitcast.60), kind=kOutput, calls=%fused_computation.5 | convolution fusion | flops 483114912 | bytes 15975568 | tf_op jit(solution)/shard_map/ipha,iqha->ihpq/dot_general | solution.py:66
  58.9 9.3 %exponential_reduce_fusion = f32[6,784]{1,0:T(8,128)S(1)} fusion(f32[6,784,784]{1,2,0:T(8,128)} %get-tuple-element.58, f32[6,784]{1,0:T(8,128)S(1)} %get-tuple-element.57, pred[784]{0:T(1024)(128)(4,1)S(1)} %compare_reduce_fusion), kind=kLoop, calls=%fused_computation.3 | loop fusion | flops 14747040 | bytes 14790160 | tf_op jit(solution)/shard_map/reduce_sum | solution.py:73
  68.2 8.3 %fusion.1 = bf16[6,784,784]{1,2,0:T(8,128)(2,1)S(1)} fusion(f32[6,784,784]{1,2,0:T(8,128)} %get-tuple-element.58, f32[6,784]{1,0:T(8,128)S(1)} %log_add_fusion, pred[784]{0:T(1024)(128)(4,1)S(1)} %compare_reduce_fusion), kind=kLoop, calls=%fused_computation.6 | loop fusion | flops 14751744 | bytes 22147216 | tf_op jit(solution)/shard_map/convert_element_type | solution.py:74
  82.6 22.1 %reduce-scatter.5.cloned.1.call-done = bf16[392,768]{1,0:T(8,128)(2,1)} async-done(((bf16[784,768]{1,0:T(8,128)(2,1)}), bf16[392,768]{1,0:T(8,128)(2,1)}) %reduce-scatter.5.cloned.1.call-update) | async-done | bytes 602128 | tf_op jit(solution)/shard_map/reduce_scatter | solution.py:81
  109.4 22.6 %all-gather.7.cloned.1.call-done = bf16[784,768]{1,0:T(8,128)(2,1)} async-done(((bf16[392,768]{1,0:T(8,128)(2,1)}), bf16[784,768]{1,0:T(8,128)(2,1)}) %all-gather.7.cloned.1.call-update) | async-done | bytes 1204240 | tf_op jit(solution)/shard_map/all_gather | solution.py:91
  132.0 6.3 %fusion.39 = f32[784,1536]{1,0:T(8,128)} fusion(bf16[784,768]{1,0:T(8,128)(2,1)} %all-gather.7.cloned.1.call-done, bf16[768,1536]{1,0:T(8,128)(2,1)} %param.31), kind=kOutput, calls=%fused_computation.98 | convolution fusion | flops 1849688064 | bytes 8380416 | tf_op jit(solution)/shard_map/dot_general | solution.py:92
  138.3 18.2 %all-gather.9.cloned.1.call-done = bf16[784,768]{1,0:T(8,128)(2,1)} async-done(((bf16[392,768]{1,0:T(8,128)(2,1)}), bf16[784,768]{1,0:T(8,128)(2,1)}) %all-gather.9.cloned.1.call-update) | async-done | bytes 1204240 | tf_op jit(solution)/shard_map/all_gather | solution.py:105
  156.5 15.6 %convert_reduce_fusion = (f32[1536]{0:T(1024)S(1)}, bf16[784,1536]{1,0:T(8,128)(2,1)S(1)}, f32[784,1536]{1,0:T(8,128)}) fusion(f32[784,1536]{1,0:T(8,128)} %fusion.39, f32[1536]{0:T(1024)S(1)} %copy-done.39, bf16[784,768]{1,0:T(8,128)(2,1)} %all-gather.9.cloned.1.call-done, bf16[1536,768]{1,0:T(8,128)(2,1)S(1)} %copy-done), kind=kOutput, calls=%fused_computation.9 | convolution fusion | flops 1940003328 | bytes 15618048 | tf_op jit(solution)/shard_map/gd,fd->gf/dot_general | solution.py:107
  176.7 5.0 multiply_convert_fusion.1
  186.3 12.5 %reduce-scatter.9.cloned.1.call-done = bf16[392,768]{1,0:T(8,128)(2,1)} async-done(((bf16[784,768]{1,0:T(8,128)(2,1)}), bf16[392,768]{1,0:T(8,128)(2,1)}) %reduce-scatter.9.cloned.1.call-update) | async-done | bytes 602128 | tf_op jit(solution)/shard_map/reduce_scatter | solution.py:113
  200.7 22.3 %reduce-scatter.7.cloned.1.call-done = bf16[392,768]{1,0:T(8,128)(2,1)} async-done(((bf16[784,768]{1,0:T(8,128)(2,1)}), bf16[392,768]{1,0:T(8,128)(2,1)}) %reduce-scatter.7.cloned.1.call-update) | async-done | bytes 602128 | tf_op jit(solution)/shard_map/reduce_scatter | solution.py:96
  227.9 8.4 %reduce-scatter.11.cloned.1.call-start = ((), (), s32[]{:S(2)}) async-start(), calls=%async_computation.11 | async-start | bytes 1806336 | tf_op jit(solution)/shard_map/reduce_scatter | solution.py:167
  236.3 14.8 %all-gather.11.cloned.1.call-done = bf16[784,768]{1,0:T(8,128)(2,1)} async-done(((bf16[392,768]{1,0:T(8,128)(2,1)}), bf16[784,768]{1,0:T(8,128)(2,1)}) %all-gather.11.cloned.1.call-update) | async-done | bytes 1204240 | tf_op jit(solution)/shard_map/all_gather | solution.py:128
  254.5 6.4 %convolution_convert_fusion.4 = bf16[6,64,784]{2,1,0:T(8,128)(2,1)S(1)} fusion(bf16[784,6,64]{0,2,1:T(8,128)(2,1)} %bitcast.64, bf16[6,784,784]{1,2,0:T(8,128)(2,1)} %copy-done.2), kind=kOutput, calls=%fused_computation.57 | convolution fusion | flops 472356864 | bytes 8580096 | tf_op jit(solution)/shard_map/ihpq,ipha->iqha/dot_general | solution.py:140
  261.0 12.1 %multiply_reduce_fusion = (f32[6,784]{1,0:T(8,128)S(1)}, f32[6,784,784]{1,2,0:T(8,128)}) fusion(f32[6,784,784]{1,2,0:T(8,128)} %get-tuple-element.58, f32[6,784]{1,0:T(8,128)S(1)} %log_add_fusion, pred[784]{0:T(1024)(128)(4,1)S(1)} %compare_reduce_fusion, bf16[784,6,64]{0,2,1:T(8,128)(2,1)S(1)} %bitcast.65, bf16[784,6,64]{0,2,1:T(8,128)(2,1)S(1)} %bitcast.63), kind=kOutput, calls=%fused_computation.1 | convolution fusion | flops 490490784 | bytes 30746128 | tf_op jit(solution)/shard_map/ipha,iqha->ihpq/dot_general | solution.py:137
  273.0 12.3 %multiply_convert_fusion = bf16[6,784,784]{1,2,0:T(8,128)(2,1)S(1)} fusion(f32[6,784,784]{1,2,0:T(8,128)} %get-tuple-element.60, f32[6,784,784]{1,2,0:T(8,128)} %get-tuple-element.58, f32[6,784]{1,0:T(8,128)S(1)} %get-tuple-element.59, f32[6,784]{1,0:T(8,128)S(1)} %log_add_fusion, pred[784]{0:T(1024)(128)(4,1)S(1)} %compare_reduce_fusion), kind=kLoop, calls=%fused_computation | loop fusion | flops 22127616 | bytes 36917776 | tf_op jit(solution)/shard_map/convert_element_type | solution.py:147
  290.7 4.5 convolution_convert_fusion
  295.5 7.0 %fusion.41 = f32[768,1536]{1,0:T(8,128)} fusion(bf16[784,768]{1,0:T(8,128)(2,1)} %all-gather.7.cloned.1.call-done, bf16[784,1536]{1,0:T(8,128)(2,1)} %copy-done.21), kind=kOutput, calls=%fused_computation.100 | convolution fusion | flops 1849688064 | bytes 8331264 | tf_op jit(solution)/shard_map/gd,gf->df/dot_general | solution.py:110
  302.5 4.4 fusion.42
  315.4 64.0 %all-reduce.1 = (f32[384]{0:T(512)}, f32[384]{0:T(512)}, f32[1536]{0:T(1024)}) all-reduce(f32[384]{0:T(512)S(1)} %get-tuple-element.56, f32[384]{0:T(512)S(1)} %get-tuple-element.55, f32[1536]{0:T(1024)S(1)} %get-tuple-element.39), channel_id=1, replica_groups=mesh['dp'=16,'mp'=2] {'dp'}, use_global_device_ids=true, to_apply=%region_21.22 | all-reduce | flops 2304 | bytes 18432 | tf_op jit(solution)/shard_map/psum | solution.py:255
  385.6 39.1 %all-reduce = (f32[768]{0:T(1024)}, f32[768]{0:T(1024)}, f32[768]{0:T(1024)}, f32[768]{0:T(1024)}, f32[768]{0:T(1024)}, /*index=5*/f32[768]{0:T(1024)}) all-reduce(f32[768]{0:T(1024)S(1)} %get-tuple-element.19, f32[768]{0:T(1024)S(1)} %get-tuple-element.22, ...), channel_id=1, replica_groups=mesh['dp'=16,'mp'=2] {'dp','mp'}, use_global_device_ids=true, to_apply=%region_16.17 | all-reduce | flops 4608 | bytes 36864 | tf_op jit(solution)/shard_map/psum | solution.py:270
  424.7 160.8 %all-reduce.5.cloned.1.call-done = (f32[768,384]{1,0:T(8,128)}, f32[768,384]{1,0:T(8,128)}, f32[768,384]{1,0:T(8,128)}, f32[384,768]{1,0:T(8,128)}, f32[768,1536]{1,0:T(8,128)}, /*index=5*/f32[1536,768]{1,0:T(8,128)}) async-done(((f32[768,384]{1,0:T(8,128)}, f32[768,384]{1,0:T(8,128)}, f32[768,384]{1,0:T(8,128)}, f32[384,768]{1,0:T(8,128)}, f32[768,1536]{1,0:T(8,128)}, /*index=5*/f32[1536,768]{1,0:T(8,128)}), ...) | async-done | bytes 14155792 | tf_op jit(solution)/shard_map/psum | solution.py:255
  (169 shorter events, 78.8 us)
Async XLA Ops:
  7.2 149.3 %copy-start = (bf16[1536,768]{1,0:T(8,128)(2,1)S(1)}, bf16[1536,768]{1,0:T(8,128)(2,1)}, u32[]{:S(2)}) copy-start(bf16[1536,768]{1,0:T(8,128)(2,1)} %param.33) | copy-start | bytes 7077892
  7.2 31.0 %all-gather.5.cloned.1.call-start = ((), (), s32[]{:S(2)}) async-start(), calls=%async_computation.4 | async-start | bytes 1806336 | tf_op jit(solution)/shard_map/all_gather | solution.py:53
  12.3 92.4 %reduce-scatter.5.cloned.1.call-start = ((), (), s32[]{:S(2)}) async-start(), calls=%async_computation.5 | async-start | bytes 1806336 | tf_op jit(solution)/shard_map/reduce_scatter | solution.py:81
  79.8 24.9 %copy-start.3 = (bf16[392,768]{1,0:T(8,128)(2,1)S(1)}, bf16[392,768]{1,0:T(8,128)(2,1)}, u32[]{:S(2)}) copy-start(bf16[392,768]{1,0:T(8,128)(2,1)} %param.18) | copy-start | bytes 1806340
  79.8 24.9 %copy-start.30 = (f32[768]{0:T(1024)S(1)}, f32[768]{0:T(1024)}, u32[]{:S(2)}) copy-start(f32[768]{0:T(1024)} %param.28) | copy-start | bytes 9220
  82.5 25.1 %copy-start.34 = (f32[768]{0:T(1024)S(1)}, f32[768]{0:T(1024)}, u32[]{:S(2)}) copy-start(f32[768]{0:T(1024)} %param.29) | copy-start | bytes 9220
  82.5 25.1 %copy-start.40 = (f32[768]{0:T(1024)S(1)}, f32[768]{0:T(1024)}, u32[]{:S(2)}) copy-start(f32[768]{0:T(1024)} %param.30) | copy-start | bytes 9220
  82.5 49.5 %all-gather.7.cloned.1.call-start = ((), (), s32[]{:S(2)}) async-start(), calls=%async_computation.6 | async-start | bytes 1806336 | tf_op jit(solution)/shard_map/all_gather | solution.py:91
  108.8 47.7 %all-gather.9.cloned.1.call-start = ((), (), s32[]{:S(2)}) async-start(), calls=%async_computation.8 | async-start | bytes 1806336 | tf_op jit(solution)/shard_map/all_gather | solution.py:105
  109.4 47.1 %copy-start.39 = (f32[1536]{0:T(1024)S(1)}, f32[1536]{0:T(1024)}, u32[]{:S(2)}) copy-start(f32[1536]{0:T(1024)} %param.32) | copy-start | bytes 18436
  109.4 89.4 %reduce-scatter.9.cloned.1.call-start = ((), (), s32[]{:S(2)}) async-start(), calls=%async_computation.9 | async-start | bytes 1806336 | tf_op jit(solution)/shard_map/reduce_scatter | solution.py:113
  156.5 17.0 %copy-start.43 = (bf16[768,1536]{1,0:T(8,128)(2,1)S(1)}, bf16[768,1536]{1,0:T(8,128)(2,1)}, u32[]{:S(2)}) copy-start(bf16[768,1536]{1,0:T(8,128)(2,1)} %param.31) | copy-start | bytes 7077892
  176.6 46.3 %reduce-scatter.7.cloned.1.call-start = ((), (), s32[]{:S(2)}) async-start(), calls=%async_computation.7 | async-start | bytes 1806336 | tf_op jit(solution)/shard_map/reduce_scatter | solution.py:96
  186.3 36.7 %copy-start.5 = (bf16[392,768]{1,0:T(8,128)(2,1)S(1)}, bf16[392,768]{1,0:T(8,128)(2,1)}, u32[]{:S(2)}) copy-start(bf16[392,768]{1,0:T(8,128)(2,1)} %reduce-scatter.5.cloned.1.call-done) | copy-start | bytes 1806340
  186.3 36.7 %copy-start.41 = (f32[768]{0:T(1024)S(1)}, f32[768]{0:T(1024)}, u32[]{:S(2)}) copy-start(f32[768]{0:T(1024)} %param.34) | copy-start | bytes 9220
  186.3 64.8 %all-gather.11.cloned.1.call-start = ((), (), s32[]{:S(2)}) async-start(), calls=%async_computation.10 | async-start | bytes 1806336 | tf_op jit(solution)/shard_map/all_gather | solution.py:128
  227.9 151.5 %reduce-scatter.11.cloned.1.call-start = ((), (), s32[]{:S(2)}) async-start(), calls=%async_computation.11 | async-start | bytes 1806336 | tf_op jit(solution)/shard_map/reduce_scatter | solution.py:167
  261.0 28.9 %copy-start.13 = (bf16[6,64,784]{2,1,0:T(8,128)(2,1)}, bf16[6,64,784]{2,1,0:T(8,128)(2,1)S(1)}, u32[]{:S(2)}) copy-start(bf16[6,64,784]{2,1,0:T(8,128)(2,1)S(1)} %convolution_convert_fusion.4) | copy-start | bytes 1806340
  273.0 12.3 %copy-start.6 = (bf16[784,384]{0,1:T(8,128)(2,1)S(1)}, bf16[784,384]{0,1:T(8,128)(2,1)}, u32[]{:S(2)}) copy-start(bf16[784,384]{0,1:T(8,128)(2,1)} %copy.48) | copy-start | bytes 1806340
  295.2 290.3 %all-reduce.5.cloned.1.call-start = ((), (), s32[]{:S(2)}) async-start(), calls=%async_computation.12 | async-start | bytes 28311552 | tf_op jit(solution)/shard_map/psum | solution.py:255
  313.4 66.1 %copy-start.32 = (f32[392]{0:T(512)S(1)}, f32[392]{0:T(512)}, u32[]{:S(2)}) copy-start(f32[392]{0:T(512)} %copy-done.31) | copy-start | bytes 4708
  313.4 66.1 %copy-start.33 = (f32[768]{0:T(1024)S(1)}, f32[768]{0:T(1024)}, u32[]{:S(2)}) copy-start(f32[768]{0:T(1024)} %param.20) | copy-start | bytes 9220
  313.4 67.7 %copy-start.38 = (f32[392]{0:T(512)S(1)}, f32[392]{0:T(512)}, u32[]{:S(2)}) copy-start(f32[392]{0:T(512)} %copy-done.37) | copy-start | bytes 4708
  313.4 67.7 %copy-start.36 = (f32[392]{0:T(512)S(1)}, f32[392]{0:T(512)}, u32[]{:S(2)}) copy-start(f32[392]{0:T(512)} %copy-done.35) | copy-start | bytes 4708
  (35 other events, 144.6 us)
Sparse Core Ops, SparseCore 0:
  12.4 25.7 all-gather.4
  82.6 22.0 reduce-scatter.4
  108.9 23.0 all-gather.6
  133.4 23.0 all-gather.8
  176.7 22.0 reduce-scatter.8
  200.9 22.0 reduce-scatter.6
  228.0 23.0 all-gather.10
  295.3 22.0 reduce-scatter.10
  323.7 261.7 all-reduce.4
where the time goes:
time: 613 us; the launch traced here: 604 us
  waiting for transfers between devices  295 us (48%)
  blocking collectives  103 us (17%)
  matrix products  90.6 us (15%)
  other arithmetic  60.9 us (10%)
  local copies, waits for them, and re-layouts  31.1 us (5%)
  between operations  14.6 us (2%)
  starting transfers between devices  8.92 us (1%)
    psum x1, waiting for transfers between devices, local(): lax.psum((grad_wquery, grad_bquery, grad_wkey, grad_wvalue, grad_bvalue,...  161 us
    psum x1, blocking collectives, local(): lax.psum((grad_wquery, grad_bquery, grad_wkey, grad_wvalue, grad_bvalue,...  64 us
    psum x1, blocking collectives, local(): lax.psum((grad_gain1, grad_shift1, grad_boutput, grad_gain2, grad_shift2,...  39.1 us
    all_gather x1, waiting for transfers between devices, head_layer(): gathered2 = lax.all_gather(normed2, 'mp', axis=0, tiled=True)  22.6 us
    reduce_scatter x1, waiting for transfers between devices, head_layer(): lax.psum_scatter(jnp.dot(part_rows, w_down, preferred_element_type=jnp.fl...  22.3 us
    reduce_scatter x1, waiting for transfers between devices, head_layer(): lax.psum_scatter(jnp.dot(part_rows, w_output, preferred_element_type=jnp....  22.1 us
    all_gather x1, waiting for transfers between devices, head_layer(): gathered1 = lax.all_gather(normed1, 'mp', axis=0, tiled=True)  21.1 us
    unnamed x108, local copies, waits for them, and re-layouts  20.5 us
  transfers between devices with their start and end apart: 9, of which 8 were waited for; matrix products, arithmetic and copies ran while one was open for 8% of the time, Pallas kernels for 0%

commit v1 on v0

v1 whole, which is shorter than its diff:
```python
import functools

import jax
import jax.numpy as jnp
from jax import lax
from jax.experimental import pallas as pl
from jax.experimental.pallas import tpu as pltpu
from jax.sharding import PartitionSpec as P

HEAD = 64
LANES = 256
epsilon = 1e-06
masked_score = -1e30
low, wide = jnp.bfloat16, jnp.float32
params = pltpu.CompilerParams(vmem_limit_bytes=48 << 20)


def cost(flops, moved, exps=0):
    return pl.CostEstimate(flops=flops, bytes_accessed=moved, transcendentals=exps)


def whole(array):
    return pl.BlockSpec(array.shape, lambda *_: (0,) * len(array.shape))


def shaped(shape, kind):
    return jax.ShapeDtypeStruct(shape, kind)


def mm(left, right, left_dim, right_dim):
    return lax.dot_general(
        left, right, (((left_dim,), (right_dim,)), ((), ())), preferred_element_type=wide
    )


def normalize(values, gain, shift):
    centred = values - jnp.mean(values, axis=-1, keepdims=True)
    spread = jnp.mean(centred * centred, axis=-1, keepdims=True)
    return centred * lax.rsqrt(spread + epsilon) * gain + shift


def normalize_back(values, gain, grad):
    centred = values - jnp.mean(values, axis=-1, keepdims=True)
    inverse = lax.rsqrt(jnp.mean(centred * centred, axis=-1, keepdims=True) + epsilon)
    unit = centred * inverse
    scaled = grad * gain
    by_values = inverse * (
        scaled
        - jnp.mean(scaled, axis=-1, keepdims=True)
        - unit * jnp.mean(scaled * unit, axis=-1, keepdims=True)
    )
    return by_values, jnp.sum(grad * unit, axis=0), jnp.sum(grad, axis=0)


def spans(extent):
    edges = list(range(0, extent, LANES))
    if len(edges) > 1 and extent - edges[-1] < LANES // 2:
        edges.pop()
    return list(zip(edges, edges[1:] + [extent]))


def split_three(row):
    first = row.astype(low).astype(wide)
    second = (row - first).astype(low).astype(wide)
    return first, second, row - first - second


def head_rows(part, width, head):
    return pl.ds(pl.multiple_of(part * width + head * HEAD, HEAD), HEAD)


def attention_forward_kernel(
    own_ref, other_ref, vectors_ref, w_ref, b_ref, bias_ref, qkv_ref, own_context_ref, other_context_ref, exact_ref,
    log_ref, turned_ref
):
    head = pl.program_id(0)
    own = own_ref.shape[0]
    rows = 2 * own
    width = w_ref.shape[0] // 3

    @pl.when(head == 0)
    def _():
        gain, shift = vectors_ref[0:1], vectors_ref[1:2]
        normed = jnp.concatenate(
            [normalize(ref[...].astype(wide), gain, shift) for ref in (own_ref, other_ref)], axis=0
        ).astype(low)
        turned_ref[...] = normed.T
        for part in range(3):
            at = slice(part * width, (part + 1) * width)
            qkv_ref[at] = (mm(w_ref[at], normed, 1, 1) + b_ref[at]).astype(low)

    queries = qkv_ref[head_rows(0, width, head)] * jnp.array(HEAD**-0.5, low)
    keys = jnp.concatenate([qkv_ref[head_rows(1, width, head)], bias_ref[...]], axis=0).T
    values = qkv_ref[head_rows(2, width, head)]
    index = lax.broadcasted_iota(jnp.int32, (16, rows), 0)
    queries = jnp.concatenate([queries, jnp.where(index == 0, 1.0, 0.0).astype(low)], axis=0)
    pieces = []
    for start, stop in spans(rows):
        scores = mm(keys, queries[:, start:stop], 1, 0)
        highest = jnp.max(scores, axis=0, keepdims=True)
        powers = jnp.exp(scores - highest)
        total = jnp.sum(powers, axis=0, keepdims=True)
        log_ref[0, :, start:stop] = highest + jnp.log(total)
        pieces.append(mm(values, powers.astype(low), 1, 0) * (1.0 / total))
    context = jnp.concatenate(pieces, axis=1)
    exact_ref[...] = context
    context = context.astype(low)
    own_context_ref[...] = context[:, :own]
    other_context_ref[...] = context[:, own:]


def attention_forward(own, other, vectors, w, b, bias):
    count, features = own.shape
    width = w.shape[0] // 3
    rows = 2 * count
    by_head = lambda columns: pl.BlockSpec((HEAD, columns), lambda head: (head, 0))
    return pl.pallas_call(
        attention_forward_kernel,
        name="attention_forward",
        grid=(width // HEAD,),
        in_specs=[whole(a) for a in (own, other, vectors, w, b, bias)],
        out_specs=[
            pl.BlockSpec((3 * width, rows), lambda head: (0, 0)),
            by_head(count),
            by_head(count),
            by_head(rows),
            pl.BlockSpec((1, 1, rows), lambda head: (head, 0, 0)),
            pl.BlockSpec((features, rows), lambda head: (0, 0)),
        ],
        out_shape=[
            shaped((3 * width, rows), low),
            shaped((width, count), low),
            shaped((width, count), low),
            shaped((width, rows), wide),
            shaped((width // HEAD, 1, rows), wide),
            shaped((features, rows), low),
        ],
        compiler_params=params,
        cost_estimate=cost(10 * 10**9, 10**7, 4 * 10**6),
    )(own, other, vectors, w, b, bias)


def attention_backward_kernel(qkv_ref, exact_ref, log_ref, bias_ref, own_grad_ref, other_grad_ref, out_ref):
    head = pl.program_id(0)
    rows = qkv_ref.shape[1]
    width = qkv_ref.shape[0] // 3
    scale = HEAD**-0.5
    queries = qkv_ref[head_rows(0, width, head)] * jnp.array(scale, low)
    keys = qkv_ref[head_rows(1, width, head)]
    values = qkv_ref[head_rows(2, width, head)]
    grads = jnp.concatenate([own_grad_ref[...], other_grad_ref[...]], axis=1)
    overlap = jnp.sum(grads.astype(wide) * exact_ref[...], axis=0, keepdims=True)
    index = lax.broadcasted_iota(jnp.int32, (16, rows), 0)

    def stack(top, *extra):
        block = jnp.zeros((16, rows), wide)
        for place, row in enumerate(extra):
            block = jnp.where(index == place, row, block)
        return jnp.concatenate([top, block.astype(low)], axis=0)

    bias = bias_ref[0:1].astype(wide)
    queries_more = stack(queries, 1.0, *split_three(-log_ref[0]))
    keys_more = stack(keys, bias, 1.0, 1.0, 1.0).T
    grads_more = stack(grads, *split_three(-overlap))
    values_more = stack(values, 1.0, 1.0, 1.0).T
    grad_keys = jnp.zeros((HEAD, rows), wide)
    grad_values = jnp.zeros((HEAD, rows), wide)
    for start, stop in spans(rows):
        at = slice(start, stop)
        chances = jnp.exp(mm(keys_more, queries_more[:, at], 1, 0))
        grad_values = grad_values + mm(grads[:, at], chances.astype(low), 1, 1)
        grad_scores = (chances * mm(values_more, grads_more[:, at], 1, 0)).astype(low)
        out_ref[head_rows(0, width, head), at] = (mm(keys, grad_scores, 1, 0) * scale).astype(low)
        grad_keys = grad_keys + mm(queries[:, at], grad_scores, 1, 1)
    out_ref[head_rows(1, width, head)] = grad_keys.astype(low)
    out_ref[head_rows(2, width, head)] = grad_values.astype(low)


def attention_backward(qkv, exact, logs, bias, own_grad, other_grad):
    rows = qkv.shape[1]
    width = qkv.shape[0] // 3
    by_head = lambda columns: pl.BlockSpec((HEAD, columns), lambda head: (head, 0))
    return pl.pallas_call(
        attention_backward_kernel,
        name="attention_backward",
        grid=(width // HEAD,),
        in_specs=[
            whole(qkv),
            by_head(rows),
            pl.BlockSpec((1, 1, rows), lambda head: (head, 0, 0)),
            whole(bias),
            by_head(rows // 2),
            by_head(rows // 2),
        ],
        out_specs=whole(qkv),
        out_shape=shaped(qkv.shape, low),
        compiler_params=params,
        cost_estimate=cost(10 * 10**9, 10**7, 4 * 10**6),
    )(qkv, exact, logs, bias, own_grad, other_grad)


def gelu_both(values):
    below = 0.5 * (1.0 + lax.erf(values * (0.5**0.5)))
    density = jnp.exp(values * values * -0.5) * (2.0 * jnp.pi) ** -0.5
    return values * below, below + values * density


def feed_forward_kernel(
    tokens_ref, mine_ref, peer_ref, w_mine_ref, w_peer_ref, vectors_ref, cotangent_ref, up_ref, b_up_ref, down_ref,
    hidden_ref, normed_ref, activated_ref, grad_pre_ref, grad_normed_ref, branch_ref, grad_b_ref, grad_sum, sum_
):
    step = pl.program_id(0)

    @pl.when(step == 0)
    def _():
        attention = mm(mine_ref[...], w_mine_ref[...], 0, 0) + mm(peer_ref[...], w_peer_ref[...], 0, 0)
        hidden = tokens_ref[...].astype(wide) + (attention + vectors_ref[2:3])
        hidden_ref[...] = hidden
        normed_ref[...] = normalize(hidden, vectors_ref[3:4], vectors_ref[4:5]).astype(low)
        grad_sum[...] = jnp.zeros_like(grad_sum)
        sum_[...] = jnp.zeros_like(sum_)

    up, down = up_ref[...], down_ref[...]
    pre_gelu = mm(normed_ref[...], up, 1, 0) + b_up_ref[...]
    grad_active = mm(cotangent_ref[...], down, 1, 1)
    activated, slope = gelu_both(pre_gelu)
    activated = activated.astype(low)
    grad_pre = (grad_active * slope).astype(low)
    activated_ref[...] = activated
    grad_pre_ref[...] = grad_pre
    grad_b_ref[...] = jnp.sum(grad_pre.astype(wide), axis=0, keepdims=True)
    grad_sum[...] += mm(grad_pre, up, 1, 1)
    sum_[...] += mm(activated, down, 1, 0)

    @pl.when(step == pl.num_programs(0) - 1)
    def _():
        grad_normed_ref[...] = grad_sum[...].astype(low)
        branch_ref[...] = sum_[...].astype(low)


def feed_forward(tokens, mine, peer, w_mine, w_peer, vectors, cotangent, up, b_up, down):
    rows, features = tokens.shape
    units = up.shape[1]
    block = 512
    hidden_units = pl.BlockSpec((rows, block), lambda step: (0, step))
    return pl.pallas_call(
        feed_forward_kernel,
        name="feed_forward",
        grid=(units // block,),
        in_specs=[whole(a) for a in (tokens, mine, peer, w_mine, w_peer, vectors, cotangent)]
        + [
            pl.BlockSpec((features, block), lambda step: (0, step)),
            pl.BlockSpec((1, block), lambda step: (0, step)),
            pl.BlockSpec((block, features), lambda step: (step, 0)),
        ],
        out_specs=[whole(tokens), whole(tokens), hidden_units, hidden_units, whole(tokens), whole(tokens)]
        + [pl.BlockSpec((1, block), lambda step: (0, step))],
        out_shape=[
            shaped((rows, features), wide),
            shaped((rows, features), low),
            shaped((rows, units), low),
            shaped((rows, units), low),
            shaped((rows, features), low),
            shaped((rows, features), low),
            shaped((1, units), wide),
        ],
        scratch_shapes=[pltpu.VMEM((rows, features), wide), pltpu.VMEM((rows, features), wide)],
        compiler_params=params,
        cost_estimate=cost(5 * 10**9, 10**7, 10**6),
    )(tokens, mine, peer, w_mine, w_peer, vectors, cotangent, up, b_up, down)


def middle_kernel(
    part_ref, came_ref, hidden_ref, cotangent_ref, vectors_ref, w_mine_ref, w_peer_ref,
    grad_hidden_ref, branch_ref, mine_ref, peer_ref, sums_ref
):
    grad = part_ref[...].astype(wide) + came_ref[...].astype(wide)
    cotangent = cotangent_ref[...].astype(wide)
    by_hidden, by_gain, by_shift = normalize_back(hidden_ref[...], vectors_ref[3:4], grad)
    grad_hidden = by_hidden + cotangent
    grad_hidden_ref[...] = grad_hidden
    branch = grad_hidden.astype(low)
    branch_ref[...] = branch
    mine_ref[...] = mm(w_mine_ref[...], branch, 1, 1).astype(low)
    peer_ref[...] = mm(w_peer_ref[...], branch, 1, 1).astype(low)
    sums_ref[...] = jnp.zeros_like(sums_ref)
    sums_ref[0:1] = jnp.sum(branch.astype(wide), axis=0, keepdims=True)
    sums_ref[1:2] = by_gain[None]
    sums_ref[2:3] = by_shift[None]
    sums_ref[3:4] = jnp.sum(cotangent, axis=0, keepdims=True)


def middle(part, came, hidden, cotangent, vectors, w_mine, w_peer):
    rows, features = part.shape
    width = w_mine.shape[0]
    args = (part, came, hidden, cotangent, vectors, w_mine, w_peer)
    return pl.pallas_call(
        middle_kernel,
        name="second_norm_backward",
        out_shape=[
            shaped((rows, features), wide),
            shaped((rows, features), low),
            shaped((width, rows), low),
            shaped((width, rows), low),
            shaped((8, features), wide),
        ],
        compiler_params=params,
        cost_estimate=cost(10**9, 5 * 10**6),
    )(*args)


def last_kernel(part_ref, came_ref, tokens_ref, grad_hidden_ref, vectors_ref, out_ref, sums_ref):
    grad = part_ref[...].astype(wide) + came_ref[...].astype(wide)
    by_tokens, by_gain, by_shift = normalize_back(tokens_ref[...].astype(wide), vectors_ref[0:1], grad)
    out_ref[...] = grad_hidden_ref[...] + by_tokens
    sums_ref[...] = jnp.zeros_like(sums_ref)
    sums_ref[0:1] = by_gain[None]
    sums_ref[1:2] = by_shift[None]


def last(part, came, tokens, grad_hidden, vectors):
    rows, features = part.shape
    return pl.pallas_call(
        last_kernel,
        name="first_norm_backward",
        out_shape=[shaped((rows, features), wide), shaped((8, features), wide)],
        compiler_params=params,
        cost_estimate=cost(10**8, 5 * 10**6),
    )(part, came, tokens, grad_hidden, vectors)


def by_inputs_kernel(grads_ref, w_ref, own_ref, other_ref, sums_ref):
    own = own_ref.shape[0]
    grads = grads_ref[...]
    other_ref[...] = mm(grads[:, own:], w_ref[...], 0, 0).astype(low)
    own_ref[...] = mm(grads[:, :own], w_ref[...], 0, 0).astype(low)
    sums_ref[...] = mm(jnp.ones((8, grads.shape[1]), low), grads, 1, 1)


def by_inputs(grads, w):
    rows, features = grads.shape[1] // 2, w.shape[1]
    return pl.pallas_call(
        by_inputs_kernel,
        name="first_normed_gradient",
        out_shape=[
            shaped((rows, features), low),
            shaped((rows, features), low),
            shaped((8, grads.shape[0]), wide),
        ],
        compiler_params=params,
        cost_estimate=cost(2 * 10**9, 5 * 10**6),
    )(grads, w)


def weight_gradient_kernel(core_ref, *refs, dims, pairs):
    away_ref, kept_ref = refs[2 * pairs :]
    step, blocks = pl.program_id(0), pl.num_programs(0) // 2
    total = mm(refs[0][...], refs[1][...], *dims)
    for j in range(1, pairs):
        total = total + mm(refs[2 * j][...], refs[2 * j + 1][...], *dims)

    @pl.when(step < blocks)
    def _():
        away_ref[...] = total.astype(low)

    @pl.when(step >= blocks)
    def _():
        kept_ref[...] = total


def weight_gradient(core, pairs, dims, block):
    left, right = pairs[0]
    rows, columns = left.shape[1 - dims[0]], right.shape[1 - dims[1]]
    half = rows // 2
    blocks = half // block

    def place(step, core_ref):
        side = jnp.where(step < blocks, 1 - core_ref[0], core_ref[0])
        at = side * blocks + lax.rem(step, blocks)
        return (0, at) if dims[0] == 0 else (at, 0)

    specs, flat = [], []
    for left, right in pairs:
        shape = (left.shape[0], block) if dims[0] == 0 else (block, left.shape[1])
        specs += [pl.BlockSpec(shape, place), whole(right)]
        flat += [left, right]
    return pl.pallas_call(
        functools.partial(weight_gradient_kernel, dims=dims, pairs=len(pairs)),
        name="weight_gradient",
        grid_spec=pltpu.PrefetchScalarGridSpec(
            num_scalar_prefetch=1,
            grid=(2 * blocks,),
            in_specs=specs,
            out_specs=[
                pl.BlockSpec((block, columns), lambda step, _: (jnp.minimum(step, blocks - 1), 0)),
                pl.BlockSpec((block, columns), lambda step, _: (jnp.maximum(step - blocks, 0), 0)),
            ],
        ),
        out_shape=[shaped((half, columns), low), shaped((half, columns), wide)],
        compiler_params=params,
        cost_estimate=cost(2 * 10**9, 10**7),
    )(core, *flat)


def after(value, *others):
    return lax.optimization_barrier((value, *others))[0]


def swap_mp(value):
    return lax.ppermute(value, "mp", [(0, 1), (1, 0)])


def swap_dp(value, mask, count):
    return lax.ppermute(value, "dp", [(i, i ^ mask) for i in range(count)])


def rows_at(value, at, rows):
    return lax.dynamic_slice_in_dim(value, at * rows, rows, 0)


def rows_set(value, block, at):
    return lax.dynamic_update_slice_in_dim(value, block, at * block.shape[0], 0)


def chip_sum(block, radices, stride, chip, count):
    if not radices:
        return block.astype(low)
    radix = radices[0]
    digit = (chip // stride) & (radix - 1)
    rows = block.shape[0] // radix
    total = rows_at(block, digit, rows)
    came = [
        swap_dp(rows_at(block, digit ^ j, rows).astype(low), 2 * stride * j, count) for j in range(1, radix)
    ]
    for piece in came:
        total = total + piece.astype(wide)
    mine = chip_sum(total, radices[1:], stride * radix, chip, count)
    gathered = rows_set(jnp.zeros(block.shape, low), mine, digit)
    for j in range(1, radix):
        gathered = rows_set(gathered, swap_dp(mine, 2 * stride * j, count), digit ^ j)
    return gathered


def device_sum(away, kept, radices, place, count):
    core, chip = place & 1, place >> 1
    half = kept + swap_dp(away, 1, count).astype(wide)
    half = chip_sum(half, radices, 1, chip, count)
    other = swap_dp(half, 1, count)
    first = jnp.where(core == 0, half, other)
    second = jnp.where(core == 0, other, half)
    return jnp.concatenate([first, second], axis=0).astype(wide)


def small_sum(block, count):
    mask = 1
    while mask < count:
        block = block + swap_dp(block, mask, count)
        mask *= 2
    return block


def local(
    count,
    tokens,
    tissue,
    first_gain,
    first_shift,
    w_query,
    b_query,
    w_key,
    w_value,
    b_value,
    w_output,
    b_output,
    second_gain,
    second_shift,
    w_upward,
    b_upward,
    w_down,
    b_down,
    cotangent,
):
    place, side = lax.axis_index("dp"), lax.axis_index("mp")
    core = place & 1
    core_list = core.reshape(1)
    own = tokens.shape[0]
    width = w_query.shape[1]
    bits = (count // 2).bit_length() - 1
    binary = (2,) * bits

    tokens_other = swap_mp(tokens)
    w_peer = swap_mp(after(w_output, tokens_other))
    cotangent_other = swap_mp(after(cotangent, tokens_other))
    valid = tissue[0] > 0
    valid = jnp.where(side == 0, valid, jnp.roll(valid, own))
    bias = jnp.where(valid, 0.0, masked_score).astype(low)
    bias = jnp.pad(bias[None], ((0, 15), (0, 0)))
    vectors = jnp.stack([first_gain, first_shift, b_output, second_gain, second_shift, b_down])
    vectors = jnp.pad(vectors, ((0, 2), (0, 0)))
    w_stack = jnp.concatenate([w_query, w_key, w_value], axis=1).T
    b_stack = jnp.concatenate([b_query, jnp.zeros_like(b_query), b_value])[:, None]

    qkv, own_context, other_context, exact, logs, turned = attention_forward(
        tokens, tokens_other, vectors, w_stack, b_stack, bias
    )
    peer_own = swap_mp(other_context)
    peer_other = swap_mp(own_context)
    b_up = b_upward[None]
    shared = (w_upward, b_up, w_down)
    _, normed_b, active_b, pre_b, part_b, branch_b, sum_b = feed_forward(
        tokens_other, other_context, peer_other, w_output, w_peer, vectors, cotangent_other, *shared
    )
    came = swap_mp(part_b)
    hidden, normed_a, active_a, pre_a, part_a, branch_a, sum_a = feed_forward(
        tokens, own_context, peer_own, w_output, w_peer, vectors, cotangent, *shared
    )
    pieces_down = weight_gradient(
        core_list, ((active_a, cotangent), (active_b, cotangent_other)), (0, 0), w_down.shape[0] // 2
    )
    grad_down = device_sum(*pieces_down, binary, place, count)
    pieces_up = weight_gradient(
        core_list, ((normed_a, pre_a), (normed_b, pre_b)), (0, 0), w_upward.shape[0] // 2
    )
    grad_upward = device_sum(*pieces_up, binary, place, count)

    grad_hidden, grad_branch, mine_own, peer_grad, sums = middle(
        part_a, came, hidden, cotangent, vectors, w_output, w_peer
    )
    mine_other = swap_mp(peer_grad)
    branch_other = swap_mp(after(grad_branch, mine_other))
    branch_came = swap_mp(after(branch_b, mine_other))
    output = (
        hidden + (branch_a.astype(wide) + branch_came.astype(wide) + b_down)
    ).astype(low)
    grads = attention_backward(qkv, exact, logs, bias, mine_own, mine_other)
    pieces_out = weight_gradient(
        core_list, ((own_context, grad_branch), (other_context, branch_other)), (1, 0), width // 2
    )
    grad_woutput = device_sum(*pieces_out, binary, place, count)
    pieces_stack = weight_gradient(core_list, ((turned, grads),), (1, 1), turned.shape[0] // 2)
    tail = (2, 4) + (2,) * (bits - 3) if bits >= 3 else binary
    grad_stack = device_sum(*pieces_stack, tail, place, count)
    part_a, part_b, stack_sums = by_inputs(grads, w_stack)
    came = swap_mp(part_b)
    grad_tokens, sums_first = last(part_a, came, tokens, grad_hidden, vectors)

    sums = jnp.concatenate([sums_first[:2], sums[:4]], axis=0)
    sums = sums + swap_mp(sums)
    columns = sums.shape[1]
    split = jnp.concatenate(
        [stack_sums[0, :width], stack_sums[0, 2 * width :], (sum_a + sum_b)[0]]
    ).reshape(-1, columns)
    small = small_sum(jnp.concatenate([sums, split], axis=0), count)
    split = small[6:].reshape(-1)
    return (
        output,
        grad_tokens,
        small[0],
        small[1],
        grad_stack[:, :width],
        split[:width],
        grad_stack[:, width : 2 * width],
        grad_stack[:, 2 * width :],
        split[width : 2 * width],
        grad_woutput,
        small[2],
        small[3],
        small[4],
        grad_upward,
        split[2 * width :],
        grad_down,
        small[5],
    )


def solution(mesh):
    in_specs = (
        P(("dp", "mp"), None),
        P("dp", None),
        P(),
        P(),
        P(None, "mp"),
        P("mp"),
        P(None, "mp"),
        P(None, "mp"),
        P("mp"),
        P("mp", None),
        P(),
        P(),
        P(),
        P(None, "mp"),
        P("mp"),
        P("mp", None),
        P(),
        P(("dp", "mp"), None),
    )
    out_specs = (
        P(("dp", "mp"), None),
        P(("dp", "mp"), None),
        P(),
        P(),
        P(None, "mp"),
        P("mp"),
        P(None, "mp"),
        P(None, "mp"),
        P("mp"),
        P("mp", None),
        P(),
        P(),
        P(),
        P(None, "mp"),
        P("mp"),
        P("mp", None),
        P(),
    )
    return jax.shard_map(
        functools.partial(local, mesh.shape["dp"]), mesh=mesh, in_specs=in_specs, out_specs=out_specs, check_vma=False)
```

time: 613 us -> 299 us (0.49)
  waiting for transfers between devices: 295 us -> 111 us
  blocking collectives: 103 us -> 0 us
  matrix products: 90.6 us -> 0 us
  Pallas kernels: 0 us -> 77.5 us
  starting transfers between devices: 8.92 us -> 57.7 us
  other arithmetic: 60.9 us -> 20.1 us
  between operations: 14.6 us -> 1.61 us
    psum x1 -> x0, waiting for transfers between devices: 161 us -> none  [local(): lax.psum((grad_wquery, grad_bquery, grad_wkey, grad_wvalue, grad_bvalue,...]
    ppermute x0 -> x49, waiting for transfers between devices: none -> 111 us  [the longest x38 78.6 us: swap_dp(): return lax.ppermute(value, 'dp', [(i, i ^ mask) for i in range(count)])]
    psum x2 -> x0, blocking collectives: 103 us -> none  [the longest x1 64 us: local(): lax.psum((grad_wquery, grad_bquery, grad_wkey, grad_wvalue, grad_bvalue,...]
    dot_general x18 -> x0, matrix products: 90.6 us -> none  [the longest x1 15.6 us: head_layer(): jnp.einsum('gd,fd->gf', grad_rows, w_down, preferred_element_type=jnp.flo...]
    pallas_call x0 -> x11, Pallas kernels: none -> 77.5 us  [the longest x2 17.9 us: feed_forward(): pl.pallas_call(feed_forward_kernel, name='feed_forward', grid=(units // b...]
    all_gather x4 -> x0, waiting for transfers between devices: 76.7 us -> none  [the longest x1 22.6 us: head_layer(): gathered2 = lax.all_gather(normed2, 'mp', axis=0, tiled=True)]
    ppermute x0 -> x49, starting transfers between devices: none -> 57.7 us  [the longest x38 44.2 us: swap_dp(): return lax.ppermute(value, 'dp', [(i, i ^ mask) for i in range(count)])]
    reduce_scatter x4 -> x0, waiting for transfers between devices: 56.9 us -> none  [the longest x1 22.3 us: head_layer(): lax.psum_scatter(jnp.dot(part_rows, w_down, preferred_element_type=jnp.fl...]
  transfers between devices with their start and end apart: 9 -> 49, of which waited for: 8 -> 22; matrix products, arithmetic and copies ran while one was open for 8% -> 11% of each run, Pallas kernels for 0% -> 26%
where the time goes in v1:
time: 299 us; the launch traced here: 296 us
  waiting for transfers between devices  111 us (37%)
  Pallas kernels  77.5 us (26%)
  starting transfers between devices  57.7 us (19%)
  local copies, waits for them, and re-layouts  28 us (9%)
  other arithmetic  20.1 us (7%)
    ppermute x38, waiting for transfers between devices, swap_dp(): return lax.ppermute(value, 'dp', [(i, i ^ mask) for i in range(count)])  78.6 us
    ppermute x38, starting transfers between devices, swap_dp(): return lax.ppermute(value, 'dp', [(i, i ^ mask) for i in range(count)])  44.2 us
    ppermute x11, waiting for transfers between devices, swap_mp(): return lax.ppermute(value, 'mp', [(0, 1), (1, 0)])  32.8 us
    pallas_call x2, Pallas kernels, feed_forward(): pl.pallas_call(feed_forward_kernel, name='feed_forward', grid=(units // b...  17.9 us
    pallas_call x1, Pallas kernels, attention_forward(): pl.pallas_call(attention_forward_kernel, name='attention_forward', grid=(...  17.4 us
    pallas_call x1, Pallas kernels, attention_backward(): pl.pallas_call(attention_backward_kernel, name='attention_backward', grid...  16.6 us
    unnamed x89, local copies, waits for them, and re-layouts  16.5 us
    pallas_call x4, Pallas kernels, weight_gradient(): pl.pallas_call(functools.partial(weight_gradient_kernel, dims=dims, pairs...  16.2 us
  transfers between devices with their start and end apart: 49, of which 22 were waited for; matrix products, arithmetic and copies ran while one was open for 11% of the time, Pallas kernels for 26%

profile of v1, /device:TPU:0, one launch (start us, length us, event | category | flops | bytes accessed | tf_op | source)
XLA Modules:
  0.0 296.3 jit_solution(18433285666603313243)
XLA Ops:
  19.7 17.4 %attention_forward.1 = (bf16[1152,784]{1,0:T(8,128)(2,1)}, bf16[384,392]{1,0:T(8,128)(2,1)S(1)}, bf16[384,392]{1,0:T(8,128)(2,1)S(1)}, f32[384,784]{1,0:T(8,128)...) custom-call(bf16[392,768]{1,0:T(8,128)(2,1)S(1)} %copy-done.4, ...), custom_call_target="tpu_custom_call" | custom-call | flops 10000000000 | bytes 10000000 | tf_op jit(solution)/shard_map/attention_forward/pallas_call | solution.py:117
  42.2 13.0 %collective-permute-done.3.peer_ref = bf16[384,392]{1,0:T(8,128)(2,1)S(1)} collective-permute-done((bf16[384,392]{1,0:T(8,128)(2,1)S(1)}, bf16[384,392]{1,0:T(8,128)(2,1)S(1)}, u32[]{:S(2)}, u32[]{:S(2)}) %collective-permute-start.3) | collective-permute-done | bytes 301088 | tf_op jit(solution)/shard_map/ppermute | solution.py:410
  58.2 9.4 %feed_forward.3 = (f32[392,768]{1,0:T(8,128)}, bf16[392,768]{1,0:T(8,128)(2,1)S(1)}, bf16[392,1536]{1,0:T(8,128)(2,1)}, bf16[392,1536]{1,0:T(8,128)(2,1)}, bf16[...) custom-call(bf16[392,768]{1,0:T(8,128)(2,1)} %collective-permute-done.other_ref.tokens_ref, ...), custom_call_target="tpu_custom_call" | custom-call | flops 5000000000 | bytes 10000000 | tf_op jit(solution)/shard_map/feed_forward/pallas_call | solution.py:246
  69.4 8.5 %feed_forward.2 = (f32[392,768]{1,0:T(8,128)S(1)}, bf16[392,768]{1,0:T(8,128)(2,1)S(1)}, bf16[392,1536]{1,0:T(8,128)(2,1)}, bf16[392,1536]{1,0:T(8,128)(2,1)}, b...) custom-call(bf16[392,768]{1,0:T(8,128)(2,1)S(1)} %copy-done.4, ...), custom_call_target="tpu_custom_call" | custom-call | flops 5000000000 | bytes 10000000 | tf_op jit(solution)/shard_map/feed_forward/pallas_call | solution.py:246
  81.1 5.1 %weight_gradient.6 = (bf16[384,1536]{1,0:T(8,128)(2,1)}, f32[384,1536]{1,0:T(8,128)}) custom-call(s32[1]{0:T(128)} %bitcast.1.core_ref, bf16[392,768]{1,0:T(8,128)(2,1)S(1)} %get-tuple-element.89.refs_0_, bf16[392,1536]{1,0:T(8,128)(2,1)S(1)} %copy-done.28, bf16[392,768]{1,0:T(8,128)(2,1)S(1)} %get-tuple-element.91.refs_2_, bf16[392,1536]{1,0:T(8,128)(2,1)S(1)} %copy-done.27), custom_call_target="tpu_custom_call" | custom-call | flops 2000000000 | bytes 10000000 | tf_op jit(solution)/shard_map/weight_gradient/pallas_call | solution.py:387
  89.9 6.3 %weight_gradient.7 = (bf16[768,768]{1,0:T(8,128)(2,1)}, f32[768,768]{1,0:T(8,128)}) custom-call(s32[1]{0:T(128)} %bitcast.1.core_ref, bf16[392,1536]{1,0:T(8,128)(2,1)S(1)} %copy-done.26, bf16[392,768]{1,0:T(8,128)(2,1)S(1)} %copy-done.3, bf16[392,1536]{1,0:T(8,128)(2,1)S(1)} %copy-done.25, bf16[392,768]{1,0:T(8,128)(2,1)} %collective-permute-done.4.cotangent_ref.refs_3_), custom_call_target="tpu_custom_call" | custom-call | flops 2000000000 | bytes 10000000 | tf_op jit(solution)/shard_map/weight_gradient/pallas_call | solution.py:387
  96.6 4.5 %collective-permute-done.6.other_grad_ref = bf16[384,392]{1,0:T(8,128)(2,1)S(1)} collective-permute-done((bf16[384,392]{1,0:T(8,128)(2,1)S(1)}, bf16[384,392]{1,0:T(8,128)(2,1)S(1)}, u32[]{:S(2)}, u32[]{:S(2)}) %collective-permute-start.6) | collective-permute-done | bytes 301088 | tf_op jit(solution)/shard_map/ppermute | solution.py:410
  101.4 16.6 %attention_backward.1.grads_ref.refs_1_ = bf16[1152,784]{1,0:T(8,128)(2,1)S(1)} custom-call(bf16[1152,784]{1,0:T(8,128)(2,1)} %get-tuple-element.69.qkv_ref, f32[384,784]{1,0:T(8,128)S(1)} %copy-done.30, f32[6,1,784]{2,1,0:T(1,128)S(1)} %get-tuple-element.71.log_ref, bf16[16,784]{1,0:T(8,128)(2,1)S(1)} %pad.9.bias_ref, ...), custom_call_target="tpu_custom_call" | custom-call | flops 10000000000 | bytes 10000000 | tf_op jit(solution)/shard_map/attention_backward/pallas_call | solution.py:183
  126.5 3.6 %weight_gradient.4 = (bf16[384,1152]{1,0:T(8,128)(2,1)}, f32[384,1152]{1,0:T(8,128)S(1)}) custom-call(s32[1]{0:T(128)} %bitcast.1.core_ref, bf16[768,784]{1,0:T(8,128)(2,1)S(1)} %copy-done.24, bf16[1152,784]{1,0:T(8,128)(2,1)S(1)} %copy-done.22), custom_call_target="tpu_custom_call" | custom-call | flops 2000000000 | bytes 10000000 | tf_op jit(solution)/shard_map/weight_gradient/pallas_call | solution.py:387
  132.2 6.5 %collective-permute-done.8.came_ref = bf16[392,768]{1,0:T(8,128)(2,1)} collective-permute-done((bf16[392,768]{1,0:T(8,128)(2,1)}, bf16[392,768]{1,0:T(8,128)(2,1)}, u32[]{:S(2)}, u32[]{:S(2)}) %collective-permute-start.8) | collective-permute-done | bytes 602144 | tf_op jit(solution)/shard_map/ppermute | solution.py:410
  138.7 3.3 %first_norm_backward.1 = (f32[392,768]{1,0:T(8,128)}, f32[8,768]{1,0:T(8,128)S(1)}) custom-call(bf16[392,768]{1,0:T(8,128)(2,1)S(1)} %copy-done.9, bf16[392,768]{1,0:T(8,128)(2,1)} %collective-permute-done.8.came_ref, bf16[392,768]{1,0:T(8,128)(2,1)S(1)} %copy-done.5, f32[392,768]{1,0:T(8,128)S(1)} %get-tuple-element.75.grad_hidden_ref, ...), custom_call_target="tpu_custom_call" | custom-call | flops 100000000 | bytes 5000000 | tf_op jit(solution)/shard_map/first_norm_backward/pallas_call | solution.py:323
  144.7 5.7 %collective-permute-done.9 = f32[6,768]{1,0:T(8,128)S(1)} collective-permute-done((f32[6,768]{1,0:T(8,128)S(1)}, f32[6,768]{1,0:T(8,128)S(1)}, u32[]{:S(2)}, u32[]{:S(2)}) %collective-permute-start.9) | collective-permute-done | bytes 18464 | tf_op jit(solution)/shard_map/ppermute | solution.py:410
  155.4 10.0 %collective-permute-done.11 = f32[9,768]{1,0:T(8,128)S(1)} collective-permute-done((f32[9,768]{1,0:T(8,128)S(1)}, f32[9,768]{1,0:T(8,128)S(1)}, u32[]{:S(2)}, u32[]{:S(2)}) %collective-permute-start.11) | collective-permute-done | bytes 27680 | tf_op jit(solution)/shard_map/ppermute | solution.py:414
  189.3 7.6 %collective-permute-done.27 = bf16[48,768]{1,0:T(8,128)(2,1)S(1)} collective-permute-done((bf16[48,768]{1,0:T(8,128)(2,1)S(1)}, bf16[48,768]{1,0:T(8,128)(2,1)S(1)}, u32[]{:S(2)}, u32[]{:S(2)}) %collective-permute-start.27) | collective-permute-done | bytes 73760 | tf_op jit(solution)/shard_map/ppermute | solution.py:414
  196.9 3.4 %collective-permute-start.28 = (bf16[24,768]{1,0:T(8,128)(2,1)S(1)}, bf16[24,768]{1,0:T(8,128)(2,1)S(1)}, u32[]{:S(2)}, u32[]{:S(2)}) collective-permute-start(bf16[24,768]{1,0:T(8,128)(2,1)S(1)} %dynamic-slice_convert_fusion.12), channel_id=1, source_target_pairs={{0,16},{2,18},{4,20},{6,22},{8,24},{10,26},{12,28},{14,30},{16,0},... | collective-permute-start | bytes 110600 | tf_op jit(solution)/shard_map/ppermute | solution.py:414
  208.6 3.9 %collective-permute-start.30 = (bf16[48,768]{1,0:T(8,128)(2,1)S(1)}, bf16[48,768]{1,0:T(8,128)(2,1)S(1)}, u32[]{:S(2)}, u32[]{:S(2)}) collective-permute-start(bf16[48,768]{1,0:T(8,128)(2,1)S(1)} %constant_dynamic-update-slice_fusion.16), channel_id=1, source_target_pairs={{0,8},{2,10},{4,12},{6,14},{8,0},{10,2},{12,4},{14,6},{16,24},{18,... | collective-permute-start | bytes 221192 | tf_op jit(solution)/shard_map/ppermute | solution.py:414
  222.7 3.8 %collective-permute-start.18 = (bf16[48,1152]{1,0:T(8,128)(2,1)S(1)}, bf16[48,1152]{1,0:T(8,128)(2,1)S(1)}, u32[]{:S(2)}, u32[]{:S(2)}) collective-permute-start(bf16[48,1152]{1,0:T(8,128)(2,1)S(1)} %get-tuple-element.125), channel_id=1, source_target_pairs={{0,24},{2,26},{4,28},{6,30},{8,16},{10,18},{12,20},{14,22},{16,8},... | collective-permute-start | bytes 331784 | tf_op jit(solution)/shard_map/ppermute | solution.py:414
  228.6 4.9 %collective-permute-done.18 = bf16[48,1152]{1,0:T(8,128)(2,1)S(1)} collective-permute-done((bf16[48,1152]{1,0:T(8,128)(2,1)S(1)}, bf16[48,1152]{1,0:T(8,128)(2,1)S(1)}, u32[]{:S(2)}, u32[]{:S(2)}) %collective-permute-start.18) | collective-permute-done | bytes 110624 | tf_op jit(solution)/shard_map/ppermute | solution.py:414
  233.5 9.1 %collective-permute-done.17 = bf16[48,1152]{1,0:T(8,128)(2,1)S(1)} collective-permute-done((bf16[48,1152]{1,0:T(8,128)(2,1)S(1)}, bf16[48,1152]{1,0:T(8,128)(2,1)S(1)}, u32[]{:S(2)}, u32[]{:S(2)}) %collective-permute-start.17) | collective-permute-done | bytes 110624 | tf_op jit(solution)/shard_map/ppermute | solution.py:414
  249.6 4.4 %collective-permute-done.20 = bf16[48,1152]{1,0:T(8,128)(2,1)S(1)} collective-permute-done((bf16[48,1152]{1,0:T(8,128)(2,1)S(1)}, bf16[48,1152]{1,0:T(8,128)(2,1)S(1)}, u32[]{:S(2)}, u32[]{:S(2)}) %collective-permute-start.20) | collective-permute-done | bytes 110624 | tf_op jit(solution)/shard_map/ppermute | solution.py:414
  254.9 4.5 %collective-permute-done.38 = bf16[96,1536]{1,0:T(8,128)(2,1)S(1)} collective-permute-done((bf16[96,1536]{1,0:T(8,128)(2,1)S(1)}, bf16[96,1536]{1,0:T(8,128)(2,1)S(1)}, u32[]{:S(2)}, u32[]{:S(2)}) %collective-permute-start.38) | collective-permute-done | bytes 294944 | tf_op jit(solution)/shard_map/ppermute | solution.py:414
  260.1 6.2 %collective-permute-done.22 = bf16[192,1152]{1,0:T(8,128)(2,1)S(1)} collective-permute-done((bf16[192,1152]{1,0:T(8,128)(2,1)S(1)}, bf16[192,1152]{1,0:T(8,128)(2,1)S(1)}, u32[]{:S(2)}, u32[]{:S(2)}) %collective-permute-start.22) | collective-permute-done | bytes 442400 | tf_op jit(solution)/shard_map/ppermute | solution.py:414
  269.4 9.5 %collective-permute-done.39 = bf16[192,1536]{1,0:T(8,128)(2,1)S(1)} collective-permute-done((bf16[192,1536]{1,0:T(8,128)(2,1)S(1)}, bf16[192,1536]{1,0:T(8,128)(2,1)S(1)}, u32[]{:S(2)}, u32[]{:S(2)}) %collective-permute-start.39) | collective-permute-done | bytes 589856 | tf_op jit(solution)/shard_map/ppermute | solution.py:414
  279.1 9.1 %collective-permute-done.47 = bf16[384,768]{1,0:T(8,128)(2,1)S(1)} collective-permute-done((bf16[384,768]{1,0:T(8,128)(2,1)S(1)}, bf16[384,768]{1,0:T(8,128)(2,1)S(1)}, u32[]{:S(2)}, u32[]{:S(2)}) %collective-permute-start.47) | collective-permute-done | bytes 589856 | tf_op jit(solution)/shard_map/ppermute | solution.py:414
  (277 shorter events, 118.4 us)
Async XLA Ops:
  0.7 16.9 %collective-permute-start = (bf16[392,768]{1,0:T(8,128)(2,1)}, bf16[392,768]{1,0:T(8,128)(2,1)}, u32[]{:S(2)}, u32[]{:S(2)}) collective-permute-start(bf16[392,768]{1,0:T(8,128)(2,1)} %tokens_ref.3), channel_id=1, source_target_pairs={{0,1},{1,0},{2,3},{3,2},{4,5},{5,4},{6,7},{7,6},{8,9},{9,8},{10,11... | collective-permute-start | bytes 1806344 | tf_op jit(solution)/shard_map/ppermute | solution.py:410
  17.6 38.3 %collective-permute-start.2 = (bf16[384,768]{1,0:T(8,128)(2,1)S(1)}, bf16[384,768]{1,0:T(8,128)(2,1)S(1)}, u32[]{:S(2)}, u32[]{:S(2)}) collective-permute-start(bf16[384,768]{1,0:T(8,128)(2,1)S(1)} %copy-done.10), channel_id=1, source_target_pairs={{0,1},{1,0},{2,3},{3,2},{4,5},{5,4},{6,7},{7,6},{8,9},{9,8},{10,11... | collective-permute-start | bytes 1769480 | tf_op jit(solution)/shard_map/ppermute | solution.py:410
  19.4 36.6 %collective-permute-start.4 = (bf16[392,768]{1,0:T(8,128)(2,1)S(1)}, bf16[392,768]{1,0:T(8,128)(2,1)}, u32[]{:S(2)}, u32[]{:S(2)}) collective-permute-start(bf16[392,768]{1,0:T(8,128)(2,1)S(1)} %copy-done.3), channel_id=1, source_target_pairs={{0,1},{1,0},{2,3},{3,2},{4,5},{5,4},{6,7},{7,6},{8,9},{9,8},{10,11... | collective-permute-start | bytes 1806344 | tf_op jit(solution)/shard_map/ppermute | solution.py:410
  41.8 27.6 %collective-permute-start.1 = (bf16[384,392]{1,0:T(8,128)(2,1)}, bf16[384,392]{1,0:T(8,128)(2,1)S(1)}, u32[]{:S(2)}, u32[]{:S(2)}) collective-permute-start(bf16[384,392]{1,0:T(8,128)(2,1)} %copy-done.16), channel_id=1, source_target_pairs={{0,1},{1,0},{2,3},{3,2},{4,5},{5,4},{6,7},{7,6},{8,9},{9,8},{10,11... | collective-permute-start | bytes 903176 | tf_op jit(solution)/shard_map/ppermute | solution.py:410
  67.6 18.6 %collective-permute-start.5 = (bf16[392,768]{1,0:T(8,128)(2,1)S(1)}, bf16[392,768]{1,0:T(8,128)(2,1)S(1)}, u32[]{:S(2)}, u32[]{:S(2)}) collective-permute-start(bf16[392,768]{1,0:T(8,128)(2,1)S(1)} %get-tuple-element.66), channel_id=1, source_target_pairs={{0,1},{1,0},{2,3},{3,2},{4,5},{5,4},{6,7},{7,6},{8,9},{9,8},{10,11... | collective-permute-start | bytes 1806344 | tf_op jit(solution)/shard_map/ppermute | solution.py:410
  86.2 43.9 %collective-permute-start.33 = (bf16[384,1536]{1,0:T(8,128)(2,1)}, bf16[384,1536]{1,0:T(8,128)(2,1)}, u32[]{:S(2)}, u32[]{:S(2)}) collective-permute-start(bf16[384,1536]{1,0:T(8,128)(2,1)} %get-tuple-element.94), channel_id=1, source_target_pairs={{0,2},{2,0},{4,6},{6,4},{8,10},{10,8},{12,14},{14,12},{16,18},{18,... | collective-permute-start | bytes 3538952 | tf_op jit(solution)/shard_map/ppermute | solution.py:414
  96.2 55.9 %collective-permute-start.41 = (bf16[768,768]{1,0:T(8,128)(2,1)}, bf16[768,768]{1,0:T(8,128)(2,1)}, u32[]{:S(2)}, u32[]{:S(2)}) collective-permute-start(bf16[768,768]{1,0:T(8,128)(2,1)} %get-tuple-element.98), channel_id=1, source_target_pairs={{0,2},{2,0},{4,6},{6,4},{8,10},{10,8},{12,14},{14,12},{16,18},{18,... | collective-permute-start | bytes 3538952 | tf_op jit(solution)/shard_map/ppermute | solution.py:414
  101.1 70.2 %collective-permute-start.7 = (bf16[392,768]{1,0:T(8,128)(2,1)}, bf16[392,768]{1,0:T(8,128)(2,1)}, u32[]{:S(2)}, u32[]{:S(2)}) collective-permute-start(bf16[392,768]{1,0:T(8,128)(2,1)} %get-tuple-element.68), channel_id=1, source_target_pairs={{0,1},{1,0},{2,3},{3,2},{4,5},{5,4},{6,7},{7,6},{8,9},{9,8},{10,11... | collective-permute-start | bytes 1806344 | tf_op jit(solution)/shard_map/ppermute | solution.py:410
  121.8 16.8 %collective-permute-start.8 = (bf16[392,768]{1,0:T(8,128)(2,1)}, bf16[392,768]{1,0:T(8,128)(2,1)}, u32[]{:S(2)}, u32[]{:S(2)}) collective-permute-start(bf16[392,768]{1,0:T(8,128)(2,1)} %get-tuple-element.74), channel_id=1, source_target_pairs={{0,1},{1,0},{2,3},{3,2},{4,5},{5,4},{6,7},{7,6},{8,9},{9,8},{10,11... | collective-permute-start | bytes 1806344 | tf_op jit(solution)/shard_map/ppermute | solution.py:410
  130.1 57.8 %collective-permute-start.14 = (bf16[384,1152]{1,0:T(8,128)(2,1)}, bf16[384,1152]{1,0:T(8,128)(2,1)}, u32[]{:S(2)}, u32[]{:S(2)}) collective-permute-start(bf16[384,1152]{1,0:T(8,128)(2,1)} %get-tuple-element.84), channel_id=1, source_target_pairs={{0,2},{2,0},{4,6},{6,4},{8,10},{10,8},{12,14},{14,12},{16,18},{18,... | collective-permute-start | bytes 2654216 | tf_op jit(solution)/shard_map/ppermute | solution.py:414
  130.1 37.0 %collective-permute-start.24 = (bf16[392,768]{1,0:T(8,128)(2,1)S(1)}, bf16[392,768]{1,0:T(8,128)(2,1)S(1)}, u32[]{:S(2)}, u32[]{:S(2)}) collective-permute-start(bf16[392,768]{1,0:T(8,128)(2,1)S(1)} %copy-done.15), channel_id=1, source_target_pairs={{0,1},{1,0},{2,3},{3,2},{4,5},{5,4},{6,7},{7,6},{8,9},{9,8},{10,11... | collective-permute-start | bytes 1806344 | tf_op jit(solution)/shard_map/ppermute | solution.py:410
  150.4 27.9 %collective-permute-start.34 = (bf16[192,1536]{1,0:T(8,128)(2,1)}, bf16[192,1536]{1,0:T(8,128)(2,1)}, u32[]{:S(2)}, u32[]{:S(2)}) collective-permute-start(bf16[192,1536]{1,0:T(8,128)(2,1)} %dynamic-slice_convert_fusion.1), channel_id=1, source_target_pairs={{0,4},{2,6},{4,0},{6,2},{8,12},{10,14},{12,8},{14,10},{16,20},{18,... | collective-permute-start | bytes 1769480 | tf_op jit(solution)/shard_map/ppermute | solution.py:414
  165.4 17.1 %collective-permute-start.42 = (bf16[384,768]{1,0:T(8,128)(2,1)}, bf16[384,768]{1,0:T(8,128)(2,1)}, u32[]{:S(2)}, u32[]{:S(2)}) collective-permute-start(bf16[384,768]{1,0:T(8,128)(2,1)} %dynamic-slice_convert_fusion), channel_id=1, source_target_pairs={{0,4},{2,6},{4,0},{6,2},{8,12},{10,14},{12,8},{14,10},{16,20},{18,... | collective-permute-start | bytes 1769480 | tf_op jit(solution)/shard_map/ppermute | solution.py:414
  180.0 25.4 %collective-permute-start.35 = (bf16[96,1536]{1,0:T(8,128)(2,1)S(1)}, bf16[96,1536]{1,0:T(8,128)(2,1)S(1)}, u32[]{:S(2)}, u32[]{:S(2)}) collective-permute-start(bf16[96,1536]{1,0:T(8,128)(2,1)S(1)} %dynamic-slice_convert_fusion.4), channel_id=1, source_target_pairs={{0,8},{2,10},{4,12},{6,14},{8,0},{10,2},{12,4},{14,6},{16,24},{18,... | collective-permute-start | bytes 884744 | tf_op jit(solution)/shard_map/ppermute | solution.py:414
  183.7 21.9 %collective-permute-start.43 = (bf16[192,768]{1,0:T(8,128)(2,1)S(1)}, bf16[192,768]{1,0:T(8,128)(2,1)S(1)}, u32[]{:S(2)}, u32[]{:S(2)}) collective-permute-start(bf16[192,768]{1,0:T(8,128)(2,1)S(1)} %dynamic-slice_convert_fusion.3), channel_id=1, source_target_pairs={{0,8},{2,10},{4,12},{6,14},{8,0},{10,2},{12,4},{14,6},{16,24},{18,... | collective-permute-start | bytes 884744 | tf_op jit(solution)/shard_map/ppermute | solution.py:414
  200.4 22.2 %collective-permute-start.15 = (bf16[192,1152]{1,0:T(8,128)(2,1)S(1)}, bf16[192,1152]{1,0:T(8,128)(2,1)S(1)}, u32[]{:S(2)}, u32[]{:S(2)}) collective-permute-start(bf16[192,1152]{1,0:T(8,128)(2,1)S(1)} %dynamic-slice_convert_fusion.2), channel_id=1, source_target_pairs={{0,4},{2,6},{4,0},{6,2},{8,12},{10,14},{12,8},{14,10},{16,20},{18,... | collective-permute-start | bytes 1327112 | tf_op jit(solution)/shard_map/ppermute | solution.py:414
  205.7 16.7 %collective-permute-start.44 = (bf16[96,768]{1,0:T(8,128)(2,1)S(1)}, bf16[96,768]{1,0:T(8,128)(2,1)S(1)}, u32[]{:S(2)}, u32[]{:S(2)}) collective-permute-start(bf16[96,768]{1,0:T(8,128)(2,1)S(1)} %dynamic-slice_convert_fusion.5), channel_id=1, source_target_pairs={{0,16},{2,18},{4,20},{6,22},{8,24},{10,26},{12,28},{14,30},{16,0},... | collective-permute-start | bytes 442376 | tf_op jit(solution)/shard_map/ppermute | solution.py:414
  218.3 27.0 %collective-permute-start.37 = (bf16[48,1536]{1,0:T(8,128)(2,1)S(1)}, bf16[48,1536]{1,0:T(8,128)(2,1)S(1)}, u32[]{:S(2)}, u32[]{:S(2)}) collective-permute-start(bf16[48,1536]{1,0:T(8,128)(2,1)S(1)} %get-tuple-element.110), channel_id=1, source_target_pairs={{0,16},{2,18},{4,20},{6,22},{8,24},{10,26},{12,28},{14,30},{16,0},... | collective-permute-start | bytes 442376 | tf_op jit(solution)/shard_map/ppermute | solution.py:414
  222.5 24.8 %collective-permute-start.45 = (bf16[96,768]{1,0:T(8,128)(2,1)S(1)}, bf16[96,768]{1,0:T(8,128)(2,1)S(1)}, u32[]{:S(2)}, u32[]{:S(2)}) collective-permute-start(bf16[96,768]{1,0:T(8,128)(2,1)S(1)} %get-tuple-element.108), channel_id=1, source_target_pairs={{0,16},{2,18},{4,20},{6,22},{8,24},{10,26},{12,28},{14,30},{16,0},... | collective-permute-start | bytes 442376 | tf_op jit(solution)/shard_map/ppermute | solution.py:414
  233.5 21.4 %collective-permute-start.32 = (bf16[192,768]{1,0:T(8,128)(2,1)S(1)}, bf16[192,768]{1,0:T(8,128)(2,1)S(1)}, u32[]{:S(2)}, u32[]{:S(2)}) collective-permute-start(bf16[192,768]{1,0:T(8,128)(2,1)S(1)} %constant_dynamic-update-slice_fusion.12), channel_id=1, source_target_pairs={{0,2},{2,0},{4,6},{6,4},{8,10},{10,8},{12,14},{14,12},{16,18},{18,... | collective-permute-start | bytes 884744 | tf_op jit(solution)/shard_map/ppermute | solution.py:414
  248.4 19.2 %collective-permute-start.46 = (bf16[192,768]{1,0:T(8,128)(2,1)S(1)}, bf16[192,768]{1,0:T(8,128)(2,1)S(1)}, u32[]{:S(2)}, u32[]{:S(2)}) collective-permute-start(bf16[192,768]{1,0:T(8,128)(2,1)S(1)} %constant_dynamic-update-slice_fusion.4), channel_id=1, source_target_pairs={{0,8},{2,10},{4,12},{6,14},{8,0},{10,2},{12,4},{14,6},{16,24},{18,... | collective-permute-start | bytes 884744 | tf_op jit(solution)/shard_map/ppermute | solution.py:414
  259.5 19.5 %collective-permute-start.39 = (bf16[192,1536]{1,0:T(8,128)(2,1)S(1)}, bf16[192,1536]{1,0:T(8,128)(2,1)S(1)}, u32[]{:S(2)}, u32[]{:S(2)}) collective-permute-start(bf16[192,1536]{1,0:T(8,128)(2,1)S(1)} %constant_dynamic-update-slice_fusion.8), channel_id=1, source_target_pairs={{0,4},{2,6},{4,0},{6,2},{8,12},{10,14},{12,8},{14,10},{16,20},{18,... | collective-permute-start | bytes 1769480 | tf_op jit(solution)/shard_map/ppermute | solution.py:414
  266.4 21.9 %collective-permute-start.23 = (bf16[384,1152]{1,0:T(8,128)(2,1)S(1)}, bf16[384,1152]{1,0:T(8,128)(2,1)S(1)}, u32[]{:S(2)}, u32[]{:S(2)}) collective-permute-start(bf16[384,1152]{1,0:T(8,128)(2,1)S(1)} %constant_dynamic-update-slice_fusion.18), channel_id=1, source_target_pairs={{0,2},{2,0},{4,6},{6,4},{8,10},{10,8},{12,14},{14,12},{16,18},{18,... | collective-permute-start | bytes 2654216 | tf_op jit(solution)/shard_map/ppermute | solution.py:414
  267.6 20.6 %collective-permute-start.47 = (bf16[384,768]{1,0:T(8,128)(2,1)S(1)}, bf16[384,768]{1,0:T(8,128)(2,1)S(1)}, u32[]{:S(2)}, u32[]{:S(2)}) collective-permute-start(bf16[384,768]{1,0:T(8,128)(2,1)S(1)} %constant_dynamic-update-slice_fusion.2), channel_id=1, source_target_pairs={{0,4},{2,6},{4,0},{6,2},{8,12},{10,14},{12,8},{14,10},{16,20},{18,... | collective-permute-start | bytes 1769480 | tf_op jit(solution)/shard_map/ppermute | solution.py:414
  (68 other events, 505.8 us)

commit v2 on v1

v2 whole, which is shorter than its diff:
```python
import functools

import jax
import jax.numpy as jnp
from jax import lax
from jax.experimental import pallas as pl
from jax.experimental.pallas import tpu as pltpu
from jax.sharding import PartitionSpec as P

HEAD = 64
LANES = 256
TAIL_RADICES = (2,)
epsilon = 1e-06
masked_score = -1e30
low, wide = jnp.bfloat16, jnp.float32
params = pltpu.CompilerParams(vmem_limit_bytes=24 << 20)


def cost(flops, moved, exps=0):
    return pl.CostEstimate(flops=flops, bytes_accessed=moved, transcendentals=exps)


def whole(array):
    return pl.BlockSpec(array.shape, lambda *_: (0,) * len(array.shape))


def shaped(shape, kind):
    return jax.ShapeDtypeStruct(shape, kind)


def mm(left, right, left_dim, right_dim):
    return lax.dot_general(
        left, right, (((left_dim,), (right_dim,)), ((), ())), preferred_element_type=wide
    )


def normalize(values, gain, shift):
    centred = values - jnp.mean(values, axis=-1, keepdims=True)
    spread = jnp.mean(centred * centred, axis=-1, keepdims=True)
    return centred * lax.rsqrt(spread + epsilon) * gain + shift


def normalize_back(values, gain, grad):
    centred = values - jnp.mean(values, axis=-1, keepdims=True)
    inverse = lax.rsqrt(jnp.mean(centred * centred, axis=-1, keepdims=True) + epsilon)
    unit = centred * inverse
    scaled = grad * gain
    by_values = inverse * (
        scaled
        - jnp.mean(scaled, axis=-1, keepdims=True)
        - unit * jnp.mean(scaled * unit, axis=-1, keepdims=True)
    )
    return by_values, jnp.sum(grad * unit, axis=0), jnp.sum(grad, axis=0)


def spans(extent):
    edges = list(range(0, extent, LANES))
    if len(edges) > 1 and extent - edges[-1] < LANES // 2:
        edges.pop()
    return list(zip(edges, edges[1:] + [extent]))


def split_three(row):
    first = row.astype(low).astype(wide)
    second = (row - first).astype(low).astype(wide)
    return first, second, row - first - second


def head_rows(part, width, head):
    return pl.ds(pl.multiple_of(part * width + head * HEAD, HEAD), HEAD)


def project_kernel(
    side_ref, tokens_ref, gain_ref, shift_ref, query_ref, key_ref, value_ref, b_ref, tissue_ref,
    qkv_ref, normed_ref, w_ref, bias_ref
):
    normed = normalize(tokens_ref[...].astype(wide), gain_ref[...][None], shift_ref[...][None]).astype(low)
    normed_ref[...] = normed
    width = query_ref.shape[1]
    for part, ref in enumerate((query_ref, key_ref, value_ref)):
        at = slice(part * width, (part + 1) * width)
        turned = ref[...].T
        w_ref[at] = turned
        qkv_ref[at] = (mm(turned, normed, 1, 1) + b_ref[at]).astype(low)
    own = tokens_ref.shape[0]
    bias = jnp.where(tissue_ref[...] > 0, 0.0, masked_score)
    turned = jnp.concatenate([bias[:, own:], bias[:, :own]], axis=1)
    bias = jnp.where(side_ref[0] == 0, bias, turned)
    index = lax.broadcasted_iota(jnp.int32, bias_ref.shape, 0)
    bias_ref[...] = jnp.where(index == 0, bias, 0.0).astype(low)


def project(side, tokens, gain, shift, w_query, w_key, w_value, b, tissue):
    rows, features = tokens.shape
    width = w_query.shape[1]
    vmem = pl.BlockSpec(memory_space=pltpu.VMEM)
    return pl.pallas_call(
        project_kernel,
        name="project_own_rows",
        in_specs=[pl.BlockSpec(memory_space=pltpu.SMEM)] + [vmem] * 8,
        out_specs=[vmem] * 4,
        out_shape=[
            shaped((3 * width, rows), low),
            shaped((rows, features), low),
            shaped((3 * width, features), low),
            shaped((16, tissue.shape[1]), low),
        ],
        compiler_params=params,
        cost_estimate=cost(10**9, 5 * 10**6),
    )(side, tokens, gain, shift, w_query, w_key, w_value, b, tissue)


def attention_forward_kernel(
    own_ref, own_normed_ref, other_ref, gain_ref, shift_ref, w_ref, b_ref, bias_ref,
    qkv_ref, own_context_ref, other_context_ref, exact_ref, log_ref, normed_ref
):
    head = pl.program_id(0)
    own = other_ref.shape[0]
    rows = 2 * own
    width = w_ref.shape[0] // 3

    @pl.when(head == 0)
    def _():
        normed = normalize(other_ref[...].astype(wide), gain_ref[...][None], shift_ref[...][None]).astype(low)
        normed_ref[:own] = own_normed_ref[...]
        normed_ref[own:] = normed
        for part in range(3):
            at = slice(part * width, (part + 1) * width)
            qkv_ref[at, :own] = own_ref[at]
            qkv_ref[at, own:] = (mm(w_ref[at], normed, 1, 1) + b_ref[at]).astype(low)

    queries = qkv_ref[head_rows(0, width, head)] * jnp.array(HEAD**-0.5, low)
    keys = jnp.concatenate([qkv_ref[head_rows(1, width, head)], bias_ref[...]], axis=0).T
    values = qkv_ref[head_rows(2, width, head)]
    index = lax.broadcasted_iota(jnp.int32, (16, rows), 0)
    queries = jnp.concatenate([queries, jnp.where(index == 0, 1.0, 0.0).astype(low)], axis=0)
    pieces = []
    for start, stop in spans(rows):
        scores = mm(keys, queries[:, start:stop], 1, 0)
        highest = jnp.max(scores, axis=0, keepdims=True)
        powers = jnp.exp(scores - highest)
        total = jnp.sum(powers, axis=0, keepdims=True)
        log_ref[0, :, start:stop] = highest + jnp.log(total)
        pieces.append(mm(values, powers.astype(low), 1, 0) * (1.0 / total))
    context = jnp.concatenate(pieces, axis=1)
    exact_ref[...] = context
    context = context.astype(low)
    own_context_ref[...] = context[:, :own]
    other_context_ref[...] = context[:, own:]


def attention_forward(own, own_normed, other, gain, shift, w, b, bias):
    count, features = other.shape
    width = w.shape[0] // 3
    rows = 2 * count
    by_head = lambda columns: pl.BlockSpec((HEAD, columns), lambda head: (head, 0))
    args = (own, own_normed, other, gain, shift, w, b, bias)
    return pl.pallas_call(
        attention_forward_kernel,
        name="attention_forward",
        grid=(width // HEAD,),
        in_specs=[whole(a) for a in args],
        out_specs=[
            pl.BlockSpec((3 * width, rows), lambda head: (0, 0)),
            by_head(count),
            by_head(count),
            by_head(rows),
            pl.BlockSpec((1, 1, rows), lambda head: (head, 0, 0)),
            pl.BlockSpec((rows, features), lambda head: (0, 0)),
        ],
        out_shape=[
            shaped((3 * width, rows), low),
            shaped((width, count), low),
            shaped((width, count), low),
            shaped((width, rows), wide),
            shaped((width // HEAD, 1, rows), wide),
            shaped((rows, features), low),
        ],
        compiler_params=params,
        cost_estimate=cost(10 * 10**9, 10**7, 4 * 10**6),
    )(*args)


def attention_backward_kernel(qkv_ref, exact_ref, log_ref, bias_ref, own_grad_ref, other_grad_ref, out_ref):
    head = pl.program_id(0)
    rows = qkv_ref.shape[1]
    width = qkv_ref.shape[0] // 3
    scale = HEAD**-0.5
    queries = qkv_ref[head_rows(0, width, head)] * jnp.array(scale, low)
    keys = qkv_ref[head_rows(1, width, head)]
    values = qkv_ref[head_rows(2, width, head)]
    grads = jnp.concatenate([own_grad_ref[...], other_grad_ref[...]], axis=1)
    overlap = jnp.sum(grads.astype(wide) * exact_ref[...], axis=0, keepdims=True)
    index = lax.broadcasted_iota(jnp.int32, (16, rows), 0)

    def stack(top, *extra):
        block = jnp.zeros((16, rows), wide)
        for place, row in enumerate(extra):
            block = jnp.where(index == place, row, block)
        return jnp.concatenate([top, block.astype(low)], axis=0)

    bias = bias_ref[0:1].astype(wide)
    queries_more = stack(queries, 1.0, *split_three(-log_ref[0]))
    keys_more = stack(keys, bias, 1.0, 1.0, 1.0).T
    grads_more = stack(grads, *split_three(-overlap))
    values_more = stack(values, 1.0, 1.0, 1.0).T
    grad_keys = jnp.zeros((HEAD, rows), wide)
    grad_values = jnp.zeros((HEAD, rows), wide)
    for start, stop in spans(rows):
        at = slice(start, stop)
        chances = jnp.exp(mm(keys_more, queries_more[:, at], 1, 0))
        grad_values = grad_values + mm(grads[:, at], chances.astype(low), 1, 1)
        grad_scores = (chances * mm(values_more, grads_more[:, at], 1, 0)).astype(low)
        out_ref[head_rows(0, width, head), at] = (mm(keys, grad_scores, 1, 0) * scale).astype(low)
        grad_keys = grad_keys + mm(queries[:, at], grad_scores, 1, 1)
    out_ref[head_rows(1, width, head)] = grad_keys.astype(low)
    out_ref[head_rows(2, width, head)] = grad_values.astype(low)


def attention_backward(qkv, exact, logs, bias, own_grad, other_grad):
    rows = qkv.shape[1]
    width = qkv.shape[0] // 3
    by_head = lambda columns: pl.BlockSpec((HEAD, columns), lambda head: (head, 0))
    return pl.pallas_call(
        attention_backward_kernel,
        name="attention_backward",
        grid=(width // HEAD,),
        in_specs=[
            whole(qkv),
            by_head(rows),
            pl.BlockSpec((1, 1, rows), lambda head: (head, 0, 0)),
            whole(bias),
            by_head(rows // 2),
            by_head(rows // 2),
        ],
        out_specs=whole(qkv),
        out_shape=shaped(qkv.shape, low),
        compiler_params=params,
        cost_estimate=cost(10 * 10**9, 10**7, 4 * 10**6),
    )(qkv, exact, logs, bias, own_grad, other_grad)


def gelu_both(values):
    below = 0.5 * (1.0 + lax.erf(values * (0.5**0.5)))
    density = jnp.exp(values * values * -0.5) * (2.0 * jnp.pi) ** -0.5
    return values * below, below + values * density


def feed_forward_kernel(
    tokens_ref, mine_ref, peer_ref, w_mine_ref, w_peer_ref, b_ref, gain_ref, shift_ref, cotangent_ref,
    up_ref, b_up_ref, down_ref, *refs, other
):
    if other:
        more, refs = refs[:5], refs[5:]
        hidden_ref, grad_normed_ref, branch_ref, grad_b_ref, grad_up_ref, grad_down_ref, *scratch = refs
        normed_ref, grad_sum, sum_, turned_ref, other_turned_ref = scratch
    else:
        normed_ref, activated_ref, grad_pre_ref, grad_normed_ref, branch_ref, grad_b_ref, grad_sum, sum_ = refs
    step = pl.program_id(0)

    @pl.when(step == 0)
    def _():
        attention = mm(mine_ref[...], w_mine_ref[...], 0, 0) + mm(peer_ref[...], w_peer_ref[...], 0, 0)
        hidden = tokens_ref[...].astype(wide) + (attention + b_ref[...][None])
        normed = normalize(hidden, gain_ref[...][None], shift_ref[...][None]).astype(low)
        normed_ref[...] = normed
        grad_sum[...] = jnp.zeros_like(grad_sum)
        sum_[...] = jnp.zeros_like(sum_)
        if other:
            hidden_ref[...] = hidden
            turned_ref[...] = normed.T
            other_turned_ref[...] = more[0][...].T

    up, down = up_ref[...], down_ref[...]
    pre_gelu = mm(normed_ref[...], up, 1, 0) + b_up_ref[...]
    grad_active = mm(cotangent_ref[...], down, 1, 1)
    activated, slope = gelu_both(pre_gelu)
    activated = activated.astype(low)
    grad_pre = (grad_active * slope).astype(low)
    sums = jnp.sum(grad_pre.astype(wide), axis=0, keepdims=True)
    grad_sum[...] += mm(grad_pre, up, 1, 1)
    sum_[...] += mm(activated, down, 1, 0)
    if other:
        _, other_cotangent_ref, other_activated_ref, other_grad_pre_ref, other_grad_b_ref = more
        grad_b_ref[...] = sums + other_grad_b_ref[...]
        grad_down = mm(activated, cotangent_ref[...], 0, 0)
        grad_down_ref[...] = (grad_down + mm(other_activated_ref[...], other_cotangent_ref[...], 0, 0)).astype(low)
        grad_up = mm(turned_ref[...], grad_pre, 1, 0)
        grad_up_ref[...] = (grad_up + mm(other_turned_ref[...], other_grad_pre_ref[...], 1, 0)).astype(low)
    else:
        grad_b_ref[...] = sums
        activated_ref[...] = activated
        grad_pre_ref[...] = grad_pre

    @pl.when(step == pl.num_programs(0) - 1)
    def _():
        grad_normed_ref[...] = grad_sum[...].astype(low)
        branch_ref[...] = sum_[...].astype(low)


def feed_forward(tokens, mine, peer, w_mine, w_peer, b, gain, shift, cotangent, up, b_up, down, other=()):
    rows, features = tokens.shape
    units = up.shape[1]
    block = 512
    by_rows = pl.BlockSpec((rows, block), lambda step: (0, step))
    by_unit = pl.BlockSpec((1, block), lambda step: (0, step))
    by_up = pl.BlockSpec((features, block), lambda step: (0, step))
    by_down = pl.BlockSpec((block, features), lambda step: (step, 0))
    plain = shaped((rows, features), low)
    scratch = [pltpu.VMEM((rows, features), wide), pltpu.VMEM((rows, features), wide)]
    if other:
        out_specs = [whole(tokens)] * 3 + [by_unit, by_up, by_down]
        out_shape = [shaped((rows, features), wide), plain, plain, shaped((1, units), wide)]
        out_shape += [shaped((features, units), low), shaped((units, features), low)]
        turned = pltpu.VMEM((features, rows), low)
        scratch = [pltpu.VMEM((rows, features), low)] + scratch + [turned, turned]
    else:
        out_specs = [whole(tokens), by_rows, by_rows, whole(tokens), whole(tokens), by_unit]
        out_shape = [plain, shaped((rows, units), low), shaped((rows, units), low), plain, plain]
        out_shape += [shaped((1, units), wide)]
    return pl.pallas_call(
        functools.partial(feed_forward_kernel, other=bool(other)),
        name="feed_forward",
        grid=(units // block,),
        in_specs=[whole(a) for a in (tokens, mine, peer, w_mine, w_peer, b, gain, shift, cotangent)]
        + [by_up, by_unit, by_down]
        + ([whole(other[0]), whole(other[1]), by_rows, by_rows, by_unit] if other else []),
        out_specs=out_specs,
        out_shape=out_shape,
        scratch_shapes=scratch,
        compiler_params=params,
        cost_estimate=cost(5 * 10**9, 10**7, 10**6),
    )(tokens, mine, peer, w_mine, w_peer, b, gain, shift, cotangent, up, b_up, down, *other)


def middle_kernel(
    part_ref, came_ref, hidden_ref, cotangent_ref, gain_ref, w_mine_ref, w_peer_ref,
    grad_hidden_ref, branch_ref, mine_ref, peer_ref, sums_ref
):
    grad = part_ref[...].astype(wide) + came_ref[...].astype(wide)
    cotangent = cotangent_ref[...].astype(wide)
    by_hidden, by_gain, by_shift = normalize_back(hidden_ref[...], gain_ref[...][None], grad)
    grad_hidden = by_hidden + cotangent
    grad_hidden_ref[...] = grad_hidden
    branch = grad_hidden.astype(low)
    branch_ref[...] = branch
    mine_ref[...] = mm(w_mine_ref[...], branch, 1, 1).astype(low)
    peer_ref[...] = mm(w_peer_ref[...], branch, 1, 1).astype(low)
    sums_ref[...] = jnp.zeros_like(sums_ref)
    sums_ref[0:1] = jnp.sum(branch.astype(wide), axis=0, keepdims=True)
    sums_ref[1:2] = by_gain[None]
    sums_ref[2:3] = by_shift[None]
    sums_ref[3:4] = jnp.sum(cotangent, axis=0, keepdims=True)


def middle(part, came, hidden, cotangent, gain, w_mine, w_peer):
    rows, features = part.shape
    width = w_mine.shape[0]
    args = (part, came, hidden, cotangent, gain, w_mine, w_peer)
    return pl.pallas_call(
        middle_kernel,
        name="second_norm_backward",
        out_shape=[
            shaped((rows, features), wide),
            shaped((rows, features), low),
            shaped((width, rows), low),
            shaped((width, rows), low),
            shaped((8, features), wide),
        ],
        compiler_params=params,
        cost_estimate=cost(10**9, 5 * 10**6),
    )(*args)


def last_kernel(
    part_ref, came_ref, tokens_ref, grad_hidden_ref, gain_ref, b_ref, hidden_ref, branch_ref, branch_came_ref,
    out_ref, sums_ref, output_ref
):
    grad = part_ref[...].astype(wide) + came_ref[...].astype(wide)
    by_tokens, by_gain, by_shift = normalize_back(tokens_ref[...].astype(wide), gain_ref[...][None], grad)
    out_ref[...] = grad_hidden_ref[...] + by_tokens
    sums_ref[...] = jnp.zeros_like(sums_ref)
    sums_ref[0:1] = by_gain[None]
    sums_ref[1:2] = by_shift[None]
    branch = branch_ref[...].astype(wide) + branch_came_ref[...].astype(wide)
    output_ref[...] = (hidden_ref[...] + (branch + b_ref[...][None])).astype(low)


def last(part, came, tokens, grad_hidden, gain, b, hidden, branch, branch_came):
    rows, features = part.shape
    return pl.pallas_call(
        last_kernel,
        name="first_norm_backward",
        out_shape=[shaped((rows, features), wide), shaped((8, features), wide), shaped((rows, features), low)],
        compiler_params=params,
        cost_estimate=cost(10**8, 5 * 10**6),
    )(part, came, tokens, grad_hidden, gain, b, hidden, branch, branch_came)


def by_inputs_kernel(grads_ref, w_ref, own_ref, other_ref, sums_ref):
    own = own_ref.shape[0]
    grads = grads_ref[...]
    other_ref[...] = mm(grads[:, own:], w_ref[...], 0, 0).astype(low)
    own_ref[...] = mm(grads[:, :own], w_ref[...], 0, 0).astype(low)
    sums_ref[...] = mm(jnp.ones((8, grads.shape[1]), low), grads, 1, 1)


def by_inputs(grads, w):
    rows, features = grads.shape[1] // 2, w.shape[1]
    return pl.pallas_call(
        by_inputs_kernel,
        name="first_normed_gradient",
        out_shape=[
            shaped((rows, features), low),
            shaped((rows, features), low),
            shaped((8, grads.shape[0]), wide),
        ],
        compiler_params=params,
        cost_estimate=cost(2 * 10**9, 5 * 10**6),
    )(grads, w)


def tail_gradient_kernel(
    core_ref, grads_ref, normed_ref, own_context_ref, own_branch_ref, other_context_ref, other_branch_ref,
    away_ref, kept_ref
):
    step = pl.program_id(0)
    block = tail_block(step, core_ref[0])

    def put(total):
        @pl.when(step < 2)
        def _():
            away_ref[...] = total.astype(low)

        @pl.when(step >= 2)
        def _():
            kept_ref[...] = total

    @pl.when(block < 3)
    def _():
        put(mm(grads_ref[...], normed_ref[...], 1, 0))

    @pl.when(block == 3)
    def _():
        put(
            mm(own_context_ref[...], own_branch_ref[...], 1, 0)
            + mm(other_context_ref[...], other_branch_ref[...], 1, 0)
        )


def tail_block(step, core):
    side = jnp.where(step < 2, 1 - core, core)
    return side * 2 + (step & 1)


def tail_gradient(core, grads, normed, own_context, own_branch, other_context, other_branch):
    width, features = own_context.shape[0], normed.shape[1]
    rest = (normed, own_context, own_branch, other_context, other_branch)
    return pl.pallas_call(
        tail_gradient_kernel,
        name="tail_gradient",
        grid_spec=pltpu.PrefetchScalarGridSpec(
            num_scalar_prefetch=1,
            grid=(4,),
            in_specs=[
                pl.BlockSpec(
                    (width, grads.shape[1]),
                    lambda step, core_ref: (jnp.minimum(tail_block(step, core_ref[0]), 2), 0),
                )
            ]
            + [whole(a) for a in rest],
            out_specs=[
                pl.BlockSpec((width, features), lambda step, _: (jnp.minimum(step, 1), 0)),
                pl.BlockSpec((width, features), lambda step, _: (jnp.maximum(step - 2, 0), 0)),
            ],
        ),
        out_shape=[shaped((2 * width, features), low), shaped((2 * width, features), wide)],
        compiler_params=params,
        cost_estimate=cost(2 * 10**9, 10**7),
    )(core, grads, *rest)


def after(value, *others):
    return lax.optimization_barrier((value, *others))[0]


def swap_mp(value):
    return lax.ppermute(value, "mp", [(0, 1), (1, 0)])


def swap_dp(value, mask, count):
    return lax.ppermute(value, "dp", [(i, i ^ mask) for i in range(count)])


def rows_at(value, at, rows):
    return lax.dynamic_slice_in_dim(value, at * rows, rows, 0)


def rows_set(value, block, at):
    return lax.dynamic_update_slice_in_dim(value, block, at * block.shape[0], 0)


def scatter_sum(block, radix, stride, chip, count):
    digit = (chip // stride) & (radix - 1)
    rows = block.shape[0] // radix
    pieces = [rows_at(block, digit ^ j, rows).astype(low) for j in range(1, radix)]
    total = rows_at(block, digit, rows)
    return total, [swap_dp(piece, 2 * stride * j, count) for j, piece in enumerate(pieces, 1)], pieces


def add_all(total, pieces):
    for piece in pieces:
        total = total + piece.astype(wide)
    return total


def widen(pair):
    rows = pair.shape[0] // 2
    return pair[:rows].astype(wide) + pair[rows:].astype(wide)


def pack_rows(rows):
    top = lax.reduce_precision(rows, exponent_bits=8, mantissa_bits=7)
    return jnp.concatenate([top, rows - top], axis=0).astype(low)


def gather_sum(block, sums, radix, stride, chip, count):
    digit = (chip // stride) & (radix - 1)
    packed = pack_rows(sums)
    extra, rows = packed.shape[0], block.shape[0]
    sent = jnp.concatenate([packed, block], axis=0)
    blocks = {0: block}
    for j in range(1, radix):
        came = swap_dp(sent, 2 * stride * j, count)
        sums = sums + widen(came[:extra])
        blocks[j] = came[extra:]
    orders = [jnp.concatenate([blocks[k ^ d] for k in range(radix)], axis=0) for d in range(radix)]
    whole_block = orders[0]
    for d in range(1, radix):
        whole_block = jnp.where(digit == d, orders[d], whole_block)
    return whole_block, sums


def levels(chips, first):
    out, stride = [], 1
    for radix in first:
        if (chips // stride) % radix == 0:
            out.append((radix, stride))
            stride *= radix
    while stride < chips:
        out.append((2, stride))
        stride *= 2
    return out


def tail_finish_kernel(core_ref, half_ref, came_ref, small_ref, *refs):
    extra = came_ref.shape[0] - half_ref.shape[0]
    rows = extra // 2
    small = small_ref[...] + (came_ref[:rows].astype(wide) + came_ref[rows:extra].astype(wide))
    columns = small.shape[1]
    for row in range(6):
        refs[4 + row][...] = small[row]
    refs[10][...] = small[6, : columns // 2]
    refs[11][...] = small[6, columns // 2 :]
    refs[12][:columns] = small[7]
    refs[12][columns:] = small[8]
    for core in range(2):

        @pl.when(core_ref[0] == core)
        def _():
            width = half_ref.shape[0] // 2
            mine, other = (half_ref, 0), (came_ref, extra)
            (first, at), (second, to) = (mine, other) if core == 0 else (other, mine)
            refs[0][...] = first[at : at + width].astype(wide).T
            refs[1][...] = first[at + width : at + 2 * width].astype(wide).T
            refs[2][...] = second[to : to + width].astype(wide).T
            refs[3][...] = second[to + width : to + 2 * width].astype(wide)


def tail_finish(core, half, came, small):
    rows, features = half.shape
    width = rows // 2
    vmem = pl.BlockSpec(memory_space=pltpu.VMEM)
    vectors = [features] * 6 + [features // 2] * 2 + [2 * features]
    return pl.pallas_call(
        tail_finish_kernel,
        name="tail_finish",
        in_specs=[pl.BlockSpec(memory_space=pltpu.SMEM), vmem, vmem, vmem],
        out_specs=[vmem] * 13,
        out_shape=[shaped((features, width), wide)] * 3
        + [shaped((width, features), wide)]
        + [shaped((n,), wide) for n in vectors],
        compiler_params=params,
        cost_estimate=cost(10**6, 10**7),
    )(core, half, came, small)


def local(
    count,
    tokens,
    tissue,
    first_gain,
    first_shift,
    w_query,
    b_query,
    w_key,
    w_value,
    b_value,
    w_output,
    b_output,
    second_gain,
    second_shift,
    w_upward,
    b_upward,
    w_down,
    b_down,
    cotangent,
):
    place, side = lax.axis_index("dp"), lax.axis_index("mp")
    core = place & 1
    core_list = core.reshape(1)
    own = tokens.shape[0]
    width = w_query.shape[1]
    tokens_other = swap_mp(tokens)
    half_width = width // 2
    w_half = swap_mp(after(rows_at(w_output, core, half_width), tokens_other))
    cotangent_other = swap_mp(after(cotangent, tokens_other))
    b_stack = jnp.concatenate([b_query, jnp.zeros_like(b_query), b_value])[:, None]
    own_qkv, own_normed, w_stack, bias = project(
        side.reshape(1), tokens, first_gain, first_shift, w_query, w_key, w_value, b_stack, tissue
    )

    qkv, own_context, other_context, exact, logs, normed1 = attention_forward(
        own_qkv, own_normed, after(tokens_other, own_qkv), first_gain, first_shift, w_stack, b_stack, bias
    )
    w_traded = swap_dp(after(w_half, own_context), 1, count)
    w_peer = jnp.where(
        core == 0,
        jnp.concatenate([w_half, w_traded], axis=0),
        jnp.concatenate([w_traded, w_half], axis=0),
    )
    peer_own = swap_mp(other_context)
    peer_other = swap_mp(own_context)
    b_up = b_upward[None]
    shared = (w_upward, b_up, w_down)
    second = (b_output, second_gain, second_shift)
    normed_b, active_b, pre_b, part_b, branch_b, sum_b = feed_forward(
        tokens_other, other_context, peer_other, w_output, w_peer, *second, cotangent_other, *shared
    )
    came = swap_mp(part_b)
    hidden, part_a, branch_a, grad_bupward, grad_upward, grad_down = feed_forward(
        after(tokens, part_b), own_context, peer_own, w_output, w_peer, *second, cotangent, *shared,
        other=(normed_b, cotangent_other, active_b, pre_b, sum_b),
    )
    sum_down, sum_upward = lax.psum((grad_down, grad_upward), "dp")

    grad_hidden, grad_branch, mine_own, peer_grad, sums = middle(
        part_a, came, after(hidden, grad_down), cotangent, second_gain, w_output, w_peer
    )
    mine_other = swap_mp(peer_grad)

    def rest(mine_own, mine_other):
        chip = place >> 1
        steps = levels(count // 2, TAIL_RADICES)
        branch_other = swap_mp(after(grad_branch, mine_other))
        branch_came = swap_mp(after(branch_b, mine_other))
        grads = attention_backward(qkv, exact, logs, bias, mine_own, mine_other)
        away, kept = tail_gradient(
            core_list, grads, normed1, own_context, grad_branch, other_context, branch_other
        )
        half = kept + swap_dp(away, 1, count).astype(wide)
        total, arrived, sent = scatter_sum(half, *steps[0], chip, count)
        first_a, first_b, stack_sums = by_inputs(after(grads, branch_came, *sent), w_stack)
        came = swap_mp(first_b)
        half = add_all(total, arrived)
        for step in steps[1:]:
            total, arrived, sent = scatter_sum(half, *step, chip, count)
            half = add_all(total, arrived)
        half = half.astype(low)
        grad_tokens, sums_first, output = last(
            first_a, came, tokens, grad_hidden, first_gain, b_down, hidden, branch_a, branch_came
        )

        shared = jnp.concatenate([sums_first[:2], sums[:4]], axis=0)
        shared = shared + swap_mp(shared)
        columns = shared.shape[1]
        split = jnp.concatenate([stack_sums[0, :width], stack_sums[0, 2 * width :], grad_bupward[0]])
        small = jnp.concatenate([shared, split.reshape(-1, columns)], axis=0)
        small = jnp.pad(small, ((0, -small.shape[0] % 4), (0, 0)))
        for step in reversed(steps):
            half, small = gather_sum(half, small, *step, chip, count)
        came = swap_dp(jnp.concatenate([pack_rows(small), half], axis=0), 1, count)
        return (output, grad_tokens, *tail_finish(core_list, half, came, small))

    def none(mine_own, mine_other):
        return jax.tree.map(lambda a: jnp.zeros(a.shape, a.dtype), jax.eval_shape(rest, mine_own, mine_other))

    output, grad_tokens, grad_wquery, grad_wkey, grad_wvalue, grad_woutput, *small = lax.cond(
        tissue[0, 0] >= 0, rest, none, after(mine_own, grad_upward), mine_other
    )
    return (
        output,
        grad_tokens,
        small[0],
        small[1],
        grad_wquery,
        small[6],
        grad_wkey,
        grad_wvalue,
        small[7],
        grad_woutput,
        small[2],
        small[3],
        small[4],
        sum_upward.astype(wide),
        small[8],
        sum_down.astype(wide),
        small[5],
    )


def solution(mesh):
    in_specs = (
        P(("dp", "mp"), None),
        P("dp", None),
        P(),
        P(),
        P(None, "mp"),
        P("mp"),
        P(None, "mp"),
        P(None, "mp"),
        P("mp"),
        P("mp", None),
        P(),
        P(),
        P(),
        P(None, "mp"),
        P("mp"),
        P("mp", None),
        P(),
        P(("dp", "mp"), None),
    )
    out_specs = (
        P(("dp", "mp"), None),
        P(("dp", "mp"), None),
        P(),
        P(),
        P(None, "mp"),
        P("mp"),
        P(None, "mp"),
        P(None, "mp"),
        P("mp"),
        P("mp", None),
        P(),
        P(),
        P(),
        P(None, "mp"),
        P("mp"),
        P("mp", None),
        P(),
    )
    return jax.shard_map(
        functools.partial(local, mesh.shape["dp"]), mesh=mesh, in_specs=in_specs, out_specs=out_specs, check_vma=False)
```

time: 299 us -> 241 us (0.81)
  starting transfers between devices: 57.7 us -> 20.7 us
  local copies, waits for them, and re-layouts: 28 us -> 13.4 us
  between operations: 1.61 us -> 14.9 us
  waiting for transfers between devices: 111 us -> 100 us
  other arithmetic: 20.1 us -> 14.1 us
    ppermute x38 -> x9, starting transfers between devices: 44.2 us -> 6.14 us  [swap_dp(): return lax.ppermute(value, 'dp', [(i, i ^ mask) for i in range(count)])]
    ppermute x38 -> x9, waiting for transfers between devices: 78.6 us -> 62.2 us  [swap_dp(): return lax.ppermute(value, 'dp', [(i, i ^ mask) for i in range(count)])]
    unnamed x89 -> x44, local copies, waits for them, and re-layouts: 16.5 us -> 7.95 us
    ppermute x11, waiting for transfers between devices: 32.8 us -> 38 us  [swap_mp(): return lax.ppermute(value, 'mp', [(0, 1), (1, 0)])]
    another operation x9 -> x1, local copies, waits for them, and re-layouts: 4.22 us -> 0.01 us  [the longest x7 4.17 us: local(): jnp.stack([first_gain, first_shift, b_output, second_gain, second_shift,...]
    add x17 -> x4, other arithmetic: 7.72 us -> 3.82 us  [the longest x2 2.21 us: add_all(): total = total + piece.astype(wide)]
    cond x0 -> x20, local copies, waits for them, and re-layouts: none -> 3 us
    convert_element_type x6 -> x3, other arithmetic: 8.95 us -> 7.22 us  [the longest x1 4.65 us: local(): sum_upward.astype(wide)]
  transfers between devices with their start and end apart: 49 -> 21, of which waited for: 22 -> 12; matrix products, arithmetic and copies ran while one was open for 11% -> 4% of each run, Pallas kernels for 26% -> 31%
where the time goes in v2:
time: 241 us
  waiting for transfers between devices  100 us (41%)
  Pallas kernels  77.2 us (32%)
  starting transfers between devices  20.7 us (9%)
  between operations  14.9 us (6%)
  other arithmetic  14.1 us (6%)
  local copies, waits for them, and re-layouts  13.4 us (6%)
    ppermute x9, waiting for transfers between devices, swap_dp(): return lax.ppermute(value, 'dp', [(i, i ^ mask) for i in range(count)])  62.2 us
    ppermute x11, waiting for transfers between devices, swap_mp(): return lax.ppermute(value, 'mp', [(0, 1), (1, 0)])  38 us
    pallas_call x2, Pallas kernels, feed_forward(): pl.pallas_call(functools.partial(feed_forward_kernel, other=bool(other)),...  22.8 us
    pallas_call x1, Pallas kernels, attention_backward(): pl.pallas_call(attention_backward_kernel, name='attention_backward', grid...  16.6 us
    pallas_call x1, Pallas kernels, attention_forward(): pl.pallas_call(attention_forward_kernel, name='attention_forward', grid=(...  15.2 us
    ppermute x11, starting transfers between devices, swap_mp(): return lax.ppermute(value, 'mp', [(0, 1), (1, 0)])  14.5 us
    unnamed x44, local copies, waits for them, and re-layouts  7.95 us
    pallas_call x1, Pallas kernels, tail_gradient(): pl.pallas_call(tail_gradient_kernel, name='tail_gradient', grid_spec=pltp...  6.18 us
  transfers between devices with their start and end apart: 21, of which 12 were waited for; matrix products, arithmetic and copies ran while one was open for 4% of the time, Pallas kernels for 31%

profile of v2, /device:TPU:0, one launch (start us, length us, event | category | flops | bytes accessed | tf_op | source)
XLA Modules:
  0.0 240.7 jit_solution(1903411182909887276)
XLA Ops:
  7.2 3.0 %collective-permute-start.12 = (bf16[392,768]{1,0:T(8,128)(2,1)}, bf16[392,768]{1,0:T(8,128)(2,1)S(1)}, u32[]{:S(2)}, u32[]{:S(2)}) collective-permute-start(bf16[392,768]{1,0:T(8,128)(2,1)} %tokens_ref.2), channel_id=1, source_target_pairs={{0,1},{1,0},{2,3},{3,2},{4,5},{5,4},{6,7},{7,6},{8,9},{9,8},{10,11... | collective-permute-start | bytes 1806344 | tf_op jit(solution)/shard_map/ppermute | solution.py:488
  15.8 2.6 %project_own_rows.1 = (bf16[1152,392]{1,0:T(8,128)(2,1)S(1)}, bf16[392,768]{1,0:T(8,128)(2,1)S(1)}, bf16[1152,768]{1,0:T(8,128)(2,1)S(1)}, bf16[16,784]{1,0:T(8,128)(2,1)S(1)}) custom-call(s32[1]{0:T(128)} %bitcast.2.side_ref, bf16[392,768]{1,0:T(8,128)(2,1)} %tokens_ref.2, f32[768]{0:T(1024)} %gain_ref.6, f32[768]{0:T(1024)S(1)} %copy-done.10, ...), custom_call_target="tpu_custom_call" | custom-call | flops 1000000000 | bytes 5000000 | tf_op jit(solution)/shard_map/project_own_rows/pallas_call | solution.py:97
  18.4 5.6 %collective-permute-done.12.other_ref.tokens_ref = bf16[392,768]{1,0:T(8,128)(2,1)S(1)} collective-permute-done((bf16[392,768]{1,0:T(8,128)(2,1)}, bf16[392,768]{1,0:T(8,128)(2,1)S(1)}, u32[]{:S(2)}, u32[]{:S(2)}) %collective-permute-start.12) | collective-permute-done | bytes 602144 | tf_op jit(solution)/shard_map/ppermute | solution.py:488
  26.1 15.2 %attention_forward.1 = (bf16[1152,784]{1,0:T(8,128)(2,1)}, bf16[384,392]{1,0:T(8,128)(2,1)}, bf16[384,392]{1,0:T(8,128)(2,1)}, f32[384,784]{1,0:T(8,128)}, f32[6...) custom-call(bf16[1152,392]{1,0:T(8,128)(2,1)S(1)} %get-tuple-element.157.own_ref, ...), custom_call_target="tpu_custom_call" | custom-call | flops 10000000000 | bytes 10000000 | tf_op jit(solution)/shard_map/attention_forward/pallas_call | solution.py:158
  44.9 9.1 %collective-permute-done.13.peer_ref = bf16[384,392]{1,0:T(8,128)(2,1)S(1)} collective-permute-done((bf16[384,392]{1,0:T(8,128)(2,1)}, bf16[384,392]{1,0:T(8,128)(2,1)S(1)}, u32[]{:S(2)}, u32[]{:S(2)}) %collective-permute-start.13) | collective-permute-done | bytes 301088 | tf_op jit(solution)/shard_map/ppermute | solution.py:488
  57.4 8.5 %feed_forward.2 = (bf16[392,768]{1,0:T(8,128)(2,1)S(1)}, bf16[392,1536]{1,0:T(8,128)(2,1)S(1)}, bf16[392,1536]{1,0:T(8,128)(2,1)S(1)}, bf16[392,768]{1,0:T(8,128...) custom-call(bf16[392,768]{1,0:T(8,128)(2,1)S(1)} %collective-permute-done.12.other_ref.tokens_ref, ...), custom_call_target="tpu_custom_call" | custom-call | flops 5000000000 | bytes 10000000 | tf_op jit(solution)/shard_map/feed_forward/pallas_call | solution.py:321
  67.2 14.3 %feed_forward.3 = (f32[392,768]{1,0:T(8,128)S(1)}, bf16[392,768]{1,0:T(8,128)(2,1)S(1)}, bf16[392,768]{1,0:T(8,128)(2,1)}, f32[1,1536]{1,0:T(1,128)S(1)}, bf16[7...) custom-call(bf16[392,768]{1,0:T(8,128)(2,1)S(1)} %copy-done.22, bf16[384,392]{1,0:T(8,128)(2,1)} %get-tuple-element.166.mine_ref, ...), custom_call_target="tpu_custom_call" | custom-call | flops 5000000000 | bytes 10000000 | tf_op jit(solution)/shard_map/feed_forward/pallas_call | solution.py:321
  86.4 7.7 %collective-permute-done.19 = bf16[384,392]{1,0:T(8,128)(2,1)S(1)} collective-permute-done((bf16[384,392]{1,0:T(8,128)(2,1)S(1)}, bf16[384,392]{1,0:T(8,128)(2,1)S(1)}, u32[]{:S(2)}, u32[]{:S(2)}) %collective-permute-start.19) | collective-permute-done | bytes 301088 | tf_op jit(solution)/shard_map/ppermute | solution.py:488
  94.2 132.4 %conditional.1 = (bf16[392,768]{1,0:T(8,128)(2,1)}, f32[392,768]{1,0:T(8,128)}, f32[768,384]{1,0:T(8,128)}, f32[768,384]{1,0:T(8,128)}, f32[768,384]{1,0:T(8,128...) conditional(s32[]{:T(128)} %bitcast.1, () %tuple.26, ...), branch_computations={%region_0.1_spmd, %region_1.2_spmd} | conditional | flops 14120058880 | bytes 143829024 | solution.py:698
  94.7 16.6 %attention_backward.1.grads_ref = bf16[1152,784]{1,0:T(8,128)(2,1)S(1)} custom-call(bf16[1152,784]{1,0:T(8,128)(2,1)} %get-tuple-element.45.qkv_ref, f32[384,784]{1,0:T(8,128)S(1)} %get-tuple-element.46.exact_ref, f32[6,1,784]{2,1,0:T(1,128)S(1)} %get-tuple-element.47.log_ref, bf16[16,784]{1,0:T(8,128)(2,1)S(1)} %get-tuple-element.48.bias_ref, ...), custom_call_target="tpu_custom_call" | custom-call | flops 10000000000 | bytes 10000000 | tf_op jit(solution)/shard_map/cond/branch_1_fun/attention_backward/pallas_call | solution.py:224
  111.4 6.2 %tail_gradient.1 = (bf16[768,768]{1,0:T(8,128)(2,1)}, f32[768,768]{1,0:T(8,128)S(1)}) custom-call(s32[1]{0:T(128)} %bitcast.core_ref, bf16[1152,784]{1,0:T(8,128)(2,1)S(1)} %attention_backward.1.grads_ref, bf16[784,768]{1,0:T(8,128)(2,1)S(1)} %copy-done.30, bf16[384,392]{1,0:T(8,128)(2,1)} %get-tuple-element.55.own_context_ref, bf16[392,768]{1,0:T(8,128)(2,1)} %copy-done.27, ...), custom_call_target="tpu_custom_call" | custom-call | flops 2000000000 | bytes 10000000 | tf_op jit(solution)/shard_map/cond/branch_1_fun/tail_gradient/pallas_call | solution.py:459
  126.2 7.6 %collective-permute-done.branch_came_ref = bf16[392,768]{1,0:T(8,128)(2,1)S(1)} collective-permute-done((bf16[392,768]{1,0:T(8,128)(2,1)}, bf16[392,768]{1,0:T(8,128)(2,1)S(1)}, u32[]{:S(2)}, u32[]{:S(2)}) %collective-permute-start) | collective-permute-done | bytes 602144 | tf_op jit(solution)/shard_map/cond/branch_1_fun/ppermute | solution.py:488
  135.4 4.6 %first_normed_gradient.1 = (bf16[392,768]{1,0:T(8,128)(2,1)S(1)}, bf16[392,768]{1,0:T(8,128)(2,1)S(1)}, f32[8,1152]{1,0:T(8,128)S(1)}) custom-call(bf16[1152,784]{1,0:T(8,128)(2,1)S(1)} %copy-done.15, bf16[1152,768]{1,0:T(8,128)(2,1)} %get-tuple-element.63.w_ref), custom_call_target="tpu_custom_call" | custom-call | flops 2000000000 | bytes 5000000 | tf_op jit(solution)/shard_map/cond/branch_1_fun/first_normed_gradient/pallas_call | solution.py:410
  141.5 3.0 %collective-permute-done.5 = bf16[384,768]{1,0:T(8,128)(2,1)} collective-permute-done((bf16[384,768]{1,0:T(8,128)(2,1)}, bf16[384,768]{1,0:T(8,128)(2,1)}, u32[]{:S(2)}, u32[]{:S(2)}) %collective-permute-start.5) | collective-permute-done | bytes 589856 | tf_op jit(solution)/shard_map/cond/branch_1_fun/ppermute | solution.py:492
  147.5 7.8 %collective-permute-done.3.came_ref = bf16[392,768]{1,0:T(8,128)(2,1)S(1)} collective-permute-done((bf16[392,768]{1,0:T(8,128)(2,1)S(1)}, bf16[392,768]{1,0:T(8,128)(2,1)S(1)}, u32[]{:S(2)}, u32[]{:S(2)}) %collective-permute-start.3) | collective-permute-done | bytes 602144 | tf_op jit(solution)/shard_map/cond/branch_1_fun/ppermute | solution.py:488
  155.3 4.2 %first_norm_backward.1 = (f32[392,768]{1,0:T(8,128)}, f32[8,768]{1,0:T(8,128)S(1)}, bf16[392,768]{1,0:T(8,128)(2,1)}) custom-call(bf16[392,768]{1,0:T(8,128)(2,1)S(1)} %get-tuple-element.64.part_ref, bf16[392,768]{1,0:T(8,128)(2,1)S(1)} %collective-permute-done.3.came_ref, bf16[392,768]{1,0:T(8,128)(2,1)S(1)} %copy-done.23, ...), custom_call_target="tpu_custom_call" | custom-call | flops 100000000 | bytes 5000000 | tf_op jit(solution)/shard_map/cond/branch_1_fun/first_norm_backward/pallas_call | solution.py:391
  162.2 2.7 %collective-permute-start.7 = (bf16[96,768]{1,0:T(8,128)(2,1)S(1)}, bf16[96,768]{1,0:T(8,128)(2,1)S(1)}, u32[]{:S(2)}, u32[]{:S(2)}) collective-permute-start(bf16[96,768]{1,0:T(8,128)(2,1)S(1)} %dynamic-slice_convert_fusion.2), channel_id=1, source_target_pairs={{0,16},{2,18},{4,20},{6,22},{8,24},{10,26},{12,28},{14,30},{16,0},... | collective-permute-start | bytes 442376 | tf_op jit(solution)/shard_map/cond/branch_1_fun/ppermute | solution.py:492
  164.9 7.2 %collective-permute-done.7 = bf16[96,768]{1,0:T(8,128)(2,1)S(1)} collective-permute-done((bf16[96,768]{1,0:T(8,128)(2,1)S(1)}, bf16[96,768]{1,0:T(8,128)(2,1)S(1)}, u32[]{:S(2)}, u32[]{:S(2)}) %collective-permute-start.7) | collective-permute-done | bytes 147488 | tf_op jit(solution)/shard_map/cond/branch_1_fun/ppermute | solution.py:492
  172.3 15.0 %collective-permute-done.8 = bf16[120,768]{1,0:T(8,128)(2,1)S(1)} collective-permute-done((bf16[120,768]{1,0:T(8,128)(2,1)S(1)}, bf16[120,768]{1,0:T(8,128)(2,1)S(1)}, u32[]{:S(2)}, u32[]{:S(2)}) %collective-permute-start.8) | collective-permute-done | bytes 184352 | tf_op jit(solution)/shard_map/cond/branch_1_fun/ppermute | solution.py:492
  187.5 17.1 %collective-permute-done.9 = bf16[216,768]{1,0:T(8,128)(2,1)S(1)} collective-permute-done((bf16[216,768]{1,0:T(8,128)(2,1)S(1)}, bf16[216,768]{1,0:T(8,128)(2,1)S(1)}, u32[]{:S(2)}, u32[]{:S(2)}) %collective-permute-start.9) | collective-permute-done | bytes 331808 | tf_op jit(solution)/shard_map/cond/branch_1_fun/ppermute | solution.py:492
  205.0 15.2 %collective-permute-done.10 = bf16[408,768]{1,0:T(8,128)(2,1)S(1)} collective-permute-done((bf16[408,768]{1,0:T(8,128)(2,1)S(1)}, bf16[408,768]{1,0:T(8,128)(2,1)S(1)}, u32[]{:S(2)}, u32[]{:S(2)}) %collective-permute-start.10) | collective-permute-done | bytes 626720 | tf_op jit(solution)/shard_map/cond/branch_1_fun/ppermute | solution.py:492
  220.9 2.9 %collective-permute-done.11.came_ref = bf16[792,768]{1,0:T(8,128)(2,1)S(1)} collective-permute-done((bf16[792,768]{1,0:T(8,128)(2,1)S(1)}, bf16[792,768]{1,0:T(8,128)(2,1)S(1)}, u32[]{:S(2)}, u32[]{:S(2)}) %collective-permute-start.11) | collective-permute-done | bytes 1216544 | tf_op jit(solution)/shard_map/cond/branch_1_fun/ppermute | solution.py:492
  223.8 2.8 %tail_finish.1 = (f32[768,384]{1,0:T(8,128)}, f32[768,384]{1,0:T(8,128)}, f32[768,384]{1,0:T(8,128)}, f32[384,768]{1,0:T(8,128)}, f32[768]{0:T(1024)}, /*index=5...) custom-call(s32[1]{0:T(128)} %bitcast.core_ref, ...), custom_call_target="tpu_custom_call" | custom-call | flops 1000000 | bytes 10000000 | tf_op jit(solution)/shard_map/cond/branch_1_fun/tail_finish/pallas_call | solution.py:585
  226.7 4.6 %convert_element_type.62 = f32[768,1536]{1,0:T(8,128)} convert(bf16[768,1536]{1,0:T(8,128)(2,1)} %get-tuple-element.210) | non-fusion elementwise | flops 1179648 | bytes 7077888 | tf_op jit(solution)/shard_map/convert_element_type | solution.py:715
  (134 shorter events, 41.9 us)
Async XLA Ops:
  7.2 219.4 %all-reduce.4.cloned.1.call-start = ((), (), s32[]{:S(2)}) async-start(), calls=%async_computation | async-start | bytes 9437184 | tf_op jit(solution)/shard_map/psum | solution.py:655
  7.2 16.8 %collective-permute-start.12 = (bf16[392,768]{1,0:T(8,128)(2,1)}, bf16[392,768]{1,0:T(8,128)(2,1)S(1)}, u32[]{:S(2)}, u32[]{:S(2)}) collective-permute-start(bf16[392,768]{1,0:T(8,128)(2,1)} %tokens_ref.2), channel_id=1, source_target_pairs={{0,1},{1,0},{2,3},{3,2},{4,5},{5,4},{6,7},{7,6},{8,9},{9,8},{10,11... | collective-permute-start | bytes 1806344 | tf_op jit(solution)/shard_map/ppermute | solution.py:488
  24.1 17.2 %collective-permute-start.14 = (bf16[192,768]{1,0:T(8,128)(2,1)S(1)}, bf16[192,768]{1,0:T(8,128)(2,1)S(1)}, u32[]{:S(2)}, u32[]{:S(2)}) collective-permute-start(bf16[192,768]{1,0:T(8,128)(2,1)S(1)} %constant_dynamic-slice_fusion), channel_id=1, source_target_pairs={{0,1},{1,0},{2,3},{3,2},{4,5},{5,4},{6,7},{7,6},{8,9},{9,8},{10,11... | collective-permute-start | bytes 884744 | tf_op jit(solution)/shard_map/ppermute | solution.py:488
  25.8 28.2 %collective-permute-start.16 = (bf16[392,768]{1,0:T(8,128)(2,1)S(1)}, bf16[392,768]{1,0:T(8,128)(2,1)S(1)}, u32[]{:S(2)}, u32[]{:S(2)}) collective-permute-start(bf16[392,768]{1,0:T(8,128)(2,1)S(1)} %copy-done.1), channel_id=1, source_target_pairs={{0,1},{1,0},{2,3},{3,2},{4,5},{5,4},{6,7},{7,6},{8,9},{9,8},{10,11... | collective-permute-start | bytes 1806344 | tf_op jit(solution)/shard_map/ppermute | solution.py:488
  26.1 27.9 %copy-start.2 = (f32[768]{0:T(1024)S(1)}, f32[768]{0:T(1024)}, u32[]{:S(2)}) copy-start(f32[768]{0:T(1024)} %gain_ref.9) | copy-start | bytes 9220
  26.1 27.9 %copy-start.11 = (f32[768]{0:T(1024)S(1)}, f32[768]{0:T(1024)}, u32[]{:S(2)}) copy-start(f32[768]{0:T(1024)} %b_ref.3) | copy-start | bytes 9220
  26.1 27.9 %copy-start.12 = (f32[768]{0:T(1024)S(1)}, f32[768]{0:T(1024)}, u32[]{:S(2)}) copy-start(f32[768]{0:T(1024)} %shift_ref.7) | copy-start | bytes 9220
  41.3 2.3 collective-permute-start.15
  41.4 12.6 %collective-permute-start.13 = (bf16[384,392]{1,0:T(8,128)(2,1)}, bf16[384,392]{1,0:T(8,128)(2,1)S(1)}, u32[]{:S(2)}, u32[]{:S(2)}) collective-permute-start(bf16[384,392]{1,0:T(8,128)(2,1)} %get-tuple-element.166.mine_ref), channel_id=1, source_target_pairs={{0,1},{1,0},{2,3},{3,2},{4,5},{5,4},{6,7},{7,6},{8,9},{9,8},{10,11... | collective-permute-start | bytes 903176 | tf_op jit(solution)/shard_map/ppermute | solution.py:488
  43.2 23.9 %collective-permute-start.17 = (bf16[384,392]{1,0:T(8,128)(2,1)}, bf16[384,392]{1,0:T(8,128)(2,1)S(1)}, u32[]{:S(2)}, u32[]{:S(2)}) collective-permute-start(bf16[384,392]{1,0:T(8,128)(2,1)} %get-tuple-element.165.mine_ref), channel_id=1, source_target_pairs={{0,1},{1,0},{2,3},{3,2},{4,5},{5,4},{6,7},{7,6},{8,9},{9,8},{10,11... | collective-permute-start | bytes 903176 | tf_op jit(solution)/shard_map/ppermute | solution.py:488
  65.8 15.7 %collective-permute-start.18 = (bf16[392,768]{1,0:T(8,128)(2,1)S(1)}, bf16[392,768]{1,0:T(8,128)(2,1)S(1)}, u32[]{:S(2)}, u32[]{:S(2)}) collective-permute-start(bf16[392,768]{1,0:T(8,128)(2,1)S(1)} %get-tuple-element.170), channel_id=1, source_target_pairs={{0,1},{1,0},{2,3},{3,2},{4,5},{5,4},{6,7},{7,6},{8,9},{9,8},{10,11... | collective-permute-start | bytes 1806344 | tf_op jit(solution)/shard_map/ppermute | solution.py:488
  83.8 10.3 %collective-permute-start.19 = (bf16[384,392]{1,0:T(8,128)(2,1)S(1)}, bf16[384,392]{1,0:T(8,128)(2,1)S(1)}, u32[]{:S(2)}, u32[]{:S(2)}) collective-permute-start(bf16[384,392]{1,0:T(8,128)(2,1)S(1)} %get-tuple-element.183), channel_id=1, source_target_pairs={{0,1},{1,0},{2,3},{3,2},{4,5},{5,4},{6,7},{7,6},{8,9},{9,8},{10,11... | collective-permute-start | bytes 903176 | tf_op jit(solution)/shard_map/ppermute | solution.py:488
  94.2 17.2 %collective-permute-start.1 = (bf16[392,768]{1,0:T(8,128)(2,1)S(1)}, bf16[392,768]{1,0:T(8,128)(2,1)S(1)}, u32[]{:S(2)}, u32[]{:S(2)}) collective-permute-start(bf16[392,768]{1,0:T(8,128)(2,1)S(1)} %get-tuple-element.58.own_branch_ref), channel_id=1, source_target_pairs={{0,1},{1,0},{2,3},{3,2},{4,5},{5,4},{6,7},{7,6},{8,9},{9,8},{10,11... | collective-permute-start | bytes 1806344 | tf_op jit(solution)/shard_map/cond/branch_1_fun/ppermute | solution.py:488
  117.6 3.2 %collective-permute-start.2 = (bf16[768,768]{1,0:T(8,128)(2,1)}, bf16[768,768]{1,0:T(8,128)(2,1)}, u32[]{:S(2)}, u32[]{:S(2)}) collective-permute-start(bf16[768,768]{1,0:T(8,128)(2,1)} %get-tuple-element.60), channel_id=1, source_target_pairs={{0,2},{2,0},{4,6},{6,4},{8,10},{10,8},{12,14},{14,12},{16,18},{18,... | collective-permute-start | bytes 3538952 | tf_op jit(solution)/shard_map/cond/branch_1_fun/ppermute | solution.py:492
  117.6 16.2 %collective-permute-start = (bf16[392,768]{1,0:T(8,128)(2,1)}, bf16[392,768]{1,0:T(8,128)(2,1)S(1)}, u32[]{:S(2)}, u32[]{:S(2)}) collective-permute-start(bf16[392,768]{1,0:T(8,128)(2,1)} %get-tuple-element.52), channel_id=1, source_target_pairs={{0,1},{1,0},{2,3},{3,2},{4,5},{5,4},{6,7},{7,6},{8,9},{9,8},{10,11... | collective-permute-start | bytes 1806344 | tf_op jit(solution)/shard_map/cond/branch_1_fun/ppermute | solution.py:488
  124.7 19.9 %collective-permute-start.5 = (bf16[384,768]{1,0:T(8,128)(2,1)}, bf16[384,768]{1,0:T(8,128)(2,1)}, u32[]{:S(2)}, u32[]{:S(2)}) collective-permute-start(bf16[384,768]{1,0:T(8,128)(2,1)} %dynamic-slice_convert_fusion), channel_id=1, source_target_pairs={{0,4},{2,6},{4,0},{6,2},{8,12},{10,14},{12,8},{14,10},{16,20},{18,... | collective-permute-start | bytes 1769480 | tf_op jit(solution)/shard_map/cond/branch_1_fun/ppermute | solution.py:492
  140.0 15.3 %collective-permute-start.3 = (bf16[392,768]{1,0:T(8,128)(2,1)S(1)}, bf16[392,768]{1,0:T(8,128)(2,1)S(1)}, u32[]{:S(2)}, u32[]{:S(2)}) collective-permute-start(bf16[392,768]{1,0:T(8,128)(2,1)S(1)} %get-tuple-element.65), channel_id=1, source_target_pairs={{0,1},{1,0},{2,3},{3,2},{4,5},{5,4},{6,7},{7,6},{8,9},{9,8},{10,11... | collective-permute-start | bytes 1806344 | tf_op jit(solution)/shard_map/cond/branch_1_fun/ppermute | solution.py:488
  145.8 15.3 %collective-permute-start.6 = (bf16[192,768]{1,0:T(8,128)(2,1)S(1)}, bf16[192,768]{1,0:T(8,128)(2,1)}, u32[]{:S(2)}, u32[]{:S(2)}) collective-permute-start(bf16[192,768]{1,0:T(8,128)(2,1)S(1)} %dynamic-slice_convert_fusion.1), channel_id=1, source_target_pairs={{0,8},{2,10},{4,12},{6,14},{8,0},{10,2},{12,4},{14,6},{16,24},{18,... | collective-permute-start | bytes 884744 | tf_op jit(solution)/shard_map/cond/branch_1_fun/ppermute | solution.py:492
  159.5 5.3 %collective-permute-start.4 = (f32[6,768]{1,0:T(8,128)S(1)}, f32[6,768]{1,0:T(8,128)S(1)}, u32[]{:S(2)}, u32[]{:S(2)}) collective-permute-start(f32[6,768]{1,0:T(8,128)S(1)} %pad_maximum_fusion.4), channel_id=1, source_target_pairs={{0,1},{1,0},{2,3},{3,2},{4,5},{5,4},{6,7},{7,6},{8,9},{9,8},{10,11... | collective-permute-start | bytes 55304 | tf_op jit(solution)/shard_map/cond/branch_1_fun/ppermute | solution.py:488
  162.2 9.9 %collective-permute-start.7 = (bf16[96,768]{1,0:T(8,128)(2,1)S(1)}, bf16[96,768]{1,0:T(8,128)(2,1)S(1)}, u32[]{:S(2)}, u32[]{:S(2)}) collective-permute-start(bf16[96,768]{1,0:T(8,128)(2,1)S(1)} %dynamic-slice_convert_fusion.2), channel_id=1, source_target_pairs={{0,16},{2,18},{4,20},{6,22},{8,24},{10,26},{12,28},{14,30},{16,0},... | collective-permute-start | bytes 442376 | tf_op jit(solution)/shard_map/cond/branch_1_fun/ppermute | solution.py:492
  172.2 15.1 %collective-permute-start.8 = (bf16[120,768]{1,0:T(8,128)(2,1)S(1)}, bf16[120,768]{1,0:T(8,128)(2,1)S(1)}, u32[]{:S(2)}, u32[]{:S(2)}) collective-permute-start(bf16[120,768]{1,0:T(8,128)(2,1)S(1)} %pad_maximum_fusion.3), channel_id=1, source_target_pairs={{0,16},{2,18},{4,20},{6,22},{8,24},{10,26},{12,28},{14,30},{16,0},... | collective-permute-start | bytes 552968 | tf_op jit(solution)/shard_map/cond/branch_1_fun/ppermute | solution.py:492
  187.4 17.2 %collective-permute-start.9 = (bf16[216,768]{1,0:T(8,128)(2,1)S(1)}, bf16[216,768]{1,0:T(8,128)(2,1)S(1)}, u32[]{:S(2)}, u32[]{:S(2)}) collective-permute-start(bf16[216,768]{1,0:T(8,128)(2,1)S(1)} %pad_maximum_fusion.2), channel_id=1, source_target_pairs={{0,8},{2,10},{4,12},{6,14},{8,0},{10,2},{12,4},{14,6},{16,24},{18,... | collective-permute-start | bytes 995336 | tf_op jit(solution)/shard_map/cond/branch_1_fun/ppermute | solution.py:492
  204.9 15.2 %collective-permute-start.10 = (bf16[408,768]{1,0:T(8,128)(2,1)S(1)}, bf16[408,768]{1,0:T(8,128)(2,1)S(1)}, u32[]{:S(2)}, u32[]{:S(2)}) collective-permute-start(bf16[408,768]{1,0:T(8,128)(2,1)S(1)} %pad_maximum_fusion.1), channel_id=1, source_target_pairs={{0,4},{2,6},{4,0},{6,2},{8,12},{10,14},{12,8},{14,10},{16,20},{18,... | collective-permute-start | bytes 1880072 | tf_op jit(solution)/shard_map/cond/branch_1_fun/ppermute | solution.py:492
  220.9 3.0 %collective-permute-start.11 = (bf16[792,768]{1,0:T(8,128)(2,1)S(1)}, bf16[792,768]{1,0:T(8,128)(2,1)S(1)}, u32[]{:S(2)}, u32[]{:S(2)}) collective-permute-start(bf16[792,768]{1,0:T(8,128)(2,1)S(1)} %pad_maximum_fusion), channel_id=1, source_target_pairs={{0,2},{2,0},{4,6},{6,4},{8,10},{10,8},{12,14},{14,12},{16,18},{18,... | collective-permute-start | bytes 3649544 | tf_op jit(solution)/shard_map/cond/branch_1_fun/ppermute | solution.py:492
  (29 other events, 233.5 us)
Sparse Core Ops, SparseCore 0:
  84.0 135.7 all-reduce.3

commit v3 on v2

v3 whole, which is shorter than its diff:
```python
import functools

import jax
import jax.numpy as jnp
from jax import lax
from jax.experimental import pallas as pl
from jax.experimental.pallas import tpu as pltpu
from jax.sharding import PartitionSpec as P

HEAD = 64
GROUP = 3
BLOCK = 512
epsilon = 1e-06
masked_score = -1e30
low, wide = jnp.bfloat16, jnp.float32
params = pltpu.CompilerParams(vmem_limit_bytes=24 << 20)


def cost(flops, moved, exps=0):
    return pl.CostEstimate(flops=flops, bytes_accessed=moved, transcendentals=exps)


def whole(array):
    return pl.BlockSpec(array.shape, lambda *_: (0,) * len(array.shape))


def shaped(shape, kind):
    return jax.ShapeDtypeStruct(shape, kind)


def stored(shape, kind):
    return pltpu.HBM(shape, kind)


def ordered_call(
    kernel, args, in_specs, out_specs, out_shape, behind=(), through=(), prefetch=0, grid=(), scratch=(), **rest
):
    count, outputs = len(args), len(out_shape)
    skipped = len(behind) + len(through)
    place = pl.BlockSpec(memory_space=pl.ANY)

    def body(*refs):
        given, refs = refs[:count], refs[count + skipped :]
        kernel(*given, *refs[:outputs], *refs[outputs + len(through) :])

    first = count + len(behind)
    out = pl.pallas_call(
        body,
        grid_spec=pltpu.PrefetchScalarGridSpec(
            num_scalar_prefetch=prefetch,
            grid=grid,
            in_specs=list(in_specs) + [place] * skipped,
            out_specs=list(out_specs) + [place] * len(through),
            scratch_shapes=list(scratch),
        ),
        out_shape=list(out_shape) + [shaped(a.shape, a.dtype) for a in through],
        input_output_aliases={first + k: outputs + k for k in range(len(through))},
        compiler_params=params,
        **rest,
    )(*args, *behind, *through)
    return list(out[:outputs]), list(out[outputs:])


def far(array):
    return pltpu.with_memory_space_constraint(array, pltpu.HBM)


def mm(left, right, left_dim, right_dim):
    return lax.dot_general(
        left, right, (((left_dim,), (right_dim,)), ((), ())), preferred_element_type=wide
    )


def normalize(values, gain, shift):
    centred = values - jnp.mean(values, axis=-1, keepdims=True)
    spread = jnp.mean(centred * centred, axis=-1, keepdims=True)
    return centred * lax.rsqrt(spread + epsilon) * gain + shift


def normalize_back(values, gain, grad):
    centred = values - jnp.mean(values, axis=-1, keepdims=True)
    inverse = lax.rsqrt(jnp.mean(centred * centred, axis=-1, keepdims=True) + epsilon)
    unit = centred * inverse
    scaled = grad * gain
    by_values = inverse * (
        scaled
        - jnp.mean(scaled, axis=-1, keepdims=True)
        - unit * jnp.mean(scaled * unit, axis=-1, keepdims=True)
    )
    return by_values, jnp.sum(grad * unit, axis=0), jnp.sum(grad, axis=0)


def split_three(row):
    first = row.astype(low).astype(wide)
    second = (row - first).astype(low).astype(wide)
    return first, second, row - first - second


def head_rows(part, width, head):
    return pl.ds(pl.multiple_of(part * width + head * HEAD, HEAD), HEAD)


def project_kernel(
    side_ref, tokens_ref, gain_ref, shift_ref, query_ref, key_ref, value_ref, b_ref, tissue_ref,
    qkv_ref, normed_ref, w_ref, bias_ref
):
    normed = normalize(tokens_ref[...].astype(wide), gain_ref[...][None], shift_ref[...][None]).astype(low)
    normed_ref[...] = normed
    width = query_ref.shape[1]
    for part, ref in enumerate((query_ref, key_ref, value_ref)):
        at = slice(part * width, (part + 1) * width)
        turned = ref[...].T
        w_ref[at] = turned
        qkv_ref[at] = (mm(turned, normed, 1, 1) + b_ref[at]).astype(low)
    own = tokens_ref.shape[0]
    bias = jnp.where(tissue_ref[...] > 0, 0.0, masked_score)
    turned = jnp.concatenate([bias[:, own:], bias[:, :own]], axis=1)
    bias = jnp.where(side_ref[0] == 0, bias, turned)
    index = lax.broadcasted_iota(jnp.int32, bias_ref.shape, 0)
    bias_ref[...] = jnp.where(index == 0, bias, 0.0).astype(low)


def project(side, tokens, gain, shift, w_query, w_key, w_value, b, tissue):
    rows, features = tokens.shape
    width = w_query.shape[1]
    vmem = pl.BlockSpec(memory_space=pltpu.VMEM)
    return pl.pallas_call(
        project_kernel,
        name="project_own_rows",
        in_specs=[pl.BlockSpec(memory_space=pltpu.SMEM)] + [vmem] * 8,
        out_specs=[vmem] * 4,
        out_shape=[
            shaped((3 * width, rows), low),
            shaped((rows, features), low),
            shaped((3 * width, features), low),
            shaped((16, tissue.shape[1]), low),
        ],
        compiler_params=params,
        cost_estimate=cost(10**9, 5 * 10**6),
    )(side, tokens, gain, shift, w_query, w_key, w_value, b, tissue)


def attention_forward_kernel(
    own_ref, own_normed_ref, other_ref, gain_ref, shift_ref, w_ref, b_ref, bias_ref,
    qkv_ref, own_context_ref, other_context_ref, exact_ref, log_ref, normed_ref
):
    group = pl.program_id(0)
    own = other_ref.shape[0]
    rows = 2 * own
    width = w_ref.shape[0] // 3

    @pl.when(group == 0)
    def _():
        normed = normalize(other_ref[...].astype(wide), gain_ref[...][None], shift_ref[...][None]).astype(low)
        normed_ref[:own] = own_normed_ref[...]
        normed_ref[own:] = normed
        for part in range(3):
            at = slice(part * width, (part + 1) * width)
            qkv_ref[at, :own] = own_ref[at]
            qkv_ref[at, own:] = (mm(w_ref[at], normed, 1, 1) + b_ref[at]).astype(low)

    index = lax.broadcasted_iota(jnp.int32, (16, rows), 0)
    ones = jnp.where(index == 0, 1.0, 0.0).astype(low)
    for local_head in range(GROUP):
        head = group * GROUP + local_head
        queries = qkv_ref[head_rows(0, width, head)] * jnp.array(HEAD**-0.5, low)
        keys = jnp.concatenate([qkv_ref[head_rows(1, width, head)], bias_ref[...]], axis=0).T
        values = qkv_ref[head_rows(2, width, head)]
        scores = mm(keys, jnp.concatenate([queries, ones], axis=0), 1, 0)
        highest = jnp.max(scores, axis=0, keepdims=True)
        powers = jnp.exp(scores - highest)
        total = jnp.sum(powers, axis=0, keepdims=True)
        log_ref[local_head] = highest + jnp.log(total)
        context = mm(values, powers.astype(low), 1, 0) * (1.0 / total)
        at = slice(local_head * HEAD, (local_head + 1) * HEAD)
        exact_ref[at] = context
        context = context.astype(low)
        own_context_ref[at] = context[:, :own]
        other_context_ref[at] = context[:, own:]


def attention_forward(own, own_normed, other, gain, shift, w, b, bias):
    count, features = other.shape
    width = w.shape[0] // 3
    rows = 2 * count
    by_head = lambda columns: pl.BlockSpec((GROUP * HEAD, columns), lambda group: (group, 0))
    args = (own, own_normed, other, gain, shift, w, b, bias)
    return pl.pallas_call(
        attention_forward_kernel,
        name="attention_forward",
        grid=(width // HEAD // GROUP,),
        in_specs=[whole(a) for a in args],
        out_specs=[
            pl.BlockSpec((3 * width, rows), lambda group: (0, 0)),
            by_head(count),
            by_head(count),
            by_head(rows),
            pl.BlockSpec((GROUP, 1, rows), lambda group: (group, 0, 0)),
            pl.BlockSpec((rows, features), lambda group: (0, 0)),
        ],
        out_shape=[
            stored((3 * width, rows), low),
            shaped((width, count), low),
            shaped((width, count), low),
            stored((width, rows), wide),
            shaped((width // HEAD, 1, rows), wide),
            stored((rows, features), low),
        ],
        compiler_params=params,
        cost_estimate=cost(10 * 10**9, 10**7, 4 * 10**6),
    )(*args)


def attention_backward_kernel(qkv_ref, exact_ref, log_ref, bias_ref, own_grad_ref, other_grad_ref, out_ref):
    rows = qkv_ref.shape[1]
    width = qkv_ref.shape[0] // 3
    scale = HEAD**-0.5
    index = lax.broadcasted_iota(jnp.int32, (16, rows), 0)

    def stack(top, *extra):
        block = jnp.zeros((16, rows), wide)
        for place, row in enumerate(extra):
            block = jnp.where(index == place, row, block)
        return jnp.concatenate([top, block.astype(low)], axis=0)

    bias = bias_ref[0:1].astype(wide)
    for local_head in range(GROUP):
        head = pl.program_id(0) * GROUP + local_head
        at = slice(local_head * HEAD, (local_head + 1) * HEAD)
        queries = qkv_ref[head_rows(0, width, head)] * jnp.array(scale, low)
        keys = qkv_ref[head_rows(1, width, head)]
        values = qkv_ref[head_rows(2, width, head)]
        grads = jnp.concatenate([own_grad_ref[at], other_grad_ref[at]], axis=1)
        overlap = jnp.sum(grads.astype(wide) * exact_ref[at], axis=0, keepdims=True)
        queries_more = stack(queries, 1.0, *split_three(-log_ref[local_head]))
        keys_more = stack(keys, bias, 1.0, 1.0, 1.0).T
        grads_more = stack(grads, *split_three(-overlap))
        values_more = stack(values, 1.0, 1.0, 1.0).T
        chances = jnp.exp(mm(keys_more, queries_more, 1, 0))
        out_ref[head_rows(2, width, head)] = mm(grads, chances.astype(low), 1, 1).astype(low)
        grad_scores = (chances * mm(values_more, grads_more, 1, 0)).astype(low)
        out_ref[head_rows(0, width, head)] = (mm(keys, grad_scores, 1, 0) * scale).astype(low)
        out_ref[head_rows(1, width, head)] = mm(queries, grad_scores, 1, 1).astype(low)


def attention_backward(qkv, exact, logs, bias, own_grad, other_grad, behind, through):
    rows = qkv.shape[1]
    width = qkv.shape[0] // 3
    by_head = lambda columns: pl.BlockSpec((GROUP * HEAD, columns), lambda group: (group, 0))
    return ordered_call(
        attention_backward_kernel,
        (qkv, exact, logs, bias, own_grad, other_grad),
        [
            whole(qkv),
            by_head(rows),
            pl.BlockSpec((GROUP, 1, rows), lambda group: (group, 0, 0)),
            whole(bias),
            by_head(rows // 2),
            by_head(rows // 2),
        ],
        [whole(qkv)],
        [shaped(qkv.shape, low)],
        behind=behind,
        through=through,
        grid=(width // HEAD // GROUP,),
        name="attention_backward",
        cost_estimate=cost(10 * 10**9, 10**7, 4 * 10**6),
    )


def gelu_both(values):
    below = 0.5 * (1.0 + lax.erf(values * (0.5**0.5)))
    density = jnp.exp(values * values * -0.5) * (2.0 * jnp.pi) ** -0.5
    return values * below, below + values * density


def feed_forward_kernel(
    tokens_ref, mine_ref, peer_ref, w_mine_ref, w_peer_ref, b_ref, gain_ref, shift_ref, cotangent_ref,
    up_ref, b_up_ref, down_ref, *refs, other
):
    if other:
        core_ref, *more = refs[:6]
        hidden_ref, grad_normed_ref, branch_ref, grad_b_ref, away_ref, kept_ref, *scratch = refs[6:]
        normed_ref, grad_sum, sum_ = scratch
    else:
        normed_ref, activated_ref, grad_pre_ref, grad_normed_ref, branch_ref, grad_b_ref, grad_sum, sum_ = refs
    step = pl.program_id(0)

    @pl.when(step == 0)
    def _():
        attention = mm(mine_ref[...], w_mine_ref[...], 0, 0) + mm(peer_ref[...], w_peer_ref[...], 0, 0)
        hidden = tokens_ref[...].astype(wide) + (attention + b_ref[...][None])
        normed = normalize(hidden, gain_ref[...][None], shift_ref[...][None]).astype(low)
        normed_ref[...] = normed
        grad_sum[...] = jnp.zeros_like(grad_sum)
        sum_[...] = jnp.zeros_like(sum_)
        if other:
            hidden_ref[...] = hidden

    up, down = up_ref[...], down_ref[...]
    pre_gelu = mm(normed_ref[...], up, 1, 0) + b_up_ref[...]
    grad_active = mm(cotangent_ref[...], down, 1, 1)
    activated, slope = gelu_both(pre_gelu)
    activated = activated.astype(low)
    grad_pre = (grad_active * slope).astype(low)
    sums = jnp.sum(grad_pre.astype(wide), axis=0, keepdims=True)
    grad_sum[...] += mm(grad_pre, up, 1, 1)
    sum_[...] += mm(activated, down, 1, 0)
    if other:
        other_normed_ref, other_cotangent_ref, other_activated_ref, other_grad_pre_ref, other_grad_b_ref = more
        grad_b_ref[...] = sums + other_grad_b_ref[...]
        grad_down = mm(activated, cotangent_ref[...], 0, 0)
        grad_down = (grad_down + mm(other_activated_ref[...], other_cotangent_ref[...], 0, 0)).astype(low)
        grad_up = mm(grad_pre, normed_ref[...], 0, 0)
        grad_up = (grad_up + mm(other_grad_pre_ref[...], other_normed_ref[...], 0, 0)).astype(low)
        is_first = core_ref[0] == 0
        away_ref[...] = jnp.where(is_first, grad_up, grad_down)
        kept_ref[...] = jnp.where(is_first, grad_down, grad_up)
    else:
        grad_b_ref[...] = sums
        activated_ref[...] = activated
        grad_pre_ref[...] = grad_pre

    @pl.when(step == pl.num_programs(0) - 1)
    def _():
        grad_normed_ref[...] = grad_sum[...].astype(low)
        branch_ref[...] = sum_[...].astype(low)


def feed_forward(tokens, mine, peer, w_mine, w_peer, b, gain, shift, cotangent, up, b_up, down, other=()):
    rows, features = tokens.shape
    units = up.shape[1]
    block = BLOCK
    by_rows = pl.BlockSpec((rows, block), lambda step: (0, step))
    by_unit = pl.BlockSpec((1, block), lambda step: (0, step))
    by_up = pl.BlockSpec((features, block), lambda step: (0, step))
    by_down = pl.BlockSpec((block, features), lambda step: (step, 0))
    plain = shaped((rows, features), low)
    scratch = [pltpu.VMEM((rows, features), wide), pltpu.VMEM((rows, features), wide)]
    if other:
        out_specs = [whole(tokens)] * 3 + [by_unit, by_down, by_down]
        out_shape = [stored((rows, features), wide), plain, stored((rows, features), low), shaped((1, units), wide)]
        out_shape += [stored((units, features), low)] * 2
        scratch = [pltpu.VMEM((rows, features), low)] + scratch
    else:
        out_specs = [whole(tokens), by_rows, by_rows, whole(tokens), whole(tokens), by_unit]
        out_shape = [plain, shaped((rows, units), low), shaped((rows, units), low), plain]
        out_shape += [stored((rows, features), low)]
        out_shape += [shaped((1, units), wide)]
    return pl.pallas_call(
        functools.partial(feed_forward_kernel, other=bool(other)),
        name="feed_forward",
        grid=(units // block,),
        in_specs=[whole(a) for a in (tokens, mine, peer, w_mine, w_peer, b, gain, shift, cotangent)]
        + [by_up, by_unit, by_down]
        + (
            [pl.BlockSpec(memory_space=pltpu.SMEM), whole(other[1]), whole(other[2]), by_rows, by_rows, by_unit]
            if other
            else []
        ),
        out_specs=out_specs,
        out_shape=out_shape,
        scratch_shapes=scratch,
        compiler_params=params,
        cost_estimate=cost(5 * 10**9, 10**7, 10**6),
    )(tokens, mine, peer, w_mine, w_peer, b, gain, shift, cotangent, up, b_up, down, *other)


def middle_kernel(
    part_ref, came_ref, hidden_ref, cotangent_ref, gain_ref, w_mine_ref, w_peer_ref,
    grad_hidden_ref, branch_ref, mine_ref, peer_ref, sums_ref
):
    grad = part_ref[...].astype(wide) + came_ref[...].astype(wide)
    cotangent = cotangent_ref[...].astype(wide)
    by_hidden, by_gain, by_shift = normalize_back(hidden_ref[...], gain_ref[...][None], grad)
    grad_hidden = by_hidden + cotangent
    grad_hidden_ref[...] = grad_hidden
    branch = grad_hidden.astype(low)
    branch_ref[...] = branch
    mine_ref[...] = mm(w_mine_ref[...], branch, 1, 1).astype(low)
    peer_ref[...] = mm(w_peer_ref[...], branch, 1, 1).astype(low)
    sums_ref[...] = jnp.zeros_like(sums_ref)
    sums_ref[0:1] = jnp.sum(branch.astype(wide), axis=0, keepdims=True)
    sums_ref[1:2] = by_gain[None]
    sums_ref[2:3] = by_shift[None]
    sums_ref[3:4] = jnp.sum(cotangent, axis=0, keepdims=True)


def middle(part, came, hidden, cotangent, gain, w_mine, w_peer, through):
    rows, features = part.shape
    width = w_mine.shape[0]
    vmem = pl.BlockSpec(memory_space=pltpu.VMEM)
    return ordered_call(
        middle_kernel,
        (part, came, hidden, cotangent, gain, w_mine, w_peer),
        [vmem] * 7,
        [vmem] * 5,
        [
            stored((rows, features), wide),
            stored((rows, features), low),
            stored((width, rows), low),
            stored((width, rows), low),
            shaped((8, features), wide),
        ],
        through=through,
        name="second_norm_backward",
        cost_estimate=cost(10**9, 5 * 10**6),
    )


def last_kernel(
    part_ref, came_ref, tokens_ref, grad_hidden_ref, gain_ref, b_ref, hidden_ref, branch_ref, branch_came_ref,
    out_ref, sums_ref, output_ref
):
    grad = part_ref[...].astype(wide) + came_ref[...].astype(wide)
    by_tokens, by_gain, by_shift = normalize_back(tokens_ref[...].astype(wide), gain_ref[...][None], grad)
    out_ref[...] = grad_hidden_ref[...] + by_tokens
    sums_ref[...] = jnp.zeros_like(sums_ref)
    sums_ref[0:1] = by_gain[None]
    sums_ref[1:2] = by_shift[None]
    branch = branch_ref[...].astype(wide) + branch_came_ref[...].astype(wide)
    output_ref[...] = (hidden_ref[...] + (branch + b_ref[...][None])).astype(low)


def last(part, came, tokens, grad_hidden, gain, b, hidden, branch, branch_came, behind, through):
    rows, features = part.shape
    vmem = pl.BlockSpec(memory_space=pltpu.VMEM)
    return ordered_call(
        last_kernel,
        (part, came, tokens, grad_hidden, gain, b, hidden, branch, branch_came),
        [vmem] * 9,
        [vmem] * 3,
        [shaped((rows, features), wide), shaped((8, features), wide), shaped((rows, features), low)],
        behind=behind,
        through=through,
        name="first_norm_backward",
        cost_estimate=cost(10**8, 5 * 10**6),
    )


def by_inputs_kernel(grads_ref, w_ref, own_ref, other_ref, sums_ref):
    own = own_ref.shape[0]
    grads = grads_ref[...]
    other_ref[...] = mm(grads[:, own:], w_ref[...], 0, 0).astype(low)
    own_ref[...] = mm(grads[:, :own], w_ref[...], 0, 0).astype(low)
    sums_ref[...] = mm(jnp.ones((8, grads.shape[1]), low), grads, 1, 1)


def by_inputs(grads, w, behind, through):
    rows, features = grads.shape[1] // 2, w.shape[1]
    vmem = pl.BlockSpec(memory_space=pltpu.VMEM)
    return ordered_call(
        by_inputs_kernel,
        (grads, w),
        [vmem] * 2,
        [vmem] * 3,
        [
            stored((rows, features), low),
            stored((rows, features), low),
            shaped((8, grads.shape[0]), wide),
        ],
        behind=behind,
        through=through,
        name="first_normed_gradient",
        cost_estimate=cost(2 * 10**9, 5 * 10**6),
    )


def tail_gradient_kernel(
    core_ref, grads_ref, normed_ref, own_context_ref, own_branch_ref, other_context_ref, other_branch_ref,
    away_ref, kept_ref
):
    step = pl.program_id(0)
    block = tail_block(step, core_ref[0])

    def put(total):
        @pl.when(step < 2)
        def _():
            away_ref[...] = total.astype(low)

        @pl.when(step >= 2)
        def _():
            kept_ref[...] = total

    @pl.when(block < 3)
    def _():
        put(mm(grads_ref[...], normed_ref[...], 1, 0))

    @pl.when(block == 3)
    def _():
        put(
            mm(own_context_ref[...], own_branch_ref[...], 1, 0)
            + mm(other_context_ref[...], other_branch_ref[...], 1, 0)
        )


def tail_block(step, core):
    side = jnp.where(step < 2, 1 - core, core)
    return side * 2 + (step & 1)


def tail_gradient(core, grads, normed, own_context, own_branch, other_context, other_branch, behind):
    width, features = own_context.shape[0], normed.shape[1]
    rest = (normed, own_context, own_branch, other_context, other_branch)
    return ordered_call(
        tail_gradient_kernel,
        (core, grads, *rest),
        [
            pl.BlockSpec(
                (width, grads.shape[1]),
                lambda step, core_ref: (jnp.minimum(tail_block(step, core_ref[0]), 2), 0),
            )
        ]
        + [whole(a) for a in rest],
        [
            pl.BlockSpec((width, features), lambda step, _: (jnp.minimum(step, 1), 0)),
            pl.BlockSpec((width, features), lambda step, _: (jnp.maximum(step - 2, 0), 0)),
        ],
        [stored((2 * width, features), low), stored((2 * width, features), wide)],
        behind=behind,
        prefetch=1,
        grid=(4,),
        name="tail_gradient",
        cost_estimate=cost(2 * 10**9, 10**7),
    )[0]


def after(value, *others):
    return lax.optimization_barrier((value, *others))[0]


def swap_mp(value):
    return lax.ppermute(value, "mp", [(0, 1), (1, 0)])


def swap_dp(value, mask, count):
    return lax.ppermute(value, "dp", [(i, i ^ mask) for i in range(count)])


def rows_at(value, at, rows):
    return lax.dynamic_slice_in_dim(value, at * rows, rows, 0)


def rows_set(value, block, at):
    return lax.dynamic_update_slice_in_dim(value, block, at * block.shape[0], 0)


class Sum:
    def __init__(self, kept, came, place, count):
        self.count, self.rows = count, kept.shape[0]
        self.terms, self.came = [(kept, 0)], came
        self.core, chip = place & 1, place >> 1
        bits = (count // 2).bit_length() - 1
        self.orders = [(k, (k + 1) % bits) for k in range(bits)]
        self.bits = [(chip >> jnp.where(self.core == 0, a, b)) & 1 for a, b in self.orders]
        self.sums = None

    def swap(self, value, step):
        partner = lambda i: i ^ (2 << self.orders[step][i & 1])
        return lax.ppermute(value, "dp", [(i, partner(i)) for i in range(self.count)])

    def rows_of(self, shift, rows):
        total = 0.0
        for array, start in self.terms:
            total = total + lax.dynamic_slice_in_dim(array, start + shift, rows, 0).astype(wide)
        return total.astype(low)

    def scatter(self, step):
        self.terms.append((self.came, 0))
        self.rows //= 2
        sent = self.rows_of((1 - self.bits[step]) * self.rows, self.rows)
        self.came = self.swap(sent, step)
        self.terms = [(array, start + self.bits[step] * self.rows) for array, start in self.terms]
        return sent

    def turn(self, sums=None):
        self.terms.append((self.came, 0))
        self.block = self.rows_of(0, self.rows)
        self.sums = sums
        return self.send(len(self.orders) - 1)

    def send(self, step):
        sent = self.block if self.sums is None else jnp.concatenate([pack_rows(self.sums), self.block], axis=0)
        self.came = self.swap(sent, step) if step >= 0 else swap_dp(sent, 1, self.count)
        return sent

    def gather(self, step):
        came = self.came
        extra = came.shape[0] - self.block.shape[0]
        if extra:
            self.sums = self.sums + widen(came[:extra])
        mine, other = self.block, came[extra:]
        self.block = jnp.where(
            self.bits[step] == 0,
            jnp.concatenate([mine, other], axis=0),
            jnp.concatenate([other, mine], axis=0),
        )
        return self.send(step - 1)


def widen(pair):
    rows = pair.shape[0] // 2
    return pair[:rows].astype(wide) + pair[rows:].astype(wide)


def pack_rows(rows):
    top = lax.reduce_precision(rows, exponent_bits=8, mantissa_bits=7)
    return jnp.concatenate([top, rows - top], axis=0).astype(low)


def up_down_finish_kernel(core_ref, mine_ref, other_ref, up_ref, down_ref):
    for core in range(2):

        @pl.when(core_ref[0] == core)
        def _():
            down, up = (mine_ref, other_ref) if core == 0 else (other_ref, mine_ref)
            down_ref[...] = down[...].astype(wide)
            up_ref[...] = up[...].astype(wide).T


def up_down_finish(core, mine, other):
    units, features = mine.shape
    block = 256
    by_unit = pl.BlockSpec((block, features), lambda step: (step, 0))
    return pl.pallas_call(
        up_down_finish_kernel,
        name="up_down_finish",
        grid=(units // block,),
        in_specs=[pl.BlockSpec(memory_space=pltpu.SMEM), by_unit, by_unit],
        out_specs=[pl.BlockSpec((features, block), lambda step: (0, step)), by_unit],
        out_shape=[shaped((features, units), wide), shaped((units, features), wide)],
        compiler_params=params,
        cost_estimate=cost(10**6, 10**7),
    )(core, mine, other)


def tail_finish_kernel(core_ref, half_ref, came_ref, small_ref, *refs):
    extra = came_ref.shape[0] - half_ref.shape[0]
    rows = extra // 2
    small = small_ref[...] + (came_ref[:rows].astype(wide) + came_ref[rows:extra].astype(wide))
    columns = small.shape[1]
    for row in range(6):
        refs[4 + row][...] = small[row]
    refs[10][...] = small[6, : columns // 2]
    refs[11][...] = small[6, columns // 2 :]
    refs[12][:columns] = small[7]
    refs[12][columns:] = small[8]
    for core in range(2):

        @pl.when(core_ref[0] == core)
        def _():
            width = half_ref.shape[0] // 2
            mine, other = (half_ref, 0), (came_ref, extra)
            (first, at), (second, to) = (mine, other) if core == 0 else (other, mine)
            refs[0][...] = first[at : at + width].astype(wide).T
            refs[1][...] = first[at + width : at + 2 * width].astype(wide).T
            refs[2][...] = second[to : to + width].astype(wide).T
            refs[3][...] = second[to + width : to + 2 * width].astype(wide)


def tail_finish(core, half, came, small):
    rows, features = half.shape
    width = rows // 2
    vmem = pl.BlockSpec(memory_space=pltpu.VMEM)
    vectors = [features] * 6 + [features // 2] * 2 + [2 * features]
    return pl.pallas_call(
        tail_finish_kernel,
        name="tail_finish",
        in_specs=[pl.BlockSpec(memory_space=pltpu.SMEM), vmem, vmem, vmem],
        out_specs=[vmem] * 13,
        out_shape=[shaped((features, width), wide)] * 3
        + [shaped((width, features), wide)]
        + [shaped((n,), wide) for n in vectors],
        compiler_params=params,
        cost_estimate=cost(10**6, 10**7),
    )(core, half, came, small)


def local(
    count,
    tokens,
    tissue,
    first_gain,
    first_shift,
    w_query,
    b_query,
    w_key,
    w_value,
    b_value,
    w_output,
    b_output,
    second_gain,
    second_shift,
    w_upward,
    b_upward,
    w_down,
    b_down,
    cotangent,
):
    place, side = lax.axis_index("dp"), lax.axis_index("mp")
    core = place & 1
    core_list = core.reshape(1)
    own = tokens.shape[0]
    width = w_query.shape[1]
    tokens_other = swap_mp(tokens)
    half_width = width // 2
    w_half = swap_mp(after(rows_at(w_output, core, half_width), tokens_other))
    cotangent_other = swap_mp(after(cotangent, tokens_other))
    b_stack = jnp.concatenate([b_query, jnp.zeros_like(b_query), b_value])[:, None]
    own_qkv, own_normed, w_stack, bias = project(
        side.reshape(1), tokens, first_gain, first_shift, w_query, w_key, w_value, b_stack, tissue
    )

    qkv, own_context, other_context, exact, logs, normed1 = attention_forward(
        own_qkv, own_normed, after(tokens_other, own_qkv), first_gain, first_shift, w_stack, b_stack, bias
    )
    w_traded = swap_dp(after(w_half, own_context), 1, count)
    w_peer = jnp.where(
        core == 0,
        jnp.concatenate([w_half, w_traded], axis=0),
        jnp.concatenate([w_traded, w_half], axis=0),
    )
    peer_other = swap_mp(own_context)
    peer_own = swap_mp(after(other_context, peer_other))
    b_up = b_upward[None]
    shared = (far(w_upward), b_up, far(w_down))
    second = (b_output, second_gain, second_shift)
    normed_b, active_b, pre_b, part_b, branch_b, sum_b = feed_forward(
        tokens_other, other_context, peer_other, w_output, w_peer, *second, cotangent_other, *shared
    )
    came = swap_mp(part_b)
    hidden, part_a, branch_a, grad_bupward, up_down_away, up_down_kept = feed_forward(
        after(tokens, part_b), own_context, peer_own, w_output, w_peer, *second, cotangent, *shared,
        other=(core_list, normed_b, cotangent_other, active_b, pre_b, sum_b),
    )
    (grad_hidden, grad_branch, mine_own, peer_grad, sums), (up_down_away,) = middle(
        part_a, came, hidden, cotangent, second_gain, w_output, w_peer, through=(up_down_away,)
    )
    up_down = Sum(up_down_kept, swap_dp(up_down_away, 1, count), place, count)
    mine_other = swap_mp(peer_grad)
    branch_other = swap_mp(after(grad_branch, mine_other))
    step = up_down.scatter(0)
    (grads,), (branch_b, *arrays) = attention_backward(
        far(qkv), far(exact), logs, bias, mine_own, mine_other, behind=(step,), through=(branch_b, up_down.terms[0][0])
    )
    up_down.terms[0] = (arrays[0], up_down.terms[0][1])
    branch_came = swap_mp(branch_b)
    steps = len(up_down.orders)
    step = up_down.scatter(1)
    away, kept = tail_gradient(
        core_list, grads, normed1, own_context, grad_branch, other_context, branch_other, behind=(step,)
    )
    (first_a, first_b, stack_sums), (kept,) = by_inputs(grads, far(w_stack), behind=(away,), through=(kept,))
    tail = Sum(kept, swap_dp(away, 1, count), place, count)
    came = swap_mp(first_b)
    tail.scatter(0)
    for k in range(2, steps):
        up_down.scatter(k)
        step = tail.scatter(k - 1)
    (grad_tokens, sums_first, output), (kept,) = last(
        first_a, came, tokens, grad_hidden, first_gain, b_down, hidden, branch_a, branch_came,
        behind=(step,), through=(tail.terms[0][0],),
    )
    tail.terms[0] = (kept, tail.terms[0][1])
    tail.scatter(steps - 1)
    up_down.turn()
    small = jnp.concatenate([sums_first[:2], sums[:4]], axis=0)
    small = small + swap_mp(small)
    columns = small.shape[1]
    split = jnp.concatenate([stack_sums[0, :width], stack_sums[0, 2 * width :], grad_bupward[0]])
    small = jnp.concatenate([small, split.reshape(-1, columns)], axis=0)
    small = jnp.pad(small, ((0, -small.shape[0] % 4), (0, 0)))
    up_down.gather(steps - 1)
    tail.turn(sums=small)
    for k in range(steps - 1, 0, -1):
        tail.gather(k)
        up_down.gather(k - 1)
    tail.gather(0)
    grad_wquery, grad_wkey, grad_wvalue, grad_woutput, *small = tail_finish(
        core_list, tail.block, tail.came, tail.sums
    )
    grad_upward, grad_down = up_down_finish(core_list, up_down.block, up_down.came)
    return (
        output,
        grad_tokens,
        small[0],
        small[1],
        grad_wquery,
        small[6],
        grad_wkey,
        grad_wvalue,
        small[7],
        grad_woutput,
        small[2],
        small[3],
        small[4],
        grad_upward,
        small[8],
        grad_down,
        small[5],
    )


def solution(mesh):
    in_specs = (
        P(("dp", "mp"), None),
        P("dp", None),
        P(),
        P(),
        P(None, "mp"),
        P("mp"),
        P(None, "mp"),
        P(None, "mp"),
        P("mp"),
        P("mp", None),
        P(),
        P(),
        P(),
        P(None, "mp"),
        P("mp"),
        P("mp", None),
        P(),
        P(("dp", "mp"), None),
    )
    out_specs = (
        P(("dp", "mp"), None),
        P(("dp", "mp"), None),
        P(),
        P(),
        P(None, "mp"),
        P("mp"),
        P(None, "mp"),
        P(None, "mp"),
        P("mp"),
        P("mp", None),
        P(),
        P(),
        P(),
        P(None, "mp"),
        P("mp"),
        P("mp", None),
        P(),
    )
    return jax.shard_map(
        functools.partial(local, mesh.shape["dp"]), mesh=mesh, in_specs=in_specs, out_specs=out_specs, check_vma=False)
```

time: 241 us -> 236 us (0.979)
  waiting for transfers between devices: 100 us -> 80.4 us
  between operations: 14.9 us -> 1.23 us
  local copies, waits for them, and re-layouts: 13.4 us -> 26.5 us
  starting transfers between devices: 20.7 us -> 30.3 us
  other arithmetic: 14.1 us -> 22.8 us
  Pallas kernels: 77.2 us -> 73.3 us
    ppermute x9 -> x5, waiting for transfers between devices: 62.2 us -> 5.99 us  [swap_dp(): return lax.ppermute(value, 'dp', [(i, i ^ mask) for i in range(count)])]
    ppermute x0 -> x12, waiting for transfers between devices: none -> 50.3 us  [swap(): lax.ppermute(value, 'dp', [(i, partner(i)) for i in range(self.count)])]
    unnamed x44 -> x114, local copies, waits for them, and re-layouts: 7.95 us -> 26.2 us
    ppermute x0 -> x12, starting transfers between devices: none -> 15.2 us  [swap(): lax.ppermute(value, 'dp', [(i, partner(i)) for i in range(self.count)])]
    ppermute x11, waiting for transfers between devices: 38 us -> 24.2 us  [swap_mp(): return lax.ppermute(value, 'mp', [(0, 1), (1, 0)])]
    select_n x3 -> x6, other arithmetic: 0.7 us -> 6.83 us  [gather(): jnp.where(self.bits[step] == 0, jnp.concatenate([mine, other], axis=0), j...]
    convert_element_type x3 -> x8, other arithmetic: 7.22 us -> 12.8 us  [rows_of(): return total.astype(low)]
    ppermute x9 -> x5, starting transfers between devices: 6.14 us -> 0.79 us  [swap_dp(): return lax.ppermute(value, 'dp', [(i, i ^ mask) for i in range(count)])]
  transfers between devices with their start and end apart: 21 -> 28, of which waited for: 12 -> 15; matrix products, arithmetic and copies ran while one was open for 4% -> 10% of each run, Pallas kernels for 31% -> 26%
where the time goes in v3:
time: 236 us; the launch traced here: 234 us
  waiting for transfers between devices  80.4 us (34%)
  Pallas kernels  73.3 us (31%)
  starting transfers between devices  30.3 us (13%)
  local copies, waits for them, and re-layouts  26.5 us (11%)
  other arithmetic  22.8 us (10%)
    ppermute x12, waiting for transfers between devices, swap(): lax.ppermute(value, 'dp', [(i, partner(i)) for i in range(self.count)])  50.3 us
    pallas_call x5, Pallas kernels, ordered_call(): pl.pallas_call(body, grid_spec=pltpu.PrefetchScalarGridSpec(num_scalar_pr...  29.6 us
    unnamed x114, local copies, waits for them, and re-layouts  26.2 us
    ppermute x11, waiting for transfers between devices, swap_mp(): return lax.ppermute(value, 'mp', [(0, 1), (1, 0)])  24.2 us
    pallas_call x2, Pallas kernels, feed_forward(): pl.pallas_call(functools.partial(feed_forward_kernel, other=bool(other)),...  23.8 us
    ppermute x12, starting transfers between devices, swap(): lax.ppermute(value, 'dp', [(i, partner(i)) for i in range(self.count)])  15.2 us
    ppermute x11, starting transfers between devices, swap_mp(): return lax.ppermute(value, 'mp', [(0, 1), (1, 0)])  14.3 us
    convert_element_type x8, other arithmetic, rows_of(): return total.astype(low)  12.8 us
  transfers between devices with their start and end apart: 28, of which 15 were waited for; matrix products, arithmetic and copies ran while one was open for 10% of the time, Pallas kernels for 26%

profile of v3, /device:TPU:0, one launch (start us, length us, event | category | flops | bytes accessed | tf_op | source)
XLA Modules:
  0.0 234.5 jit_solution(538036302051068668)
XLA Ops:
  0.7 3.0 %collective-permute-start = (bf16[392,768]{1,0:T(8,128)(2,1)}, bf16[392,768]{1,0:T(8,128)(2,1)}, u32[]{:S(2)}, u32[]{:S(2)}) collective-permute-start(bf16[392,768]{1,0:T(8,128)(2,1)} %refs_2_.1), channel_id=1, source_target_pairs={{0,1},{1,0},{2,3},{3,2},{4,5},{5,4},{6,7},{7,6},{8,9},{9,8},{10,11... | collective-permute-start | bytes 1806344 | tf_op jit(solution)/shard_map/ppermute | solution.py:533
  12.5 5.1 %collective-permute-done.other_ref.tokens_ref = bf16[392,768]{1,0:T(8,128)(2,1)} collective-permute-done((bf16[392,768]{1,0:T(8,128)(2,1)}, bf16[392,768]{1,0:T(8,128)(2,1)}, u32[]{:S(2)}, u32[]{:S(2)}) %collective-permute-start) | collective-permute-done | bytes 602144 | tf_op jit(solution)/shard_map/ppermute | solution.py:533
  19.6 11.1 %attention_forward.1 = (bf16[1152,784]{1,0:T(8,128)(2,1)}, bf16[384,392]{1,0:T(8,128)(2,1)S(1)}, bf16[384,392]{1,0:T(8,128)(2,1)S(1)}, f32[384,784]{1,0:T(8,128)...) custom-call(bf16[1152,392]{1,0:T(8,128)(2,1)S(1)} %get-tuple-element.80.own_ref, ...), custom_call_target="tpu_custom_call" | custom-call | flops 10000000000 | bytes 10000000 | tf_op jit(solution)/shard_map/attention_forward/pallas_call | solution.py:188
  33.9 13.2 %collective-permute-done.1.peer_ref = bf16[384,392]{1,0:T(8,128)(2,1)S(1)} collective-permute-done((bf16[384,392]{1,0:T(8,128)(2,1)S(1)}, bf16[384,392]{1,0:T(8,128)(2,1)S(1)}, u32[]{:S(2)}, u32[]{:S(2)}) %collective-permute-start.1) | collective-permute-done | bytes 301088 | tf_op jit(solution)/shard_map/ppermute | solution.py:533
  52.7 8.9 %feed_forward.2 = (bf16[392,768]{1,0:T(8,128)(2,1)S(1)}, bf16[392,1536]{1,0:T(8,128)(2,1)S(1)}, bf16[392,1536]{1,0:T(8,128)(2,1)S(1)}, bf16[392,768]{1,0:T(8,128...) custom-call(bf16[392,768]{1,0:T(8,128)(2,1)} %collective-permute-done.other_ref.tokens_ref, ...), custom_call_target="tpu_custom_call" | custom-call | flops 5000000000 | bytes 10000000 | tf_op jit(solution)/shard_map/feed_forward/pallas_call | solution.py:350
  62.2 14.9 %feed_forward.3 = (f32[392,768]{1,0:T(8,128)}, bf16[392,768]{1,0:T(8,128)(2,1)S(1)}, bf16[392,768]{1,0:T(8,128)(2,1)}, f32[1,1536]{1,0:T(1,128)S(1)}, bf16[1536,...) custom-call(bf16[392,768]{1,0:T(8,128)(2,1)S(1)} %copy-done.9, bf16[384,392]{1,0:T(8,128)(2,1)S(1)} %copy-done.28, ...), custom_call_target="tpu_custom_call" | custom-call | flops 5000000000 | bytes 10000000 | tf_op jit(solution)/shard_map/feed_forward/pallas_call | solution.py:350
  78.4 2.8 %second_norm_backward.1 = (f32[392,768]{1,0:T(8,128)}, bf16[392,768]{1,0:T(8,128)(2,1)}, bf16[384,392]{1,0:T(8,128)(2,1)}, bf16[384,392]{1,0:T(8,128)(2,1)}, f32...) custom-call(bf16[392,768]{1,0:T(8,128)(2,1)S(1)} %get-tuple-element.100.refs_0_, ...), custom_call_target="tpu_custom_call", output_to_operand_aliasing={{5}: (7, {})} | custom-call | flops 1000000000 | bytes 5000000 | tf_op jit(solution)/shard_map/second_norm_backward/pallas_call | solution.py:47
  83.2 3.5 %collective-permute-done.8 = bf16[1536,768]{1,0:T(8,128)(2,1)} collective-permute-done((bf16[1536,768]{1,0:T(8,128)(2,1)}, bf16[1536,768]{1,0:T(8,128)(2,1)}, u32[]{:S(2)}, u32[]{:S(2)}) %collective-permute-start.8) | collective-permute-done | bytes 2359328 | tf_op jit(solution)/shard_map/ppermute | solution.py:537
  89.7 4.0 %collective-permute-done.7.refs_5_ = bf16[384,392]{1,0:T(8,128)(2,1)} collective-permute-done((bf16[384,392]{1,0:T(8,128)(2,1)}, bf16[384,392]{1,0:T(8,128)(2,1)}, u32[]{:S(2)}, u32[]{:S(2)}) %collective-permute-start.7) | collective-permute-done | bytes 301088 | tf_op jit(solution)/shard_map/ppermute | solution.py:533
  97.5 13.7 %attention_backward.1 = (bf16[1152,784]{1,0:T(8,128)(2,1)S(1)}, bf16[392,768]{1,0:T(8,128)(2,1)}, bf16[1536,768]{1,0:T(8,128)(2,1)S(1)}) custom-call(bf16[1152,784]{1,0:T(8,128)(2,1)} %get-tuple-element.85.refs_0_, f32[384,784]{1,0:T(8,128)} %get-tuple-element.86.refs_1_, f32[6,1,784]{2,1,0:T(1,128)S(1)} %copy-done.48, ...), custom_call_target="tpu_custom_call", output_to_operand_aliasing={{1}: (7, {}), {2}: (8, {})} | custom-call | flops 10000000000 | bytes 10000000 | tf_op jit(solution)/shard_map/attention_backward/pallas_call | solution.py:47
  113.7 4.7 %tail_gradient.1 = (bf16[768,768]{1,0:T(8,128)(2,1)}, f32[768,768]{1,0:T(8,128)}) custom-call(s32[1]{0:T(128)} %bitcast.1.refs_0_.core_ref, bf16[1152,784]{1,0:T(8,128)(2,1)S(1)} %get-tuple-element.108.refs_1_.refs_0_, bf16[784,768]{1,0:T(8,128)(2,1)S(1)} %copy-done.44, bf16[384,392]{1,0:T(8,128)(2,1)S(1)} %copy-done.29, bf16[392,768]{1,0:T(8,128)(2,1)S(1)} %copy-done.23, ...), custom_call_target="tpu_custom_call" | custom-call | flops 2000000000 | bytes 10000000 | tf_op jit(solution)/shard_map/tail_gradient/pallas_call | solution.py:47
  124.6 4.8 %first_normed_gradient.1 = (bf16[392,768]{1,0:T(8,128)(2,1)}, bf16[392,768]{1,0:T(8,128)(2,1)}, f32[8,1152]{1,0:T(8,128)S(1)}, f32[768,768]{1,0:T(8,128)S(1)}) custom-call(bf16[1152,784]{1,0:T(8,128)(2,1)S(1)} %copy-done.42, bf16[1152,768]{1,0:T(8,128)(2,1)} %copy-done.43, bf16[768,768]{1,0:T(8,128)(2,1)S(1)} %copy-done.22, ...), custom_call_target="tpu_custom_call", output_to_operand_aliasing={{3}: (3, {})} | custom-call | flops 2000000000 | bytes 5000000 | tf_op jit(solution)/shard_map/first_normed_gradient/pallas_call | solution.py:47
  129.4 5.4 %collective-permute-done.22 = bf16[384,768]{1,0:T(8,128)(2,1)} collective-permute-done((bf16[384,768]{1,0:T(8,128)(2,1)S(1)}, bf16[384,768]{1,0:T(8,128)(2,1)}, u32[]{:S(2)}, u32[]{:S(2)}) %collective-permute-start.22) | collective-permute-done | bytes 589856 | tf_op jit(solution)/shard_map/ppermute | solution.py:560
  143.7 3.2 %collective-permute-done.23 = bf16[192,768]{1,0:T(8,128)(2,1)S(1)} collective-permute-done((bf16[192,768]{1,0:T(8,128)(2,1)S(1)}, bf16[192,768]{1,0:T(8,128)(2,1)S(1)}, u32[]{:S(2)}, u32[]{:S(2)}) %collective-permute-start.23) | collective-permute-done | bytes 294944 | tf_op jit(solution)/shard_map/ppermute | solution.py:560
  149.3 4.2 %collective-permute-done.14 = bf16[384,768]{1,0:T(8,128)(2,1)} collective-permute-done((bf16[384,768]{1,0:T(8,128)(2,1)}, bf16[384,768]{1,0:T(8,128)(2,1)}, u32[]{:S(2)}, u32[]{:S(2)}) %collective-permute-start.14) | collective-permute-done | bytes 589856 | tf_op jit(solution)/shard_map/ppermute | solution.py:560
  156.7 16.0 %collective-permute-done.24 = bf16[192,768]{1,0:T(8,128)(2,1)} collective-permute-done((bf16[192,768]{1,0:T(8,128)(2,1)}, bf16[192,768]{1,0:T(8,128)(2,1)}, u32[]{:S(2)}, u32[]{:S(2)}) %collective-permute-start.24) | collective-permute-done | bytes 294944 | tf_op jit(solution)/shard_map/ppermute | solution.py:560
  179.6 3.6 %first_norm_backward.1 = (f32[392,768]{1,0:T(8,128)}, f32[8,768]{1,0:T(8,128)S(1)}, bf16[392,768]{1,0:T(8,128)(2,1)}, f32[768,768]{1,0:T(8,128)S(1)}) custom-call(bf16[392,768]{1,0:T(8,128)(2,1)S(1)} %copy-done.12, bf16[392,768]{1,0:T(8,128)(2,1)} %collective-permute-done.11.refs_1_, ...), custom_call_target="tpu_custom_call", output_to_operand_aliasing={{3}: (10, {})} | custom-call | flops 100000000 | bytes 5000000 | tf_op jit(solution)/shard_map/first_norm_backward/pallas_call | solution.py:47
  187.8 5.0 %collective-permute-done.16 = bf16[96,768]{1,0:T(8,128)(2,1)S(1)} collective-permute-done((bf16[96,768]{1,0:T(8,128)(2,1)S(1)}, bf16[96,768]{1,0:T(8,128)(2,1)S(1)}, u32[]{:S(2)}, u32[]{:S(2)}) %collective-permute-start.16) | collective-permute-done | bytes 147488 | tf_op jit(solution)/shard_map/ppermute | solution.py:560
  196.8 4.0 %collective-permute-start.26 = (bf16[768,768]{1,0:T(8,128)(2,1)S(1)}, bf16[768,768]{1,0:T(8,128)(2,1)}, u32[]{:S(2)}, u32[]{:S(2)}) collective-permute-start(bf16[768,768]{1,0:T(8,128)(2,1)S(1)} %maximum_select_fusion.2), channel_id=1, source_target_pairs={{0,4},{2,10},{4,0},{6,14},{8,12},{10,2},{12,8},{14,6},{16,20},{18,... | collective-permute-start | bytes 3538952 | tf_op jit(solution)/shard_map/ppermute | solution.py:560
  203.8 7.4 %collective-permute-done.19 = bf16[216,768]{1,0:T(8,128)(2,1)S(1)} collective-permute-done((bf16[216,768]{1,0:T(8,128)(2,1)S(1)}, bf16[216,768]{1,0:T(8,128)(2,1)S(1)}, u32[]{:S(2)}, u32[]{:S(2)}) %collective-permute-start.19) | collective-permute-done | bytes 331808 | tf_op jit(solution)/shard_map/ppermute | solution.py:560
  217.2 5.0 %collective-permute-done.20 = bf16[408,768]{1,0:T(8,128)(2,1)S(1)} collective-permute-done((bf16[408,768]{1,0:T(8,128)(2,1)S(1)}, bf16[408,768]{1,0:T(8,128)(2,1)S(1)}, u32[]{:S(2)}, u32[]{:S(2)}) %collective-permute-start.20) | collective-permute-done | bytes 626720 | tf_op jit(solution)/shard_map/ppermute | solution.py:560
  224.7 2.5 %collective-permute-done.21.came_ref = bf16[792,768]{1,0:T(8,128)(2,1)S(1)} collective-permute-done((bf16[792,768]{1,0:T(8,128)(2,1)S(1)}, bf16[792,768]{1,0:T(8,128)(2,1)S(1)}, u32[]{:S(2)}, u32[]{:S(2)}) %collective-permute-start.21) | collective-permute-done | bytes 1216544 | tf_op jit(solution)/shard_map/ppermute | solution.py:537
  227.2 2.8 %tail_finish.1 = (f32[768,384]{1,0:T(8,128)}, f32[768,384]{1,0:T(8,128)}, f32[768,384]{1,0:T(8,128)}, f32[384,768]{1,0:T(8,128)}, f32[768]{0:T(1024)}, /*index=5...) custom-call(s32[1]{0:T(128)} %bitcast.1.refs_0_.core_ref, ...), custom_call_target="tpu_custom_call" | custom-call | flops 1000000 | bytes 10000000 | tf_op jit(solution)/shard_map/tail_finish/pallas_call | solution.py:666
  230.0 4.5 %up_down_finish.1 = (f32[768,1536]{1,0:T(8,128)}, f32[1536,768]{1,0:T(8,128)}) custom-call(s32[1]{0:T(128)} %bitcast.1.refs_0_.core_ref, bf16[1536,768]{1,0:T(8,128)(2,1)S(1)} %maximum_select_fusion.mine_ref, bf16[1536,768]{1,0:T(8,128)(2,1)S(1)} %collective-permute-done.27.other_ref), custom_call_target="tpu_custom_call" | custom-call | flops 1000000 | bytes 10000000 | tf_op jit(solution)/shard_map/up_down_finish/pallas_call | solution.py:625
  (198 shorter events, 79.9 us)
Async XLA Ops:
  0.7 16.9 %collective-permute-start = (bf16[392,768]{1,0:T(8,128)(2,1)}, bf16[392,768]{1,0:T(8,128)(2,1)}, u32[]{:S(2)}, u32[]{:S(2)}) collective-permute-start(bf16[392,768]{1,0:T(8,128)(2,1)} %refs_2_.1), channel_id=1, source_target_pairs={{0,1},{1,0},{2,3},{3,2},{4,5},{5,4},{6,7},{7,6},{8,9},{9,8},{10,11... | collective-permute-start | bytes 1806344 | tf_op jit(solution)/shard_map/ppermute | solution.py:533
  17.6 16.3 %collective-permute-start.2 = (bf16[192,768]{1,0:T(8,128)(2,1)S(1)}, bf16[192,768]{1,0:T(8,128)(2,1)}, u32[]{:S(2)}, u32[]{:S(2)}) collective-permute-start(bf16[192,768]{1,0:T(8,128)(2,1)S(1)} %constant_dynamic-slice_fusion), channel_id=1, source_target_pairs={{0,1},{1,0},{2,3},{3,2},{4,5},{5,4},{6,7},{7,6},{8,9},{9,8},{10,11... | collective-permute-start | bytes 884744 | tf_op jit(solution)/shard_map/ppermute | solution.py:533
  19.3 31.2 %collective-permute-start.4 = (bf16[392,768]{1,0:T(8,128)(2,1)S(1)}, bf16[392,768]{1,0:T(8,128)(2,1)}, u32[]{:S(2)}, u32[]{:S(2)}) collective-permute-start(bf16[392,768]{1,0:T(8,128)(2,1)S(1)} %copy-done.13), channel_id=1, source_target_pairs={{0,1},{1,0},{2,3},{3,2},{4,5},{5,4},{6,7},{7,6},{8,9},{9,8},{10,11... | collective-permute-start | bytes 1806344 | tf_op jit(solution)/shard_map/ppermute | solution.py:533
  32.1 15.0 %collective-permute-start.1 = (bf16[384,392]{1,0:T(8,128)(2,1)S(1)}, bf16[384,392]{1,0:T(8,128)(2,1)S(1)}, u32[]{:S(2)}, u32[]{:S(2)}) collective-permute-start(bf16[384,392]{1,0:T(8,128)(2,1)S(1)} %get-tuple-element.89.mine_ref.refs_3_), channel_id=1, source_target_pairs={{0,1},{1,0},{2,3},{3,2},{4,5},{5,4},{6,7},{7,6},{8,9},{9,8},{10,11... | collective-permute-start | bytes 903176 | tf_op jit(solution)/shard_map/ppermute | solution.py:533
  33.9 15.4 %collective-permute-start.3 = (bf16[192,768]{1,0:T(8,128)(2,1)}, bf16[192,768]{1,0:T(8,128)(2,1)S(1)}, u32[]{:S(2)}, u32[]{:S(2)}) collective-permute-start(bf16[192,768]{1,0:T(8,128)(2,1)} %collective-permute-done.2), channel_id=1, source_target_pairs={{0,2},{2,0},{4,6},{6,4},{8,10},{10,8},{12,14},{14,12},{16,18},{18,... | collective-permute-start | bytes 884744 | tf_op jit(solution)/shard_map/ppermute | solution.py:537
  47.9 14.3 %collective-permute-start.5 = (bf16[384,392]{1,0:T(8,128)(2,1)}, bf16[384,392]{1,0:T(8,128)(2,1)S(1)}, u32[]{:S(2)}, u32[]{:S(2)}) collective-permute-start(bf16[384,392]{1,0:T(8,128)(2,1)} %copy-done.30), channel_id=1, source_target_pairs={{0,1},{1,0},{2,3},{3,2},{4,5},{5,4},{6,7},{7,6},{8,9},{9,8},{10,11... | collective-permute-start | bytes 903176 | tf_op jit(solution)/shard_map/ppermute | solution.py:533
  61.6 15.5 %collective-permute-start.6 = (bf16[392,768]{1,0:T(8,128)(2,1)S(1)}, bf16[392,768]{1,0:T(8,128)(2,1)S(1)}, u32[]{:S(2)}, u32[]{:S(2)}) collective-permute-start(bf16[392,768]{1,0:T(8,128)(2,1)S(1)} %get-tuple-element.93), channel_id=1, source_target_pairs={{0,1},{1,0},{2,3},{3,2},{4,5},{5,4},{6,7},{7,6},{8,9},{9,8},{10,11... | collective-permute-start | bytes 1806344 | tf_op jit(solution)/shard_map/ppermute | solution.py:533
  81.8 11.8 %collective-permute-start.7 = (bf16[384,392]{1,0:T(8,128)(2,1)}, bf16[384,392]{1,0:T(8,128)(2,1)}, u32[]{:S(2)}, u32[]{:S(2)}) collective-permute-start(bf16[384,392]{1,0:T(8,128)(2,1)} %get-tuple-element.104), channel_id=1, source_target_pairs={{0,1},{1,0},{2,3},{3,2},{4,5},{5,4},{6,7},{7,6},{8,9},{9,8},{10,11... | collective-permute-start | bytes 903176 | tf_op jit(solution)/shard_map/ppermute | solution.py:533
  88.2 23.1 %collective-permute-start.10 = (bf16[768,768]{1,0:T(8,128)(2,1)S(1)}, bf16[768,768]{1,0:T(8,128)(2,1)}, u32[]{:S(2)}, u32[]{:S(2)}) collective-permute-start(bf16[768,768]{1,0:T(8,128)(2,1)S(1)} %add_convert_fusion.refs_6_), channel_id=1, source_target_pairs={{0,4},{2,10},{4,0},{6,14},{8,12},{10,2},{12,8},{14,6},{16,20},{18,... | collective-permute-start | bytes 3538952 | tf_op jit(solution)/shard_map/ppermute | solution.py:560
  93.6 20.0 %collective-permute-start.9 = (bf16[392,768]{1,0:T(8,128)(2,1)}, bf16[392,768]{1,0:T(8,128)(2,1)S(1)}, u32[]{:S(2)}, u32[]{:S(2)}) collective-permute-start(bf16[392,768]{1,0:T(8,128)(2,1)} %get-tuple-element.111.refs_4_), channel_id=1, source_target_pairs={{0,1},{1,0},{2,3},{3,2},{4,5},{5,4},{6,7},{7,6},{8,9},{9,8},{10,11... | collective-permute-start | bytes 1806344 | tf_op jit(solution)/shard_map/ppermute | solution.py:533
  118.4 19.7 %collective-permute-start.13 = (bf16[768,768]{1,0:T(8,128)(2,1)}, bf16[768,768]{1,0:T(8,128)(2,1)}, u32[]{:S(2)}, u32[]{:S(2)}) collective-permute-start(bf16[768,768]{1,0:T(8,128)(2,1)} %get-tuple-element.113.refs_2_), channel_id=1, source_target_pairs={{0,2},{2,0},{4,6},{6,4},{8,10},{10,8},{12,14},{14,12},{16,18},{18,... | collective-permute-start | bytes 3538952 | tf_op jit(solution)/shard_map/ppermute | solution.py:537
  118.4 16.3 %collective-permute-start.22 = (bf16[384,768]{1,0:T(8,128)(2,1)S(1)}, bf16[384,768]{1,0:T(8,128)(2,1)}, u32[]{:S(2)}, u32[]{:S(2)}) collective-permute-start(bf16[384,768]{1,0:T(8,128)(2,1)S(1)} %add_convert_fusion.2.refs_7_), channel_id=1, source_target_pairs={{0,8},{2,18},{4,12},{6,22},{8,0},{10,26},{12,4},{14,30},{16,24},{1... | collective-permute-start | bytes 1769480 | tf_op jit(solution)/shard_map/ppermute | solution.py:560
  136.0 11.0 %collective-permute-start.23 = (bf16[192,768]{1,0:T(8,128)(2,1)S(1)}, bf16[192,768]{1,0:T(8,128)(2,1)S(1)}, u32[]{:S(2)}, u32[]{:S(2)}) collective-permute-start(bf16[192,768]{1,0:T(8,128)(2,1)S(1)} %add_convert_fusion.4), channel_id=1, source_target_pairs={{0,16},{2,6},{4,20},{6,2},{8,24},{10,14},{12,28},{14,10},{16,0},{1... | collective-permute-start | bytes 884744 | tf_op jit(solution)/shard_map/ppermute | solution.py:560
  140.1 13.4 %collective-permute-start.14 = (bf16[384,768]{1,0:T(8,128)(2,1)}, bf16[384,768]{1,0:T(8,128)(2,1)}, u32[]{:S(2)}, u32[]{:S(2)}) collective-permute-start(bf16[384,768]{1,0:T(8,128)(2,1)} %add_convert_fusion.1), channel_id=1, source_target_pairs={{0,4},{2,10},{4,0},{6,14},{8,12},{10,2},{12,8},{14,6},{16,20},{18,... | collective-permute-start | bytes 1769480 | tf_op jit(solution)/shard_map/ppermute | solution.py:560
  141.6 33.3 %collective-permute-start.12 = (bf16[392,768]{1,0:T(8,128)(2,1)}, bf16[392,768]{1,0:T(8,128)(2,1)}, u32[]{:S(2)}, u32[]{:S(2)}) collective-permute-start(bf16[392,768]{1,0:T(8,128)(2,1)} %get-tuple-element.119), channel_id=1, source_target_pairs={{0,1},{1,0},{2,3},{3,2},{4,5},{5,4},{6,7},{7,6},{8,9},{9,8},{10,11... | collective-permute-start | bytes 1806344 | tf_op jit(solution)/shard_map/ppermute | solution.py:533
  142.2 32.7 %collective-permute-start.11 = (bf16[392,768]{1,0:T(8,128)(2,1)}, bf16[392,768]{1,0:T(8,128)(2,1)}, u32[]{:S(2)}, u32[]{:S(2)}) collective-permute-start(bf16[392,768]{1,0:T(8,128)(2,1)} %get-tuple-element.116), channel_id=1, source_target_pairs={{0,1},{1,0},{2,3},{3,2},{4,5},{5,4},{6,7},{7,6},{8,9},{9,8},{10,11... | collective-permute-start | bytes 1806344 | tf_op jit(solution)/shard_map/ppermute | solution.py:533
  149.1 23.6 %collective-permute-start.24 = (bf16[192,768]{1,0:T(8,128)(2,1)}, bf16[192,768]{1,0:T(8,128)(2,1)}, u32[]{:S(2)}, u32[]{:S(2)}) collective-permute-start(bf16[192,768]{1,0:T(8,128)(2,1)} %add_convert_fusion.3), channel_id=1, source_target_pairs={{0,16},{2,6},{4,20},{6,2},{8,24},{10,14},{12,28},{14,10},{16,0},{1... | collective-permute-start | bytes 884744 | tf_op jit(solution)/shard_map/ppermute | solution.py:560
  154.8 29.1 %collective-permute-start.15 = (bf16[192,768]{1,0:T(8,128)(2,1)S(1)}, bf16[192,768]{1,0:T(8,128)(2,1)}, u32[]{:S(2)}, u32[]{:S(2)}) collective-permute-start(bf16[192,768]{1,0:T(8,128)(2,1)S(1)} %add_convert_fusion.5.refs_9_), channel_id=1, source_target_pairs={{0,8},{2,18},{4,12},{6,22},{8,0},{10,26},{12,4},{14,30},{16,24},{1... | collective-permute-start | bytes 884744 | tf_op jit(solution)/shard_map/ppermute | solution.py:560
  174.9 19.9 %collective-permute-start.25 = (bf16[384,768]{1,0:T(8,128)(2,1)}, bf16[384,768]{1,0:T(8,128)(2,1)}, u32[]{:S(2)}, u32[]{:S(2)}) collective-permute-start(bf16[384,768]{1,0:T(8,128)(2,1)} %maximum_select_fusion.5), channel_id=1, source_target_pairs={{0,8},{2,18},{4,12},{6,22},{8,0},{10,26},{12,4},{14,30},{16,24},{1... | collective-permute-start | bytes 1769480 | tf_op jit(solution)/shard_map/ppermute | solution.py:560
  185.0 7.8 %collective-permute-start.16 = (bf16[96,768]{1,0:T(8,128)(2,1)S(1)}, bf16[96,768]{1,0:T(8,128)(2,1)S(1)}, u32[]{:S(2)}, u32[]{:S(2)}) collective-permute-start(bf16[96,768]{1,0:T(8,128)(2,1)S(1)} %add_convert_fusion.7), channel_id=1, source_target_pairs={{0,16},{2,6},{4,20},{6,2},{8,24},{10,14},{12,28},{14,10},{16,0},{1... | collective-permute-start | bytes 442376 | tf_op jit(solution)/shard_map/ppermute | solution.py:560
  194.6 8.5 %collective-permute-start.18 = (bf16[120,768]{1,0:T(8,128)(2,1)S(1)}, bf16[120,768]{1,0:T(8,128)(2,1)S(1)}, u32[]{:S(2)}, u32[]{:S(2)}) collective-permute-start(bf16[120,768]{1,0:T(8,128)(2,1)S(1)} %pad_maximum_fusion.3), channel_id=1, source_target_pairs={{0,16},{2,6},{4,20},{6,2},{8,24},{10,14},{12,28},{14,10},{16,0},{1... | collective-permute-start | bytes 552968 | tf_op jit(solution)/shard_map/ppermute | solution.py:560
  196.8 18.3 %collective-permute-start.26 = (bf16[768,768]{1,0:T(8,128)(2,1)S(1)}, bf16[768,768]{1,0:T(8,128)(2,1)}, u32[]{:S(2)}, u32[]{:S(2)}) collective-permute-start(bf16[768,768]{1,0:T(8,128)(2,1)S(1)} %maximum_select_fusion.2), channel_id=1, source_target_pairs={{0,4},{2,10},{4,0},{6,14},{8,12},{10,2},{12,8},{14,6},{16,20},{18,... | collective-permute-start | bytes 3538952 | tf_op jit(solution)/shard_map/ppermute | solution.py:560
  211.9 10.3 %collective-permute-start.20 = (bf16[408,768]{1,0:T(8,128)(2,1)S(1)}, bf16[408,768]{1,0:T(8,128)(2,1)S(1)}, u32[]{:S(2)}, u32[]{:S(2)}) collective-permute-start(bf16[408,768]{1,0:T(8,128)(2,1)S(1)} %pad_maximum_fusion.1), channel_id=1, source_target_pairs={{0,4},{2,10},{4,0},{6,14},{8,12},{10,2},{12,8},{14,6},{16,20},{18,... | collective-permute-start | bytes 1880072 | tf_op jit(solution)/shard_map/ppermute | solution.py:560
  217.1 12.9 %collective-permute-start.27 = (bf16[1536,768]{1,0:T(8,128)(2,1)S(1)}, bf16[1536,768]{1,0:T(8,128)(2,1)S(1)}, u32[]{:S(2)}, u32[]{:S(2)}) collective-permute-start(bf16[1536,768]{1,0:T(8,128)(2,1)S(1)} %maximum_select_fusion.mine_ref), channel_id=1, source_target_pairs={{0,2},{2,0},{4,6},{6,4},{8,10},{10,8},{12,14},{14,12},{16,18},{18,... | collective-permute-start | bytes 7077896 | tf_op jit(solution)/shard_map/ppermute | solution.py:537
  (61 other events, 438.7 us)

commit v4 on v3

--- a/solution.py
+++ b/solution.py
@@ -37,7 +37,7 @@
 ):
     count, outputs = len(args), len(out_shape)
     skipped = len(behind) + len(through)
-    place = pl.BlockSpec(memory_space=pl.ANY)
+    place, kept = pl.BlockSpec(memory_space=pl.ANY), pl.BlockSpec(memory_space=pltpu.HBM)
 
     def body(*refs):
         given, refs = refs[:count], refs[count + skipped :]
@@ -49,11 +49,11 @@
         grid_spec=pltpu.PrefetchScalarGridSpec(
             num_scalar_prefetch=prefetch,
             grid=grid,
-            in_specs=list(in_specs) + [place] * skipped,
-            out_specs=list(out_specs) + [place] * len(through),
+            in_specs=list(in_specs) + [place] * len(behind) + [kept] * len(through),
+            out_specs=list(out_specs) + [kept] * len(through),
             scratch_shapes=list(scratch),
         ),
-        out_shape=list(out_shape) + [shaped(a.shape, a.dtype) for a in through],
+        out_shape=list(out_shape) + [stored(a.shape, a.dtype) for a in through],
         input_output_aliases={first + k: outputs + k for k in range(len(through))},
         compiler_params=params,
         **rest,
@@ -551,7 +551,8 @@
         self.terms, self.came = [(kept, 0)], came
         self.core, chip = place & 1, place >> 1
         bits = (count // 2).bit_length() - 1
-        self.orders = [(k, (k + 1) % bits) for k in range(bits)]
+        other = [1, 0] if bits > 1 else [0]
+        self.orders = list(zip(range(bits), other + list(range(2, bits))))
         self.bits = [(chip >> jnp.where(self.core == 0, a, b)) & 1 for a, b in self.orders]
         self.sums = None
 
@@ -750,7 +751,7 @@
     away, kept = tail_gradient(
         core_list, grads, normed1, own_context, grad_branch, other_context, branch_other, behind=(step,)
     )
-    (first_a, first_b, stack_sums), (kept,) = by_inputs(grads, far(w_stack), behind=(away,), through=(kept,))
+    (first_a, first_b, stack_sums), (kept,) = by_inputs(grads, far(w_stack), behind=(far(away),), through=(kept,))
     tail = Sum(kept, swap_dp(away, 1, count), place, count)
     came = swap_mp(first_b)
     tail.scatter(0)
@@ -758,7 +759,7 @@
         up_down.scatter(k)
         step = tail.scatter(k - 1)
     (grad_tokens, sums_first, output), (kept,) = last(
-        first_a, came, tokens, grad_hidden, first_gain, b_down, hidden, branch_a, branch_came,
+        far(first_a), came, far(tokens), far(grad_hidden), first_gain, b_down, far(hidden), far(branch_a), branch_came,
         behind=(step,), through=(tail.terms[0][0],),
     )
     tail.terms[0] = (kept, tail.terms[0][1])

time: 236 us -> 220 us (0.932)
  local copies, waits for them, and re-layouts: 26.5 us -> 11.1 us
  other arithmetic: 22.8 us -> 20 us
    unnamed x114 -> x54, local copies, waits for them, and re-layouts: 26.2 us -> 10.8 us
    select_n x6, other arithmetic: 6.83 us -> 4.3 us  [gather(): jnp.where(self.bits[step] == 0, jnp.concatenate([mine, other], axis=0), j...]
  transfers between devices with their start and end apart: 28 -> 28, of which waited for: 15 -> 14; matrix products, arithmetic and copies ran while one was open for 10% -> 9% of each run, Pallas kernels for 26% -> 28%
where the time goes in v4:
time: 220 us; the launch traced here: 219 us
  waiting for transfers between devices  81.5 us (37%)
  Pallas kernels  74.6 us (34%)
  starting transfers between devices  31 us (14%)
  other arithmetic  20 us (9%)
  local copies, waits for them, and re-layouts  11.1 us (5%)
    ppermute x12, waiting for transfers between devices, swap(): lax.ppermute(value, 'dp', [(i, partner(i)) for i in range(self.count)])  52.5 us
    pallas_call x5, Pallas kernels, ordered_call(): pl.pallas_call(body, grid_spec=pltpu.PrefetchScalarGridSpec(num_scalar_pr...  31.4 us
    pallas_call x2, Pallas kernels, feed_forward(): pl.pallas_call(functools.partial(feed_forward_kernel, other=bool(other)),...  24.1 us
    ppermute x11, waiting for transfers between devices, swap_mp(): return lax.ppermute(value, 'mp', [(0, 1), (1, 0)])  22.8 us
    ppermute x12, starting transfers between devices, swap(): lax.ppermute(value, 'dp', [(i, partner(i)) for i in range(self.count)])  16 us
    ppermute x11, starting transfers between devices, swap_mp(): return lax.ppermute(value, 'mp', [(0, 1), (1, 0)])  14.4 us
    convert_element_type x8, other arithmetic, rows_of(): return total.astype(low)  13 us
    unnamed x54, local copies, waits for them, and re-layouts  10.8 us
  transfers between devices with their start and end apart: 28, of which 14 were waited for; matrix products, arithmetic and copies ran while one was open for 9% of the time, Pallas kernels for 28%

profile of v4, /device:TPU:0, one launch (start us, length us, event | category | flops | bytes accessed | tf_op | source)
XLA Modules:
  0.0 219.3 jit_solution(6217638856343898848)
XLA Ops:
  0.7 3.0 %collective-permute-start = (bf16[392,768]{1,0:T(8,128)(2,1)}, bf16[392,768]{1,0:T(8,128)(2,1)S(1)}, u32[]{:S(2)}, u32[]{:S(2)}) collective-permute-start(bf16[392,768]{1,0:T(8,128)(2,1)} %refs_2_.1), channel_id=1, source_target_pairs={{0,1},{1,0},{2,3},{3,2},{4,5},{5,4},{6,7},{7,6},{8,9},{9,8},{10,11... | collective-permute-start | bytes 1806344 | tf_op jit(solution)/shard_map/ppermute | solution.py:533
  12.5 5.0 %collective-permute-done.other_ref.tokens_ref = bf16[392,768]{1,0:T(8,128)(2,1)S(1)} collective-permute-done((bf16[392,768]{1,0:T(8,128)(2,1)}, bf16[392,768]{1,0:T(8,128)(2,1)S(1)}, u32[]{:S(2)}, u32[]{:S(2)}) %collective-permute-start) | collective-permute-done | bytes 602144 | tf_op jit(solution)/shard_map/ppermute | solution.py:533
  19.6 10.4 %attention_forward.1 = (bf16[1152,784]{1,0:T(8,128)(2,1)}, bf16[384,392]{1,0:T(8,128)(2,1)S(1)}, bf16[384,392]{1,0:T(8,128)(2,1)}, f32[384,784]{1,0:T(8,128)}, f...) custom-call(bf16[1152,392]{1,0:T(8,128)(2,1)S(1)} %get-tuple-element.80.own_ref, ...), custom_call_target="tpu_custom_call" | custom-call | flops 10000000000 | bytes 10000000 | tf_op jit(solution)/shard_map/attention_forward/pallas_call | solution.py:188
  31.7 15.3 %collective-permute-done.1.peer_ref = bf16[384,392]{1,0:T(8,128)(2,1)S(1)} collective-permute-done((bf16[384,392]{1,0:T(8,128)(2,1)S(1)}, bf16[384,392]{1,0:T(8,128)(2,1)S(1)}, u32[]{:S(2)}, u32[]{:S(2)}) %collective-permute-start.1) | collective-permute-done | bytes 301088 | tf_op jit(solution)/shard_map/ppermute | solution.py:533
  48.7 9.1 %feed_forward.2 = (bf16[392,768]{1,0:T(8,128)(2,1)S(1)}, bf16[392,1536]{1,0:T(8,128)(2,1)S(1)}, bf16[392,1536]{1,0:T(8,128)(2,1)S(1)}, bf16[392,768]{1,0:T(8,128...) custom-call(bf16[392,768]{1,0:T(8,128)(2,1)S(1)} %collective-permute-done.other_ref.tokens_ref, ...), custom_call_target="tpu_custom_call" | custom-call | flops 5000000000 | bytes 10000000 | tf_op jit(solution)/shard_map/feed_forward/pallas_call | solution.py:350
  58.4 15.0 %feed_forward.3 = (f32[392,768]{1,0:T(8,128)}, bf16[392,768]{1,0:T(8,128)(2,1)S(1)}, bf16[392,768]{1,0:T(8,128)(2,1)}, f32[1,1536]{1,0:T(1,128)S(1)}, bf16[1536,...) custom-call(bf16[392,768]{1,0:T(8,128)(2,1)S(1)} %copy-done.3, bf16[384,392]{1,0:T(8,128)(2,1)S(1)} %get-tuple-element.89.mine_ref.refs_3_, ...), custom_call_target="tpu_custom_call" | custom-call | flops 5000000000 | bytes 10000000 | tf_op jit(solution)/shard_map/feed_forward/pallas_call | solution.py:350
  74.6 2.8 %second_norm_backward.1 = (f32[392,768]{1,0:T(8,128)}, bf16[392,768]{1,0:T(8,128)(2,1)}, bf16[384,392]{1,0:T(8,128)(2,1)}, bf16[384,392]{1,0:T(8,128)(2,1)}, f32...) custom-call(bf16[392,768]{1,0:T(8,128)(2,1)S(1)} %get-tuple-element.100.refs_0_, ...), custom_call_target="tpu_custom_call", output_to_operand_aliasing={{5}: (7, {})} | custom-call | flops 1000000000 | bytes 5000000 | tf_op jit(solution)/shard_map/second_norm_backward/pallas_call | solution.py:47
  78.8 3.3 %collective-permute-done.8 = bf16[1536,768]{1,0:T(8,128)(2,1)S(1)} collective-permute-done((bf16[1536,768]{1,0:T(8,128)(2,1)}, bf16[1536,768]{1,0:T(8,128)(2,1)S(1)}, u32[]{:S(2)}, u32[]{:S(2)}) %collective-permute-start.8) | collective-permute-done | bytes 2359328 | tf_op jit(solution)/shard_map/ppermute | solution.py:537
  90.6 13.6 %attention_backward.1 = (bf16[1152,784]{1,0:T(8,128)(2,1)S(1)}, bf16[392,768]{1,0:T(8,128)(2,1)}, bf16[1536,768]{1,0:T(8,128)(2,1)}) custom-call(bf16[1152,784]{1,0:T(8,128)(2,1)} %get-tuple-element.85.refs_0_, f32[384,784]{1,0:T(8,128)} %get-tuple-element.86.refs_1_, ...), custom_call_target="tpu_custom_call", output_to_operand_aliasing={{1}: (7, {}), {2}: (8, {})} | custom-call | flops 10000000000 | bytes 10000000 | tf_op jit(solution)/shard_map/attention_backward/pallas_call | solution.py:47
  104.2 2.4 %add_convert_fusion.2.refs_7_ = bf16[384,768]{1,0:T(8,128)(2,1)S(1)} fusion(bf16[768,768]{1,0:T(8,128)(2,1)} %collective-permute-done.10, s32[]{:T(128)S(6)} %select_n.133, bf16[1536,768]{1,0:T(8,128)(2,1)} %copy-done.23, s32[]{:T(128)S(6)} %select_n.132, bf16[1536,768]{1,0:T(8,128)(2,1)} %get-tuple-element.112), kind=kLoop, calls=%fused_computation.6 | loop fusion | flops 1769472 | bytes 2359304 | tf_op jit(solution)/shard_map/convert_element_type | solution.py:567
  106.8 5.7 %tail_gradient.1 = (bf16[768,768]{1,0:T(8,128)(2,1)}, f32[768,768]{1,0:T(8,128)}) custom-call(s32[1]{0:T(128)} %bitcast.1.refs_0_.core_ref, bf16[1152,784]{1,0:T(8,128)(2,1)S(1)} %get-tuple-element.108.refs_1_.refs_0_, bf16[784,768]{1,0:T(8,128)(2,1)S(1)} %copy-done.22, bf16[384,392]{1,0:T(8,128)(2,1)S(1)} %get-tuple-element.89.mine_ref.refs_3_, ...), custom_call_target="tpu_custom_call" | custom-call | flops 2000000000 | bytes 10000000 | tf_op jit(solution)/shard_map/tail_gradient/pallas_call | solution.py:47
  115.7 4.8 %first_normed_gradient.1 = (bf16[392,768]{1,0:T(8,128)(2,1)}, bf16[392,768]{1,0:T(8,128)(2,1)}, f32[8,1152]{1,0:T(8,128)S(1)}, f32[768,768]{1,0:T(8,128)}) custom-call(bf16[1152,784]{1,0:T(8,128)(2,1)S(1)} %copy-done.20, bf16[1152,768]{1,0:T(8,128)(2,1)} %copy-done.21, bf16[768,768]{1,0:T(8,128)(2,1)} %get-tuple-element.113.refs_2_, ...), custom_call_target="tpu_custom_call", output_to_operand_aliasing={{3}: (3, {})} | custom-call | flops 2000000000 | bytes 5000000 | tf_op jit(solution)/shard_map/first_normed_gradient/pallas_call | solution.py:47
  123.9 2.6 %collective-permute-start.23 = (bf16[192,768]{1,0:T(8,128)(2,1)S(1)}, bf16[192,768]{1,0:T(8,128)(2,1)S(1)}, u32[]{:S(2)}, u32[]{:S(2)}) collective-permute-start(bf16[192,768]{1,0:T(8,128)(2,1)S(1)} %add_convert_fusion.4), channel_id=1, source_target_pairs={{0,16},{2,18},{4,20},{6,22},{8,24},{10,26},{12,28},{14,30},{16,0},... | collective-permute-start | bytes 884744 | tf_op jit(solution)/shard_map/ppermute | solution.py:561
  132.4 7.4 %collective-permute-done.23 = bf16[192,768]{1,0:T(8,128)(2,1)S(1)} collective-permute-done((bf16[192,768]{1,0:T(8,128)(2,1)S(1)}, bf16[192,768]{1,0:T(8,128)(2,1)S(1)}, u32[]{:S(2)}, u32[]{:S(2)}) %collective-permute-start.23) | collective-permute-done | bytes 294944 | tf_op jit(solution)/shard_map/ppermute | solution.py:561
  142.6 4.1 %collective-permute-start.15 = (bf16[192,768]{1,0:T(8,128)(2,1)S(1)}, bf16[192,768]{1,0:T(8,128)(2,1)}, u32[]{:S(2)}, u32[]{:S(2)}) collective-permute-start(bf16[192,768]{1,0:T(8,128)(2,1)S(1)} %add_convert_fusion.5.refs_9_), channel_id=1, source_target_pairs={{0,8},{2,6},{4,12},{6,2},{8,0},{10,14},{12,4},{14,10},{16,24},{18,... | collective-permute-start | bytes 884744 | tf_op jit(solution)/shard_map/ppermute | solution.py:561
  146.7 9.7 %collective-permute-done.24 = bf16[192,768]{1,0:T(8,128)(2,1)} collective-permute-done((bf16[192,768]{1,0:T(8,128)(2,1)S(1)}, bf16[192,768]{1,0:T(8,128)(2,1)}, u32[]{:S(2)}, u32[]{:S(2)}) %collective-permute-start.24) | collective-permute-done | bytes 294944 | tf_op jit(solution)/shard_map/ppermute | solution.py:561
  158.1 4.5 %first_norm_backward.1 = (f32[392,768]{1,0:T(8,128)}, f32[8,768]{1,0:T(8,128)S(1)}, bf16[392,768]{1,0:T(8,128)(2,1)}, f32[768,768]{1,0:T(8,128)}) custom-call(bf16[392,768]{1,0:T(8,128)(2,1)} %get-tuple-element.115.refs_0_, bf16[392,768]{1,0:T(8,128)(2,1)S(1)} %collective-permute-done.11.refs_1_, ...), custom_call_target="tpu_custom_call", output_to_operand_aliasing={{3}: (10, {})} | custom-call | flops 100000000 | bytes 5000000 | tf_op jit(solution)/shard_map/first_norm_backward/pallas_call | solution.py:47
  166.5 6.5 %collective-permute-done.16 = bf16[96,768]{1,0:T(8,128)(2,1)S(1)} collective-permute-done((bf16[96,768]{1,0:T(8,128)(2,1)S(1)}, bf16[96,768]{1,0:T(8,128)(2,1)S(1)}, u32[]{:S(2)}, u32[]{:S(2)}) %collective-permute-start.16) | collective-permute-done | bytes 147488 | tf_op jit(solution)/shard_map/ppermute | solution.py:561
  178.0 7.9 %collective-permute-done.18 = bf16[120,768]{1,0:T(8,128)(2,1)S(1)} collective-permute-done((bf16[120,768]{1,0:T(8,128)(2,1)}, bf16[120,768]{1,0:T(8,128)(2,1)S(1)}, u32[]{:S(2)}, u32[]{:S(2)}) %collective-permute-start.18) | collective-permute-done | bytes 184352 | tf_op jit(solution)/shard_map/ppermute | solution.py:561
  186.8 10.9 %collective-permute-done.19 = bf16[216,768]{1,0:T(8,128)(2,1)S(1)} collective-permute-done((bf16[216,768]{1,0:T(8,128)(2,1)}, bf16[216,768]{1,0:T(8,128)(2,1)S(1)}, u32[]{:S(2)}, u32[]{:S(2)}) %collective-permute-start.19) | collective-permute-done | bytes 331808 | tf_op jit(solution)/shard_map/ppermute | solution.py:561
  200.2 8.2 %collective-permute-done.20 = bf16[408,768]{1,0:T(8,128)(2,1)S(1)} collective-permute-done((bf16[408,768]{1,0:T(8,128)(2,1)S(1)}, bf16[408,768]{1,0:T(8,128)(2,1)S(1)}, u32[]{:S(2)}, u32[]{:S(2)}) %collective-permute-start.20) | collective-permute-done | bytes 626720 | tf_op jit(solution)/shard_map/ppermute | solution.py:561
  209.1 2.9 %collective-permute-done.21.came_ref = bf16[792,768]{1,0:T(8,128)(2,1)S(1)} collective-permute-done((bf16[792,768]{1,0:T(8,128)(2,1)S(1)}, bf16[792,768]{1,0:T(8,128)(2,1)S(1)}, u32[]{:S(2)}, u32[]{:S(2)}) %collective-permute-start.21) | collective-permute-done | bytes 1216544 | tf_op jit(solution)/shard_map/ppermute | solution.py:537
  212.0 2.8 %tail_finish.1 = (f32[768,384]{1,0:T(8,128)}, f32[768,384]{1,0:T(8,128)}, f32[768,384]{1,0:T(8,128)}, f32[384,768]{1,0:T(8,128)}, f32[768]{0:T(1024)}, /*index=5...) custom-call(s32[1]{0:T(128)} %bitcast.1.refs_0_.core_ref, ...), custom_call_target="tpu_custom_call" | custom-call | flops 1000000 | bytes 10000000 | tf_op jit(solution)/shard_map/tail_finish/pallas_call | solution.py:667
  214.8 4.5 %up_down_finish.1 = (f32[768,1536]{1,0:T(8,128)}, f32[1536,768]{1,0:T(8,128)}) custom-call(s32[1]{0:T(128)} %bitcast.1.refs_0_.core_ref, bf16[1536,768]{1,0:T(8,128)(2,1)S(1)} %maximum_select_fusion.mine_ref, bf16[1536,768]{1,0:T(8,128)(2,1)S(1)} %collective-permute-done.27.other_ref), custom_call_target="tpu_custom_call" | custom-call | flops 1000000 | bytes 10000000 | tf_op jit(solution)/shard_map/up_down_finish/pallas_call | solution.py:626
  (138 shorter events, 55.8 us)
Async XLA Ops:
  0.7 16.8 %collective-permute-start = (bf16[392,768]{1,0:T(8,128)(2,1)}, bf16[392,768]{1,0:T(8,128)(2,1)S(1)}, u32[]{:S(2)}, u32[]{:S(2)}) collective-permute-start(bf16[392,768]{1,0:T(8,128)(2,1)} %refs_2_.1), channel_id=1, source_target_pairs={{0,1},{1,0},{2,3},{3,2},{4,5},{5,4},{6,7},{7,6},{8,9},{9,8},{10,11... | collective-permute-start | bytes 1806344 | tf_op jit(solution)/shard_map/ppermute | solution.py:533
  17.5 14.2 %collective-permute-start.2 = (bf16[192,768]{1,0:T(8,128)(2,1)S(1)}, bf16[192,768]{1,0:T(8,128)(2,1)S(1)}, u32[]{:S(2)}, u32[]{:S(2)}) collective-permute-start(bf16[192,768]{1,0:T(8,128)(2,1)S(1)} %constant_dynamic-slice_fusion), channel_id=1, source_target_pairs={{0,1},{1,0},{2,3},{3,2},{4,5},{5,4},{6,7},{7,6},{8,9},{9,8},{10,11... | collective-permute-start | bytes 884744 | tf_op jit(solution)/shard_map/ppermute | solution.py:533
  19.2 29.4 %collective-permute-start.4 = (bf16[392,768]{1,0:T(8,128)(2,1)S(1)}, bf16[392,768]{1,0:T(8,128)(2,1)}, u32[]{:S(2)}, u32[]{:S(2)}) collective-permute-start(bf16[392,768]{1,0:T(8,128)(2,1)S(1)} %copy-done.4), channel_id=1, source_target_pairs={{0,1},{1,0},{2,3},{3,2},{4,5},{5,4},{6,7},{7,6},{8,9},{9,8},{10,11... | collective-permute-start | bytes 1806344 | tf_op jit(solution)/shard_map/ppermute | solution.py:533
  30.0 17.0 %collective-permute-start.1 = (bf16[384,392]{1,0:T(8,128)(2,1)S(1)}, bf16[384,392]{1,0:T(8,128)(2,1)S(1)}, u32[]{:S(2)}, u32[]{:S(2)}) collective-permute-start(bf16[384,392]{1,0:T(8,128)(2,1)S(1)} %get-tuple-element.89.mine_ref.refs_3_), channel_id=1, source_target_pairs={{0,1},{1,0},{2,3},{3,2},{4,5},{5,4},{6,7},{7,6},{8,9},{9,8},{10,11... | collective-permute-start | bytes 903176 | tf_op jit(solution)/shard_map/ppermute | solution.py:533
  31.7 16.7 %collective-permute-start.3 = (bf16[192,768]{1,0:T(8,128)(2,1)S(1)}, bf16[192,768]{1,0:T(8,128)(2,1)S(1)}, u32[]{:S(2)}, u32[]{:S(2)}) collective-permute-start(bf16[192,768]{1,0:T(8,128)(2,1)S(1)} %collective-permute-done.2), channel_id=1, source_target_pairs={{0,2},{2,0},{4,6},{6,4},{8,10},{10,8},{12,14},{14,12},{16,18},{18,... | collective-permute-start | bytes 884744 | tf_op jit(solution)/shard_map/ppermute | solution.py:537
  47.0 11.4 %collective-permute-start.5 = (bf16[384,392]{1,0:T(8,128)(2,1)}, bf16[384,392]{1,0:T(8,128)(2,1)S(1)}, u32[]{:S(2)}, u32[]{:S(2)}) collective-permute-start(bf16[384,392]{1,0:T(8,128)(2,1)} %get-tuple-element.95.mine_ref.refs_5_), channel_id=1, source_target_pairs={{0,1},{1,0},{2,3},{3,2},{4,5},{5,4},{6,7},{7,6},{8,9},{9,8},{10,11... | collective-permute-start | bytes 903176 | tf_op jit(solution)/shard_map/ppermute | solution.py:533
  57.8 15.6 %collective-permute-start.6 = (bf16[392,768]{1,0:T(8,128)(2,1)S(1)}, bf16[392,768]{1,0:T(8,128)(2,1)S(1)}, u32[]{:S(2)}, u32[]{:S(2)}) collective-permute-start(bf16[392,768]{1,0:T(8,128)(2,1)S(1)} %get-tuple-element.93), channel_id=1, source_target_pairs={{0,1},{1,0},{2,3},{3,2},{4,5},{5,4},{6,7},{7,6},{8,9},{9,8},{10,11... | collective-permute-start | bytes 1806344 | tf_op jit(solution)/shard_map/ppermute | solution.py:533
  77.4 11.7 %collective-permute-start.7 = (bf16[384,392]{1,0:T(8,128)(2,1)}, bf16[384,392]{1,0:T(8,128)(2,1)S(1)}, u32[]{:S(2)}, u32[]{:S(2)}) collective-permute-start(bf16[384,392]{1,0:T(8,128)(2,1)} %get-tuple-element.104), channel_id=1, source_target_pairs={{0,1},{1,0},{2,3},{3,2},{4,5},{5,4},{6,7},{7,6},{8,9},{9,8},{10,11... | collective-permute-start | bytes 903176 | tf_op jit(solution)/shard_map/ppermute | solution.py:533
  85.6 18.7 %collective-permute-start.10 = (bf16[768,768]{1,0:T(8,128)(2,1)S(1)}, bf16[768,768]{1,0:T(8,128)(2,1)}, u32[]{:S(2)}, u32[]{:S(2)}) collective-permute-start(bf16[768,768]{1,0:T(8,128)(2,1)S(1)} %add_convert_fusion.refs_6_), channel_id=1, source_target_pairs={{0,4},{2,10},{4,0},{6,14},{8,12},{10,2},{12,8},{14,6},{16,20},{18,... | collective-permute-start | bytes 3538952 | tf_op jit(solution)/shard_map/ppermute | solution.py:561
  89.2 17.5 %collective-permute-start.9 = (bf16[392,768]{1,0:T(8,128)(2,1)S(1)}, bf16[392,768]{1,0:T(8,128)(2,1)S(1)}, u32[]{:S(2)}, u32[]{:S(2)}) collective-permute-start(bf16[392,768]{1,0:T(8,128)(2,1)S(1)} %copy-done.9), channel_id=1, source_target_pairs={{0,1},{1,0},{2,3},{3,2},{4,5},{5,4},{6,7},{7,6},{8,9},{9,8},{10,11... | collective-permute-start | bytes 1806344 | tf_op jit(solution)/shard_map/ppermute | solution.py:533
  112.5 14.1 %collective-permute-start.13 = (bf16[768,768]{1,0:T(8,128)(2,1)}, bf16[768,768]{1,0:T(8,128)(2,1)S(1)}, u32[]{:S(2)}, u32[]{:S(2)}) collective-permute-start(bf16[768,768]{1,0:T(8,128)(2,1)} %get-tuple-element.113.refs_2_), channel_id=1, source_target_pairs={{0,2},{2,0},{4,6},{6,4},{8,10},{10,8},{12,14},{14,12},{16,18},{18,... | collective-permute-start | bytes 3538952 | tf_op jit(solution)/shard_map/ppermute | solution.py:537
  112.5 9.9 %collective-permute-start.22 = (bf16[384,768]{1,0:T(8,128)(2,1)S(1)}, bf16[384,768]{1,0:T(8,128)(2,1)S(1)}, u32[]{:S(2)}, u32[]{:S(2)}) collective-permute-start(bf16[384,768]{1,0:T(8,128)(2,1)S(1)} %add_convert_fusion.2.refs_7_), channel_id=1, source_target_pairs={{0,8},{2,6},{4,12},{6,2},{8,0},{10,14},{12,4},{14,10},{16,24},{18,... | collective-permute-start | bytes 1769480 | tf_op jit(solution)/shard_map/ppermute | solution.py:561
  123.9 15.9 %collective-permute-start.23 = (bf16[192,768]{1,0:T(8,128)(2,1)S(1)}, bf16[192,768]{1,0:T(8,128)(2,1)S(1)}, u32[]{:S(2)}, u32[]{:S(2)}) collective-permute-start(bf16[192,768]{1,0:T(8,128)(2,1)S(1)} %add_convert_fusion.4), channel_id=1, source_target_pairs={{0,16},{2,18},{4,20},{6,22},{8,24},{10,26},{12,28},{14,30},{16,0},... | collective-permute-start | bytes 884744 | tf_op jit(solution)/shard_map/ppermute | solution.py:561
  128.8 12.6 %collective-permute-start.14 = (bf16[384,768]{1,0:T(8,128)(2,1)}, bf16[384,768]{1,0:T(8,128)(2,1)}, u32[]{:S(2)}, u32[]{:S(2)}) collective-permute-start(bf16[384,768]{1,0:T(8,128)(2,1)} %add_convert_fusion.1), channel_id=1, source_target_pairs={{0,4},{2,10},{4,0},{6,14},{8,12},{10,2},{12,8},{14,6},{16,20},{18,... | collective-permute-start | bytes 1769480 | tf_op jit(solution)/shard_map/ppermute | solution.py:561
  130.3 27.6 %collective-permute-start.12 = (bf16[392,768]{1,0:T(8,128)(2,1)}, bf16[392,768]{1,0:T(8,128)(2,1)S(1)}, u32[]{:S(2)}, u32[]{:S(2)}) collective-permute-start(bf16[392,768]{1,0:T(8,128)(2,1)} %get-tuple-element.119), channel_id=1, source_target_pairs={{0,1},{1,0},{2,3},{3,2},{4,5},{5,4},{6,7},{7,6},{8,9},{9,8},{10,11... | collective-permute-start | bytes 1806344 | tf_op jit(solution)/shard_map/ppermute | solution.py:533
  130.9 27.2 %collective-permute-start.11 = (bf16[392,768]{1,0:T(8,128)(2,1)}, bf16[392,768]{1,0:T(8,128)(2,1)S(1)}, u32[]{:S(2)}, u32[]{:S(2)}) collective-permute-start(bf16[392,768]{1,0:T(8,128)(2,1)} %get-tuple-element.116), channel_id=1, source_target_pairs={{0,1},{1,0},{2,3},{3,2},{4,5},{5,4},{6,7},{7,6},{8,9},{9,8},{10,11... | collective-permute-start | bytes 1806344 | tf_op jit(solution)/shard_map/ppermute | solution.py:533
  141.3 15.2 %collective-permute-start.24 = (bf16[192,768]{1,0:T(8,128)(2,1)S(1)}, bf16[192,768]{1,0:T(8,128)(2,1)}, u32[]{:S(2)}, u32[]{:S(2)}) collective-permute-start(bf16[192,768]{1,0:T(8,128)(2,1)S(1)} %add_convert_fusion.3), channel_id=1, source_target_pairs={{0,16},{2,18},{4,20},{6,22},{8,24},{10,26},{12,28},{14,30},{16,0},... | collective-permute-start | bytes 884744 | tf_op jit(solution)/shard_map/ppermute | solution.py:561
  142.6 20.6 %collective-permute-start.15 = (bf16[192,768]{1,0:T(8,128)(2,1)S(1)}, bf16[192,768]{1,0:T(8,128)(2,1)}, u32[]{:S(2)}, u32[]{:S(2)}) collective-permute-start(bf16[192,768]{1,0:T(8,128)(2,1)S(1)} %add_convert_fusion.5.refs_9_), channel_id=1, source_target_pairs={{0,8},{2,6},{4,12},{6,2},{8,0},{10,14},{12,4},{14,10},{16,24},{18,... | collective-permute-start | bytes 884744 | tf_op jit(solution)/shard_map/ppermute | solution.py:561
  157.9 17.0 %collective-permute-start.25 = (bf16[384,768]{1,0:T(8,128)(2,1)S(1)}, bf16[384,768]{1,0:T(8,128)(2,1)}, u32[]{:S(2)}, u32[]{:S(2)}) collective-permute-start(bf16[384,768]{1,0:T(8,128)(2,1)S(1)} %maximum_select_fusion.5), channel_id=1, source_target_pairs={{0,8},{2,6},{4,12},{6,2},{8,0},{10,14},{12,4},{14,10},{16,24},{18,... | collective-permute-start | bytes 1769480 | tf_op jit(solution)/shard_map/ppermute | solution.py:561
  174.8 11.1 %collective-permute-start.18 = (bf16[120,768]{1,0:T(8,128)(2,1)}, bf16[120,768]{1,0:T(8,128)(2,1)S(1)}, u32[]{:S(2)}, u32[]{:S(2)}) collective-permute-start(bf16[120,768]{1,0:T(8,128)(2,1)} %pad_maximum_fusion.3), channel_id=1, source_target_pairs={{0,16},{2,18},{4,20},{6,22},{8,24},{10,26},{12,28},{14,30},{16,0},... | collective-permute-start | bytes 552968 | tf_op jit(solution)/shard_map/ppermute | solution.py:561
  176.5 22.7 %collective-permute-start.26 = (bf16[768,768]{1,0:T(8,128)(2,1)S(1)}, bf16[768,768]{1,0:T(8,128)(2,1)S(1)}, u32[]{:S(2)}, u32[]{:S(2)}) collective-permute-start(bf16[768,768]{1,0:T(8,128)(2,1)S(1)} %maximum_select_fusion.2), channel_id=1, source_target_pairs={{0,4},{2,10},{4,0},{6,14},{8,12},{10,2},{12,8},{14,6},{16,20},{18,... | collective-permute-start | bytes 3538952 | tf_op jit(solution)/shard_map/ppermute | solution.py:561
  186.8 10.9 %collective-permute-start.19 = (bf16[216,768]{1,0:T(8,128)(2,1)}, bf16[216,768]{1,0:T(8,128)(2,1)S(1)}, u32[]{:S(2)}, u32[]{:S(2)}) collective-permute-start(bf16[216,768]{1,0:T(8,128)(2,1)} %pad_maximum_fusion.2), channel_id=1, source_target_pairs={{0,8},{2,6},{4,12},{6,2},{8,0},{10,14},{12,4},{14,10},{16,24},{18,... | collective-permute-start | bytes 995336 | tf_op jit(solution)/shard_map/ppermute | solution.py:561
  198.1 10.3 %collective-permute-start.20 = (bf16[408,768]{1,0:T(8,128)(2,1)S(1)}, bf16[408,768]{1,0:T(8,128)(2,1)S(1)}, u32[]{:S(2)}, u32[]{:S(2)}) collective-permute-start(bf16[408,768]{1,0:T(8,128)(2,1)S(1)} %pad_maximum_fusion.1), channel_id=1, source_target_pairs={{0,4},{2,10},{4,0},{6,14},{8,12},{10,2},{12,8},{14,6},{16,20},{18,... | collective-permute-start | bytes 1880072 | tf_op jit(solution)/shard_map/ppermute | solution.py:561
  199.7 15.1 %collective-permute-start.27 = (bf16[1536,768]{1,0:T(8,128)(2,1)S(1)}, bf16[1536,768]{1,0:T(8,128)(2,1)S(1)}, u32[]{:S(2)}, u32[]{:S(2)}) collective-permute-start(bf16[1536,768]{1,0:T(8,128)(2,1)S(1)} %maximum_select_fusion.mine_ref), channel_id=1, source_target_pairs={{0,2},{2,0},{4,6},{6,4},{8,10},{10,8},{12,14},{14,12},{16,18},{18,... | collective-permute-start | bytes 7077896 | tf_op jit(solution)/shard_map/ppermute | solution.py:537
  (31 other events, 236.7 us)
